TPU v7x, 512 devices: a whole 4x8x8 slice. The times are simulated.
512 devices in a mesh: ctx: 128 (over y, z, x_lo), tp: 4 (over x_hi, core).
Axes of the slice: x: 4 (x_hi: 2, x_lo: 2; x = x_hi * 2 + x_lo), y: 8, z: 8, core: 2. Of those that a mesh axis runs over, the one named last changes fastest.
Arguments:
- features: bfloat16 [3, 2048, 16384], P(None, 'tp', 'ctx'), may hold values from -6 to 6
- short_taps: float32 [3, 3, 2048], P(None, None, 'tp'), may hold values from -3 to 3
- filters: bfloat16 [128, 16384], P('tp'), may hold values from -2 to 2
- skip_gain: float32 [2048], P('tp'), may hold values from -4 to 4
- out_weight: bfloat16 [2048, 2048], P('tp'), may hold values from -0.125 to 0.125
Outputs:
- block_out: bfloat16 [2048, 16384], P('tp', 'ctx')
All inputs are finite; a program needn't handle non-finite values.
Results may differ from a plain program's by a relative error of at most 0.009.
Values may be sent and summed in bfloat16 or wider, within the bound.
No kernel may reach another device: no remote copies, remote signals or barrier semaphores. Data moves between devices by JAX's collectives and lax.ppermute only.
A program may use at most 64 MiB of HBM per device.

v0:
```python
import math

import jax
import jax.numpy as jnp
from jax import lax
from jax.sharding import PartitionSpec as P

GROUP = 16


highest = lax.Precision.HIGHEST


def from_behind(value, axis, steps):
    count = lax.axis_size(axis)
    initial, last = (max(0, -steps), min(count, count - steps))
    return lax.ppermute(value, axis, [(source, source + steps) for source in range(initial, last)])


def left_product(matrix, stacked):
    return jnp.einsum("kn,bns->bks", matrix, stacked, precision=highest)


def right_product(stacked, matrix):
    return jnp.einsum("bks,st->bkt", stacked, matrix, precision=highest)


def split_length(total_len):
    row_count = 2
    for candidate in range(2, math.isqrt(total_len) + 1, 2):
        if total_len % candidate == 0:
            row_count = candidate
    return (row_count, total_len // row_count)


def dft_tables(row_count, col_count):
    total_len = row_count * col_count
    row_index = jnp.arange(row_count, dtype=jnp.int32)
    col_index = jnp.arange(col_count, dtype=jnp.int32)
    row_angle = (row_index[:, None] * row_index[None, :] % row_count).astype(jnp.float32) * (
        2.0 * math.pi / row_count
    )
    col_angle = (col_index[:, None] * col_index[None, :] % col_count).astype(jnp.float32) * (
        2.0 * math.pi / col_count
    )
    twist_angle = (row_index[:, None] * col_index[None, :] % total_len).astype(jnp.float32) * (
        2.0 * math.pi / total_len
    )
    return (
        jnp.cos(row_angle),
        jnp.sin(row_angle),
        jnp.cos(col_angle),
        jnp.sin(col_angle),
        jnp.cos(twist_angle),
        jnp.sin(twist_angle),
    )


def forward_dft(signal, tables):
    cos_row, sin_row, cos_col, sin_col, cos_twist, sin_twist = tables
    half_rows = signal.shape[1]
    first_real = left_product(cos_row[:, :half_rows], signal)
    first_imag = -left_product(sin_row[:, :half_rows], signal)
    twist_real = first_real * cos_twist + first_imag * sin_twist
    twist_imag = first_imag * cos_twist - first_real * sin_twist
    spec_real = right_product(twist_real, cos_col) + right_product(twist_imag, sin_col)
    spec_imag = right_product(twist_imag, cos_col) - right_product(twist_real, sin_col)
    return (spec_real, spec_imag)


def inverse_dft(spec_real, spec_imag, tables, half_rows):
    cos_row, sin_row, cos_col, sin_col, cos_twist, sin_twist = tables
    total_len = cos_row.shape[0] * cos_col.shape[0]
    middle_real = right_product(spec_real, cos_col) - right_product(spec_imag, sin_col)
    middle_imag = right_product(spec_imag, cos_col) + right_product(spec_real, sin_col)
    turned_real = middle_real * cos_twist - middle_imag * sin_twist
    turned_imag = middle_imag * cos_twist + middle_real * sin_twist
    signal = left_product(cos_row[:half_rows, :], turned_real) - left_product(
        sin_row[:half_rows, :], turned_imag
    )
    return signal / total_len


def local(features, short_taps, filters, skip_gain, out_weight):
    taps_count = short_taps.shape[0]
    chan_tp = features.shape[1]
    tok_local = features.shape[2]
    ctx_count = lax.axis_size("ctx")
    chan_dev = chan_tp // ctx_count
    group_dev = max(1, chan_dev // GROUP)
    per_group = chan_dev // group_dev
    seq_len = tok_local * ctx_count
    row_count, col_count = split_length(2 * seq_len)
    half_rows = row_count // 2
    tables = dft_tables(row_count, col_count)
    ctx_rank = lax.axis_index("ctx")
    kernel_rows = lax.dynamic_slice_in_dim(filters, ctx_rank * chan_dev // GROUP, group_dev, 0)
    kernel_real, kernel_imag = forward_dft(
        kernel_rows.astype(jnp.float32).reshape(group_dev, half_rows, col_count), tables
    )
    previous = from_behind(features[:, :, tok_local - (taps_count - 1) :], "ctx", 1)
    extended = jnp.concatenate([previous, features], axis=2).astype(jnp.float32)
    conv_all = jnp.zeros(features.shape, jnp.float32)
    for offset in range(taps_count):
        begin_at = taps_count - 1 - offset
        conv_all = (
            conv_all
            + short_taps[offset][:, :, None] * extended[:, :, begin_at : begin_at + tok_local]
        )
    query_conv = conv_all[0]
    product = (conv_all[1] * conv_all[2]).astype(jnp.bfloat16)
    gathered = lax.all_to_all(product, "ctx", split_axis=0, concat_axis=1, tiled=True)
    signal = gathered.astype(jnp.float32)
    sig_real, sig_imag = forward_dft(signal.reshape(chan_dev, half_rows, col_count), tables)
    four_shape = (group_dev, per_group, row_count, col_count)
    sig_real = sig_real.reshape(four_shape)
    sig_imag = sig_imag.reshape(four_shape)
    kernel_wide_real = kernel_real[:, None]
    kernel_wide_imag = kernel_imag[:, None]
    prod_real = (sig_real * kernel_wide_real - sig_imag * kernel_wide_imag).reshape(
        chan_dev, row_count, col_count
    )
    prod_imag = (sig_real * kernel_wide_imag + sig_imag * kernel_wide_real).reshape(
        chan_dev, row_count, col_count
    )
    longconv = inverse_dft(prod_real, prod_imag, tables, half_rows).reshape(chan_dev, seq_len)
    skip_local = lax.dynamic_slice_in_dim(skip_gain, ctx_rank * chan_dev, chan_dev, 0)
    long_mix = (longconv + skip_local[:, None] * signal).astype(jnp.bfloat16)
    restored = lax.all_to_all(long_mix, "ctx", split_axis=1, concat_axis=0, tiled=True)
    gated = (query_conv * restored.astype(jnp.float32)).astype(jnp.bfloat16)
    return lax.psum_scatter(
        lax.dot_general(
            out_weight, gated, (((0,), (0,)), ((), ())), preferred_element_type=jnp.float32
        ).astype(jnp.bfloat16),
        "tp",
        scatter_dimension=0,
        tiled=True,
    )


def solution(mesh):
    placed = (P(None, "tp", "ctx"), P(None, None, "tp"), P("tp", None), P("tp"), P("tp", None))
    return jax.shard_map(
        local, mesh=mesh, in_specs=placed, out_specs=P("tp", "ctx"), check_vma=False
    )
```

profile of v0, /device:TPU:1, one launch (start us, length us, event | category | flops | bytes accessed | tf_op | source)
XLA Modules:
  0.0 139.9 jit_solution(3832880754229626524)
XLA Ops:
  6.5 2.1 %slice.49 = bf16[3,512,2]{2,1,0:T(8,128)(2,1)} slice(bf16[3,512,128]{2,1,0:T(8,128)(2,1)} %param.5), slice={[0:3], [0:512], [126:128]} | slice | bytes 12288 | tf_op jit(solution)/shard_map/slice | solution.py:101
  8.6 3.9 %collective-permute-start = (bf16[3,512,2]{2,1,0:T(8,128)(2,1)}, bf16[3,512,2]{2,1,0:T(8,128)(2,1)S(1)}, u32[]{:S(2)}, u32[]{:S(2)}) collective-permute-start(bf16[3,512,2]{2,1,0:T(8,128)(2,1)} %slice.49), channel_id=1, source_target_pairs={{0,4},{4,8},{8,12},{12,16},{16,20},{20,24},{24,28},{28,32},{32,36}... | collective-permute-start | bytes 18440 | tf_op jit(solution)/shard_map/ppermute | solution.py:17
  14.9 1.8 %fusion.46 = f32[128,256]{1,0:T(8,128)S(1)} fusion(f32[1,128,256]{1,2,0:T(8,128)S(1)} %convolution_bitcast_fusion.1, f32[1,128,256]{1,2,0:T(8,128)S(1)} %fusion.4), kind=kOutput, calls=%fused_computation.77 | convolution fusion | flops 102137856 | bytes 393216 | tf_op jit(solution)/shard_map/bks,st->bkt/dot_general | solution.py:25
  16.7 2.5 %fusion.50 = f32[128,256]{1,0:T(8,128)} fusion(f32[1,128,256]{1,2,0:T(8,128)S(1)} %fusion.4, f32[1,128,256]{1,2,0:T(8,128)S(1)} %convolution_bitcast_fusion.1), kind=kOutput, calls=%fused_computation.81 | convolution fusion | flops 102137856 | bytes 393216 | tf_op jit(solution)/shard_map/bks,st->bkt/dot_general | solution.py:25
  19.2 1.8 %convolution_subtract_fusion.3 = f32[128,256]{1,0:T(8,128)S(1)} fusion(f32[128,256]{1,0:T(8,128)S(1)} %fusion.46, f32[1,128,256]{1,2,0:T(8,128)S(1)} %fusion.4, f32[1,128,256]{1,2,0:T(8,128)S(1)} %convolution_bitcast_fusion.1), kind=kOutput, calls=%fused_computation.12 | convolution fusion | flops 102170624 | bytes 524288 | tf_op jit(solution)/shard_map/bks,st->bkt/dot_general | solution.py:25
  23.3 20.1 %all-to-all-start = ((bf16[128,4,128]{2,1,0:T(4,128)(2,1)}), bf16[128,4,128]{2,1,0:T(4,128)(2,1)S(1)}, u32[]{:S(2)}, u32[]{:S(2)}) async-start(bf16[128,4,128]{2,1,0:T(4,128)(2,1)} %bitcast.4), calls=%async_computation | async-start | bytes 262144 | tf_op jit(solution)/shard_map/all_to_all | solution.py:112
  44.9 2.8 %convolution_add_fusion.2 = f32[128,256]{1,0:T(8,128)S(1)} fusion(f32[128,256]{1,0:T(8,128)} %fusion.50, f32[1,128,256]{1,2,0:T(8,128)} %copy-done.7, f32[1,128,256]{1,2,0:T(8,128)} %copy-done.6), kind=kOutput, calls=%fused_computation.13 | convolution fusion | flops 102170624 | bytes 524288 | tf_op jit(solution)/shard_map/bks,st->bkt/dot_general | solution.py:25
  47.7 6.8 %all-to-all-done = bf16[128,4,128]{2,1,0:T(4,128)(2,1)S(1)} async-done(((bf16[128,4,128]{2,1,0:T(4,128)(2,1)}), bf16[128,4,128]{2,1,0:T(4,128)(2,1)S(1)}, u32[]{:S(2)}, u32[]{:S(2)}) %all-to-all-start) | async-done | bytes 131104 | tf_op jit(solution)/shard_map/all_to_all | solution.py:112
  55.2 1.6 %reshape.145 = bf16[4,64,256]{2,1,0:T(8,128)(2,1)} reshape(bf16[4,128,128]{2,1,0:T(8,128)(2,1)} %bitcast.84) | data formatting | bytes 262144 | tf_op jit(solution)/shard_map/reshape | solution.py:114
  56.8 1.3 fusion.1
  58.2 1.3 convolution_bitcast_fusion
  59.5 1.9 %fusion.28 = f32[4,128,256]{2,1,0:T(8,128)S(1)} fusion(f32[4,128,256]{1,2,0:T(8,128)S(1)} %convolution_bitcast_fusion, f32[4,128,256]{1,2,0:T(8,128)S(1)} %fusion.1, f32[128,256]{0,1:T(8,128)S(1)} %get-tuple-element.8, f32[128,256]{0,1:T(8,128)S(1)} %get-tuple-element.9), kind=kOutput, calls=%fused_computation.53 | convolution fusion | flops 403963904 | bytes 1835008 | tf_op jit(solution)/shard_map/bks,st->bkt/dot_general | solution.py:25
  61.4 1.9 %fusion.30 = f32[4,128,256]{2,1,0:T(8,128)S(1)} fusion(f32[4,128,256]{1,2,0:T(8,128)S(1)} %fusion.1, f32[4,128,256]{1,2,0:T(8,128)S(1)} %convolution_bitcast_fusion, f32[128,256]{0,1:T(8,128)S(1)} %get-tuple-element.8, f32[128,256]{0,1:T(8,128)S(1)} %get-tuple-element.9), kind=kOutput, calls=%fused_computation.55 | convolution fusion | flops 403963904 | bytes 1835008 | tf_op jit(solution)/shard_map/bks,st->bkt/dot_general | solution.py:25
  63.3 1.9 %convolution_subtract_fusion.1 = f32[4,128,256]{2,1,0:T(8,128)S(1)} fusion(f32[4,128,256]{2,1,0:T(8,128)S(1)} %fusion.28, f32[4,128,256]{1,2,0:T(8,128)S(1)} %fusion.1, f32[4,128,256]{1,2,0:T(8,128)S(1)} %convolution_bitcast_fusion, f32[128,256]{0,1:T(8,128)S(1)} %get-tuple-element.8, f32[128,256]{0,1:T(8,128)S(1)} %get-tuple-element.9), kind=kOutput, calls=%fused_computation.7 | convolution fusion | flops 404094976 | bytes 2359296 | tf_op jit(solution)/shard_map/bks,st->bkt/dot_general | solution.py:25
  65.2 1.9 %convolution_add_fusion.1 = f32[4,128,256]{2,1,0:T(8,128)S(1)} fusion(f32[4,128,256]{2,1,0:T(8,128)S(1)} %fusion.30, f32[4,128,256]{1,2,0:T(8,128)S(1)} %convolution_bitcast_fusion, f32[4,128,256]{1,2,0:T(8,128)S(1)} %fusion.1, f32[128,256]{0,1:T(8,128)S(1)} %get-tuple-element.8, f32[128,256]{0,1:T(8,128)S(1)} %get-tuple-element.9), kind=kOutput, calls=%fused_computation.8 | convolution fusion | flops 404094976 | bytes 2359296 | tf_op jit(solution)/shard_map/bks,st->bkt/dot_general | solution.py:25
  67.0 1.9 %fusion.24 = f32[4,128,256]{1,2,0:T(8,128)S(1)} fusion(f32[4,128,256]{2,1,0:T(8,128)S(1)} %convolution_subtract_fusion.1, f32[4,128,256]{2,1,0:T(8,128)S(1)} %convolution_add_fusion.1, f32[128,256]{1,0:T(8,128)S(1)} %convolution_subtract_fusion.3, f32[128,256]{1,0:T(8,128)S(1)} %convolution_add_fusion.2), kind=kOutput, calls=%fused_computation.49 | convolution fusion | flops 403963904 | bytes 1835008 | tf_op jit(solution)/shard_map/bks,st->bkt/dot_general | solution.py:25
  69.0 1.7 %fusion.26 = f32[4,128,256]{1,2,0:T(8,128)S(1)} fusion(f32[4,128,256]{2,1,0:T(8,128)S(1)} %convolution_subtract_fusion.1, f32[4,128,256]{2,1,0:T(8,128)S(1)} %convolution_add_fusion.1, f32[128,256]{1,0:T(8,128)S(1)} %convolution_subtract_fusion.3, f32[128,256]{1,0:T(8,128)S(1)} %convolution_add_fusion.2), kind=kOutput, calls=%fused_computation.51 | convolution fusion | flops 403963904 | bytes 1835008 | tf_op jit(solution)/shard_map/bks,st->bkt/dot_general | solution.py:25
  70.7 1.7 %convolution_add_fusion = f32[4,128,256]{1,2,0:T(8,128)S(1)} fusion(f32[4,128,256]{1,2,0:T(8,128)S(1)} %fusion.24, f32[4,128,256]{2,1,0:T(8,128)S(1)} %convolution_subtract_fusion.1, f32[4,128,256]{2,1,0:T(8,128)S(1)} %convolution_add_fusion.1, f32[128,256]{1,0:T(8,128)S(1)} %convolution_subtract_fusion.3, f32[128,256]{1,0:T(8,128)S(1)} %convolution_add_fusion.2), kind=kOutput, calls=%fused_computation.5 | convolution fusion | flops 404094976 | bytes 2359296 | tf_op jit(solution)/shard_map/bks,st->bkt/dot_general | solution.py:25
  72.4 1.7 %convolution_subtract_fusion = f32[4,128,256]{1,2,0:T(8,128)S(1)} fusion(f32[4,128,256]{1,2,0:T(8,128)S(1)} %fusion.26, f32[4,128,256]{2,1,0:T(8,128)S(1)} %convolution_subtract_fusion.1, f32[4,128,256]{2,1,0:T(8,128)S(1)} %convolution_add_fusion.1, f32[128,256]{1,0:T(8,128)S(1)} %convolution_subtract_fusion.3, f32[128,256]{1,0:T(8,128)S(1)} %convolution_add_fusion.2), kind=kOutput, calls=%fused_computation.6 | convolution fusion | flops 404094976 | bytes 2359296 | tf_op jit(solution)/shard_map/bks,st->bkt/dot_general | solution.py:25
  74.9 1.5 %fusion.3 = f32[4,64,256]{2,1,0:T(8,128)} fusion(f32[4,256,64]{1,2,0:T(8,128)S(1)} %fusion.10, f32[4,128,256]{1,2,0:T(8,128)S(1)} %convolution_subtract_fusion, f32[4,128,256]{1,2,0:T(8,128)S(1)} %convolution_add_fusion, f32[128,256]{0,1:T(8,128)S(1)} %get-tuple-element.8, f32[128,256]{0,1:T(8,128)S(1)} %get-tuple-element.9, f32[128,128]{0,1:T(8,128)S(1)} %copy-done.5), kind=kOutput, calls=%fused_computation.11 | convolution fusion | flops 101187584 | bytes 1900544 | tf_op jit(solution)/shard_map/kn,bns->bks/dot_general | solution.py:21
  77.6 18.3 %all_to_all.23 = bf16[4,128,128]{2,0,1:T(4,128)(2,1)S(1)} all-to-all(bf16[4,128,128]{2,0,1:T(4,128)(2,1)S(1)} %copy.49), channel_id=1, replica_groups=mesh['ctx'=128,'tp'=4] {'ctx'}, dimensions={1} | all-to-all | bytes 262144 | tf_op jit(solution)/shard_map/all_to_all | solution.py:129
  95.9 1.3 fusion
  97.2 34.2 %reduce-scatter.2.cloned.1.call-done = bf16[512,128]{0,1:T(8,128)(2,1)} async-done(((bf16[2048,128]{0,1:T(8,128)(2,1)}), bf16[512,128]{0,1:T(8,128)(2,1)}) %reduce-scatter.2.cloned.1.call-update) | async-done | bytes 131088 | tf_op jit(solution)/shard_map/reduce_scatter | solution.py:131
  131.4 1.7 %copy.50 = bf16[512,128]{1,0:T(8,128)(2,1)} copy(bf16[512,128]{0,1:T(8,128)(2,1)} %reduce-scatter.2.cloned.1.call-done) | data formatting | bytes 262144 | tf_op jit(solution)/shard_map/reduce_scatter | solution.py:131
  (39 shorter events, 8.6 us)
Async XLA Ops:
  6.5 89.4 %copy-start = (bf16[512,2048]{1,0:T(8,128)(2,1)S(1)}, bf16[512,2048]{1,0:T(8,128)(2,1)}, u32[]{:S(2)}) copy-start(bf16[512,2048]{1,0:T(8,128)(2,1)} %param.9) | copy-start | bytes 6291460
  8.6 12.4 %collective-permute-start = (bf16[3,512,2]{2,1,0:T(8,128)(2,1)}, bf16[3,512,2]{2,1,0:T(8,128)(2,1)S(1)}, u32[]{:S(2)}, u32[]{:S(2)}) collective-permute-start(bf16[3,512,2]{2,1,0:T(8,128)(2,1)} %slice.49), channel_id=1, source_target_pairs={{0,4},{4,8},{8,12},{12,16},{16,20},{20,24},{24,28},{28,32},{32,36}... | collective-permute-start | bytes 18440 | tf_op jit(solution)/shard_map/ppermute | solution.py:17
  12.8 6.4 %copy-start.2 = (f32[128,128]{0,1:T(8,128)}, f32[128,128]{0,1:T(8,128)S(1)}, u32[]{:S(2)}) copy-start(f32[128,128]{0,1:T(8,128)S(1)} %fusion.85) | copy-start | bytes 196612
  13.1 1.8 %copy-start.4 = (f32[128,128]{0,1:T(8,128)}, f32[128,128]{0,1:T(8,128)S(1)}, u32[]{:S(2)}) copy-start(f32[128,128]{0,1:T(8,128)S(1)} %fusion.84) | copy-start | bytes 196612
  14.6 4.6 %copy-start.6 = (f32[1,128,256]{1,2,0:T(8,128)}, f32[1,128,256]{1,2,0:T(8,128)S(1)}, u32[]{:S(2)}) copy-start(f32[1,128,256]{1,2,0:T(8,128)S(1)} %fusion.4) | copy-start | bytes 393220
  14.9 4.3 %copy-start.7 = (f32[1,128,256]{1,2,0:T(8,128)}, f32[1,128,256]{1,2,0:T(8,128)S(1)}, u32[]{:S(2)}) copy-start(f32[1,128,256]{1,2,0:T(8,128)S(1)} %convolution_bitcast_fusion.1) | copy-start | bytes 393220
  16.7 4.3 %copy-start.8 = (f32[3,3,512]{2,1,0:T(4,128)S(1)}, f32[3,3,512]{2,1,0:T(4,128)}, u32[]{:S(2)}) copy-start(f32[3,3,512]{2,1,0:T(4,128)} %param.6) | copy-start | bytes 55300
  16.7 4.3 %copy-start.1 = (bf16[3,512,128]{2,1,0:T(8,128)(2,1)S(1)}, bf16[3,512,128]{2,1,0:T(8,128)(2,1)}, u32[]{:S(2)}) copy-start(bf16[3,512,128]{2,1,0:T(8,128)(2,1)} %param.5) | copy-start | bytes 1179652
  23.3 31.3 %all-to-all-start = ((bf16[128,4,128]{2,1,0:T(4,128)(2,1)}), bf16[128,4,128]{2,1,0:T(4,128)(2,1)S(1)}, u32[]{:S(2)}, u32[]{:S(2)}) async-start(bf16[128,4,128]{2,1,0:T(4,128)(2,1)} %bitcast.4), calls=%async_computation | async-start | bytes 262144 | tf_op jit(solution)/shard_map/all_to_all | solution.py:112
  43.3 88.0 %reduce-scatter.2.cloned.1.call-start = ((), (), s32[]{:S(2)}) async-start(), calls=%async_computation.3 | async-start | bytes 655360 | tf_op jit(solution)/shard_map/reduce_scatter | solution.py:131
  72.4 1.8 %copy-start.3 = (f32[128,128]{0,1:T(8,128)S(1)}, f32[128,128]{0,1:T(8,128)}, u32[]{:S(2)}) copy-start(f32[128,128]{0,1:T(8,128)} %copy-done.2) | copy-start | bytes 196612
  72.4 2.5 %copy-start.5 = (f32[128,128]{0,1:T(8,128)S(1)}, f32[128,128]{0,1:T(8,128)}, u32[]{:S(2)}) copy-start(f32[128,128]{0,1:T(8,128)} %copy-done.4) | copy-start | bytes 196612
Sparse Core Ops, SparseCore 0:
  97.3 34.0 reduce-scatter.1
where the time goes:
time: 140 us
  waiting for transfers between devices  41 us (29%)
  matrix products  30.2 us (22%)
  starting transfers between devices  24.2 us (17%)
  blocking collectives  18.3 us (13%)
  between operations  13.7 us (10%)
  local copies, waits for them, and re-layouts  9.05 us (6%)
  other arithmetic  3.38 us (2%)
    reduce_scatter x1, waiting for transfers between devices, local(): lax.psum_scatter(lax.dot_general(out_weight, gated, (((0,), (0,)), ((), (...  34.2 us
    dot_general x12, matrix products, right_product(): return jnp.einsum('bks,st->bkt', stacked, matrix, precision=highest)  23.5 us
    all_to_all x1, starting transfers between devices, local(): lax.all_to_all(product, 'ctx', split_axis=0, concat_axis=1, tiled=True)  20.1 us
    all_to_all x1, blocking collectives, local(): lax.all_to_all(long_mix, 'ctx', split_axis=1, concat_axis=0, tiled=True)  18.3 us
    all_to_all x1, waiting for transfers between devices, local(): lax.all_to_all(product, 'ctx', split_axis=0, concat_axis=1, tiled=True)  6.82 us
    dot_general x6, matrix products, left_product(): return jnp.einsum('kn,bns->bks', matrix, stacked, precision=highest)  5.45 us
    ppermute x1, starting transfers between devices, from_behind(): lax.ppermute(value, axis, [(source, source + steps) for source in range(i...  3.94 us
  transfers between devices with their start and end apart: 3, of which 2 were waited for; matrix products, arithmetic and copies ran while one was open for 9% of the time, Pallas kernels for 0%

commit v1 on v0

v1 whole, which is shorter than its diff:
```python
import jax
import jax.numpy as jnp
from jax import lax
from jax.experimental import pallas as pl
from jax.experimental.pallas import tpu as pltpu
from jax.sharding import PartitionSpec as P

GROUP = 16
LANES = 128
CHUNK = 1024

f32 = jnp.float32
bf16 = jnp.bfloat16


def pattern(values):
    row = lax.broadcasted_iota(jnp.int32, (8, LANES), 0) % 4
    tile = jnp.full((8, LANES), values[3], f32)
    for index in (2, 1, 0):
        tile = jnp.where(row == index, values[index], tile)
    return tile


def by_rows(tile, array):
    rows = array.shape[0]
    return (array.reshape(rows // 8, 8, LANES) * tile[None]).reshape(rows, LANES)


def short_conv(value, tiles):
    lane = lax.broadcasted_iota(jnp.int32, value.shape, 1)
    row = lax.broadcasted_iota(jnp.int32, value.shape, 0)
    total = by_rows(tiles[0], value)
    for offset in (1, 2):
        turned = pltpu.roll(value, offset, 1)
        before = jnp.where(row < 4, 0.0, pltpu.roll(turned, 4, 0))
        total = total + by_rows(tiles[offset], jnp.where(lane < offset, before, turned))
    return total


def conv_kernel(rank_ref, q_ref, k_ref, v_ref, filter_ref, taps_ref, skip_ref, out_ref, line_ref, table_ref, pair_ref, sum_ref):
    rank = rank_ref[0]
    first = rank * 4
    rows = q_ref.shape[0]
    seq_len = filter_ref.shape[1]

    def tiles_of(feature):
        return [pattern([taps_ref[offset, feature, first + c] for c in range(4)]) for offset in range(3)]

    k_conv = short_conv(k_ref[...].astype(f32), tiles_of(1))
    v_conv = short_conv(v_ref[...].astype(f32), tiles_of(2))
    kv = (k_conv * v_conv).astype(bf16).astype(f32)
    row = lax.broadcasted_iota(jnp.int32, kv.shape, 0)
    pair_ref[:, :LANES] = kv.astype(bf16)
    pair_ref[:, LANES:] = jnp.where(row < 4, 0.0, pltpu.roll(kv, 4, 0)).astype(bf16)

    own = (rank * 4 // GROUP) % 8
    line_ref[:, :LANES] = jnp.zeros((8, LANES), f32)
    for at in range(0, seq_len, CHUNK):
        piece = filter_ref[:, at : at + CHUNK].astype(f32)
        sub = lax.broadcasted_iota(jnp.int32, piece.shape, 0)
        chosen = jnp.sum(jnp.where(sub == own, piece, 0.0), axis=0, keepdims=True)
        line_ref[:, LANES + at : LANES + at + CHUNK] = jnp.broadcast_to(chosen, piece.shape)

    sum_ref[...] = jnp.zeros_like(sum_ref)
    for at in range(0, seq_len, CHUNK):
        piece = pltpu.roll(line_ref[:, at : at + CHUNK + LANES], 0, 1, stride=1, stride_axis=0)
        for tile in range(LANES // 16):
            upper = pltpu.roll(piece, 16 * tile, 1)[:, LANES:]
            lower = pltpu.roll(piece, 16 * tile + 8, 1)[:, LANES:]
            both = jnp.concatenate([upper, lower], axis=0).astype(bf16)
            for block in range(CHUNK // LANES):
                to_row = (block % 2) * LANES + 16 * tile
                to_col = (at // LANES + block) // 2 * LANES
                table_ref[to_row : to_row + 16, to_col : to_col + LANES] = both[:, block * LANES : (block + 1) * LANES]
        for part in range(CHUNK // 512):
            begin = (at // 512 + part) * 16
            moved = jnp.dot(
                pair_ref[: rows - begin, :],
                table_ref[:, begin * 16 : begin * 16 + 256],
                preferred_element_type=f32,
            )
            sum_ref[begin:, :] += moved[:, :LANES]
            sum_ref[begin + 8 :, :] += moved[: rows - begin - 8, LANES:]

    direct = pattern([skip_ref[first + c] for c in range(4)])
    kv = pair_ref[:, :LANES].astype(f32)
    long_mix = (sum_ref[...] + by_rows(direct, kv)).astype(bf16).astype(f32)
    q_conv = short_conv(q_ref[...].astype(f32), tiles_of(0))
    out_ref[...] = (q_conv * long_mix).astype(bf16)


def long_conv(rank, q, k, v, filters, short_taps, skip_gain):
    rows = q.shape[0]
    seq_len = filters.shape[1]
    whole = pl.BlockSpec((rows, LANES), lambda i, r: (0, 0))
    in_smem = pl.BlockSpec(memory_space=pltpu.SMEM)
    return pl.pallas_call(
        conv_kernel,
        out_shape=jax.ShapeDtypeStruct((rows, LANES), bf16),
        grid_spec=pltpu.PrefetchScalarGridSpec(
            num_scalar_prefetch=1,
            grid=(1,),
            in_specs=[
                whole,
                whole,
                whole,
                pl.BlockSpec((8, seq_len), lambda i, r: (r[0] * 4 // GROUP // 8, 0)),
                in_smem,
                in_smem,
            ],
            out_specs=whole,
            scratch_shapes=[
                pltpu.VMEM((8, LANES + seq_len), f32),
                pltpu.VMEM((2 * LANES, seq_len // 2), bf16),
                pltpu.VMEM((rows, 2 * LANES), bf16),
                pltpu.VMEM((rows, LANES), f32),
            ],
        ),
        cost_estimate=pl.CostEstimate(flops=1 << 31, bytes_accessed=1 << 20, transcendentals=0),
        name="long_conv",
    )(rank, q, k, v, filters, short_taps, skip_gain)


def project_kernel(gated_ref, weight_ref, out_ref):
    turned = jnp.transpose(gated_ref[...].astype(f32)).astype(bf16)
    width = out_ref.shape[2]
    for member in range(out_ref.shape[0]):
        out_ref[member] = jnp.dot(
            turned, weight_ref[:, member * width : (member + 1) * width], preferred_element_type=f32
        ).astype(bf16)


def project(gated, weight, members):
    return pl.pallas_call(
        project_kernel,
        out_shape=jax.ShapeDtypeStruct((members, gated.shape[1], weight.shape[1] // members), bf16),
        cost_estimate=pl.CostEstimate(flops=1 << 28, bytes_accessed=1 << 21, transcendentals=0),
        name="project",
    )(gated, weight)


def combine_kernel(parts_ref, out_ref):
    total = parts_ref[0].astype(f32)
    for member in range(1, parts_ref.shape[0]):
        total = total + parts_ref[member].astype(f32)
    out_ref[...] = jnp.transpose(total).astype(bf16)


def combine(parts):
    return pl.pallas_call(
        combine_kernel,
        out_shape=jax.ShapeDtypeStruct((parts.shape[2], parts.shape[1]), bf16),
        cost_estimate=pl.CostEstimate(flops=1 << 20, bytes_accessed=1 << 19, transcendentals=0),
        name="combine",
    )(parts)


def local(features, short_taps, filters, skip_gain, out_weight):
    rows_in, chan_tp, tok_local = features.shape
    ctx_count = lax.axis_size("ctx")
    tp_count = lax.axis_size("tp")
    chan_dev = chan_tp // ctx_count
    rank = jnp.full((1,), lax.axis_index("ctx"), jnp.int32)
    sent = features.reshape(rows_in, ctx_count, chan_dev, tok_local).transpose(1, 0, 2, 3)
    sent = sent.reshape(ctx_count, rows_in * chan_dev, tok_local)
    got = lax.all_to_all(sent, "ctx", 0, 0, tiled=True)
    got = got.reshape(ctx_count, rows_in, chan_dev, tok_local)
    q, k, v = (got[:, index].reshape(ctx_count * chan_dev, tok_local) for index in range(3))
    gated = long_conv(rank, q, k, v, filters, short_taps, skip_gain)
    gated = gated.reshape(ctx_count, chan_dev, tok_local)
    gated = lax.all_to_all(gated, "ctx", 0, 0, tiled=True).reshape(chan_tp, tok_local)
    parts = project(gated, out_weight, tp_count)
    return combine(lax.all_to_all(parts, "tp", 0, 0, tiled=True))


def solution(mesh):
    placed = (P(None, "tp", "ctx"), P(None, None, "tp"), P("tp", None), P("tp"), P("tp", None))
    return jax.shard_map(
        local, mesh=mesh, in_specs=placed, out_specs=P("tp", "ctx"), check_vma=False
    )
```

time: 140 us -> 88.2 us (0.63)
  matrix products: 30.2 us -> 0 us
  waiting for transfers between devices: 41 us -> 17.6 us
  blocking collectives: 18.3 us -> 36 us
  between operations: 13.7 us -> 0.04 us
  Pallas kernels: 0 us -> 10.3 us
  starting transfers between devices: 24.2 us -> 19.3 us
  local copies, waits for them, and re-layouts: 9.05 us -> 4.53 us
  other arithmetic: 3.38 us -> 0 us
    reduce_scatter x1 -> x0, waiting for transfers between devices: 34.2 us -> none  [local(): lax.psum_scatter(lax.dot_general(out_weight, gated, (((0,), (0,)), ((), (...]
    dot_general x19 -> x0, matrix products: 30.2 us -> none  [the longest x12 23.5 us: right_product(): return jnp.einsum('bks,st->bkt', stacked, matrix, precision=highest)]
    all_to_all x1 -> x2, blocking collectives: 18.3 us -> 36 us  [the longest x1 19 us: local(): lax.all_to_all(gated, 'ctx', 0, 0, tiled=True).reshape(chan_tp, tok_local)]
    all_to_all x1, waiting for transfers between devices: 6.82 us -> 17.6 us  [local(): got = lax.all_to_all(sent, 'ctx', 0, 0, tiled=True)]
    pallas_call x0 -> x3, Pallas kernels: none -> 10.3 us  [the longest x1 5.54 us: long_conv(): pl.pallas_call(conv_kernel, out_shape=jax.ShapeDtypeStruct((rows, LANES),...]
    ppermute x1 -> x0, starting transfers between devices: 3.94 us -> none  [from_behind(): lax.ppermute(value, axis, [(source, source + steps) for source in range(i...]
    dynamic_slice x2 -> x0, local copies, waits for them, and re-layouts: 1.93 us -> none  [the longest x1 1.17 us: local(): lax.dynamic_slice_in_dim(filters, ctx_rank * chan_dev // GROUP, group_dev...]
    reduce_scatter x1 -> x0, local copies, waits for them, and re-layouts: 1.66 us -> none  [local(): lax.psum_scatter(lax.dot_general(out_weight, gated, (((0,), (0,)), ((), (...]
  transfers between devices with their start and end apart: 3 -> 1, of which waited for: 2 -> 1; matrix products, arithmetic and copies ran while one was open for 9% -> 0% of each run, Pallas kernels for 0% -> 0%
where the time goes in v1:
time: 88.2 us; the launch traced here: 87.8 us
  blocking collectives  36 us (41%)
  starting transfers between devices  19.3 us (22%)
  waiting for transfers between devices  17.6 us (20%)
  Pallas kernels  10.3 us (12%)
  local copies, waits for them, and re-layouts  4.53 us (5%)
    all_to_all x1, starting transfers between devices, local(): got = lax.all_to_all(sent, 'ctx', 0, 0, tiled=True)  19.3 us
    all_to_all x1, blocking collectives, local(): lax.all_to_all(gated, 'ctx', 0, 0, tiled=True).reshape(chan_tp, tok_local)  19 us
    all_to_all x1, waiting for transfers between devices, local(): got = lax.all_to_all(sent, 'ctx', 0, 0, tiled=True)  17.6 us
    all_to_all x1, blocking collectives, local(): return combine(lax.all_to_all(parts, 'tp', 0, 0, tiled=True))  16.9 us
    pallas_call x1, Pallas kernels, long_conv(): pl.pallas_call(conv_kernel, out_shape=jax.ShapeDtypeStruct((rows, LANES),...  5.54 us
    pallas_call x1, Pallas kernels, project(): pl.pallas_call(project_kernel, out_shape=jax.ShapeDtypeStruct((members, g...  2.95 us
    slice x4, local copies, waits for them, and re-layouts, local(): got[:, index].reshape(ctx_count * chan_dev, tok_local)  2.31 us
    pallas_call x1, Pallas kernels, combine(): pl.pallas_call(combine_kernel, out_shape=jax.ShapeDtypeStruct((parts.shap...  1.83 us
  transfers between devices with their start and end apart: 1, of which 1 were waited for; matrix products, arithmetic and copies ran while one was open for 0% of the time, Pallas kernels for 0%

profile of v1, /device:TPU:1, one launch (start us, length us, event | category | flops | bytes accessed | tf_op | source)
XLA Modules:
  0.0 87.8 jit_solution(1095598944654721174)
XLA Ops:
  0.0 1.1 %copy.13 = bf16[128,3,4,128]{3,0,2,1:T(8,128)(2,1)S(1)} copy(bf16[128,3,4,128]{3,2,0,1:T(4,128)(2,1)} %bitcast.14) | data formatting | bytes 786432 | tf_op jit(solution)/shard_map/transpose | solution.py:164
  1.1 1.1 %copy.14 = bf16[128,12,128]{2,1,0:T(8,128)(2,1)} copy(bf16[128,12,128]{2,0,1:T(8,128)(2,1)S(1)} %bitcast.12) | data formatting | bytes 786432 | tf_op jit(solution)/shard_map/reshape | solution.py:165
  2.1 19.3 %all-to-all-start = ((bf16[128,12,128]{2,1,0:T(8,128)(2,1)}), bf16[128,12,128]{2,1,0:T(8,128)(2,1)S(1)}, u32[]{:S(2)}, u32[]{:S(2)}) async-start(bf16[128,12,128]{2,1,0:T(8,128)(2,1)} %copy.14), calls=%async_computation | async-start | bytes 1048576 | tf_op jit(solution)/shard_map/all_to_all | solution.py:166
  21.4 17.6 %all-to-all-done = bf16[128,12,128]{2,1,0:T(8,128)(2,1)S(1)} async-done(((bf16[128,12,128]{2,1,0:T(8,128)(2,1)}), bf16[128,12,128]{2,1,0:T(8,128)(2,1)S(1)}, u32[]{:S(2)}, u32[]{:S(2)}) %all-to-all-start) | async-done | bytes 393248 | tf_op jit(solution)/shard_map/all_to_all | solution.py:166
  39.1 0.1 copy.15
  39.2 0.8 copy.16
  40.0 0.7 copy.17
  40.7 0.8 copy.18
  41.5 5.5 %long_conv.1 = bf16[512,128]{1,0:T(8,128)(2,1)} custom-call(s32[1]{0:T(128)} %bitcast.rank_ref, bf16[512,128]{1,0:T(8,128)(2,1)} %bitcast.15, bf16[512,128]{1,0:T(8,128)(2,1)} %bitcast.16, bf16[512,128]{1,0:T(8,128)(2,1)} %bitcast.17, bf16[32,16384]{1,0:T(8,128)(2,1)} %filter_ref.1, f32[3,3,512]{2,1,0:T(4,128)} %taps_ref.1, f32[512]{0:T(512)} %skip_ref.1), custom_call_target="tpu_custom_call" | custom-call | flops 2147483648 | bytes 1048576 | tf_op jit(solution)/shard_map/long_conv/pallas_call | solution.py:97
  47.0 19.0 %all_to_all.15 = bf16[128,4,128]{2,1,0:T(4,128)(2,1)} all-to-all(bf16[128,4,128]{2,1,0:T(4,128)(2,1)} %bitcast.18), channel_id=1, replica_groups=mesh['ctx'=128,'tp'=4] {'ctx'}, dimensions={0} | all-to-all | bytes 262144 | tf_op jit(solution)/shard_map/all_to_all | solution.py:171
  66.1 3.0 %project.1 = bf16[4,128,512]{2,1,0:T(8,128)(2,1)} custom-call(bf16[512,128]{1,0:T(8,128)(2,1)} %bitcast.13, bf16[512,2048]{1,0:T(8,128)(2,1)} %weight_ref.1), custom_call_target="tpu_custom_call" | custom-call | flops 268435456 | bytes 2097152 | tf_op jit(solution)/shard_map/project/pallas_call | solution.py:134
  69.0 16.9 %all_to_all.16.parts_ref = bf16[4,128,512]{2,1,0:T(8,128)(2,1)} all-to-all(bf16[4,128,512]{2,1,0:T(8,128)(2,1)} %project.1), channel_id=1, replica_groups=mesh['ctx'=128,'tp'=4] {'tp'}, dimensions={0} | all-to-all | bytes 1048576 | tf_op jit(solution)/shard_map/all_to_all | solution.py:173
  85.9 1.8 %combine.1 = bf16[512,128]{1,0:T(8,128)(2,1)} custom-call(bf16[4,128,512]{2,1,0:T(8,128)(2,1)} %all_to_all.16.parts_ref), custom_call_target="tpu_custom_call" | custom-call | flops 1048576 | bytes 524288 | tf_op jit(solution)/shard_map/combine/pallas_call | solution.py:150
  (1 shorter events, 0.0 us)
Async XLA Ops:
  2.1 36.9 %all-to-all-start = ((bf16[128,12,128]{2,1,0:T(8,128)(2,1)}), bf16[128,12,128]{2,1,0:T(8,128)(2,1)S(1)}, u32[]{:S(2)}, u32[]{:S(2)}) async-start(bf16[128,12,128]{2,1,0:T(8,128)(2,1)} %copy.14), calls=%async_computation | async-start | bytes 1048576 | tf_op jit(solution)/shard_map/all_to_all | solution.py:166

commit v2 on v1

v2 whole, which is shorter than its diff:
```python
import jax
import jax.numpy as jnp
from jax import lax
from jax.experimental import pallas as pl
from jax.experimental.pallas import tpu as pltpu
from jax.sharding import PartitionSpec as P


GROUP = 16
LANES = 128
CHUNK = 1024
CORE_PAIRS = [(0, 1), (1, 0), (2, 3), (3, 2)]
CHIP_PAIRS = [(0, 2), (2, 0), (1, 3), (3, 1)]

f32 = jnp.float32
bf16 = jnp.bfloat16


def params(mib):
    return pltpu.CompilerParams(vmem_limit_bytes=mib << 20)


def table_kernel(rank_ref, filter_ref, table_ref, line_ref):
    seq_len = filter_ref.shape[1]
    own = (rank_ref[0] * 4 // GROUP) % 8
    line_ref[:, :LANES] = jnp.zeros((8, LANES), f32)
    for at in range(0, seq_len, CHUNK):
        piece = filter_ref[:, at : at + CHUNK].astype(f32)
        sub = lax.broadcasted_iota(jnp.int32, piece.shape, 0)
        chosen = jnp.sum(jnp.where(sub == own, piece, 0.0), axis=0, keepdims=True)
        line_ref[:, LANES + at : LANES + at + CHUNK] = jnp.broadcast_to(chosen, piece.shape)
    for at in range(0, seq_len, CHUNK):
        piece = pltpu.roll(line_ref[:, at : at + CHUNK + LANES], 0, 1, stride=1, stride_axis=0)
        for tile in range(LANES // 16):
            upper = pltpu.roll(piece, 16 * tile, 1)[:, LANES:]
            lower = pltpu.roll(piece, 16 * tile + 8, 1)[:, LANES:]
            both = jnp.concatenate([upper, lower], axis=0).astype(bf16)
            for block in range(CHUNK // LANES):
                to_row = (block % 2) * LANES + 16 * tile
                to_col = (at // LANES + block) // 2 * LANES
                table_ref[to_row : to_row + 16, to_col : to_col + LANES] = both[:, block * LANES : (block + 1) * LANES]


def make_table(rank, filters):
    seq_len = filters.shape[1]
    return pl.pallas_call(
        table_kernel,
        out_shape=jax.ShapeDtypeStruct((2 * LANES, seq_len // 2), bf16),
        grid_spec=pltpu.PrefetchScalarGridSpec(
            num_scalar_prefetch=1,
            grid=(1,),
            in_specs=[pl.BlockSpec((8, seq_len), lambda i, r: (r[0] * 4 // GROUP // 8, 0))],
            out_specs=pl.BlockSpec((2 * LANES, seq_len // 2), lambda i, r: (0, 0)),
            scratch_shapes=[pltpu.VMEM((8, LANES + seq_len), f32)],
        ),
        compiler_params=params(16),
        cost_estimate=pl.CostEstimate(flops=1 << 26, bytes_accessed=1 << 23, transcendentals=0),
        name="make_table",
    )(rank, filters)


def pattern(values):
    row = lax.broadcasted_iota(jnp.int32, (8, LANES), 0) % len(values)
    tile = jnp.full((8, LANES), values[-1], f32)
    for index in range(len(values) - 1):
        tile = jnp.where(row == index, values[index], tile)
    return tile


def conv_kernel(rank_ref, value_ref, far_ref, taps_ref, skip_ref, out_ref, pair_ref, sum_ref, table_ref, sems):
    pieces = [
        pltpu.make_async_copy(far_ref.at[:, at : at + CHUNK], table_ref.at[:, at : at + CHUNK], sems.at[at // CHUNK])
        for at in range(0, far_ref.shape[1], CHUNK)
    ]
    for piece in pieces:
        piece.start()
    blocks = value_ref.shape[0]
    rows = blocks * 4
    first = rank_ref[0] * 4
    value = value_ref[...].astype(f32)
    lane = lax.broadcasted_iota(jnp.int32, value.shape, 2)
    sub = lax.broadcasted_iota(jnp.int32, (blocks // 2, 8, LANES), 1)

    def delayed(array):
        return jnp.concatenate([jnp.zeros((1, 8, LANES), f32), array[:-1]], axis=0)

    def tile_of(offset):
        return pattern([taps_ref[offset, feature, first + c] for feature in (1, 2) for c in range(4)])[None]

    conv = tile_of(0) * value
    for offset in (1, 2):
        turned = pltpu.roll(value, offset, 2)
        conv = conv + tile_of(offset) * jnp.where(lane < offset, delayed(turned), turned)
    kv = (conv * pltpu.roll(conv, 4, 1)).astype(bf16).astype(f32)
    kv = kv.reshape(blocks // 2, 2, 8, LANES)
    even, odd = kv[:, 0], kv[:, 1]
    pair_ref[:, :LANES] = jnp.where(sub < 4, even, odd).reshape(rows, LANES).astype(bf16)
    pair_ref[:, LANES:] = jnp.where(sub < 4, delayed(odd), even).reshape(rows, LANES).astype(bf16)

    direct = pattern([skip_ref[first + c] for c in range(4)])[None]
    sum_ref[...] = (pair_ref[:, :LANES].astype(f32).reshape(rows // 8, 8, LANES) * direct).reshape(rows, LANES)
    for part in range(rows // 16):
        begin = part * 16
        if part * 256 % CHUNK == 0:
            pieces[part * 256 // CHUNK].wait()
        moved = jnp.dot(
            pair_ref[: rows - begin, :],
            table_ref[:, part * 256 : part * 256 + 256],
            preferred_element_type=f32,
        )
        sum_ref[begin:, :] += moved[:, :LANES]
        sum_ref[begin + 8 :, :] += moved[: rows - begin - 8, LANES:]
    out_ref[...] = sum_ref[...].astype(bf16)


def long_conv(rank, value, table, short_taps, skip_gain):
    rows = value.shape[0] * 4
    in_vmem = pl.BlockSpec(memory_space=pltpu.VMEM)
    in_smem = pl.BlockSpec(memory_space=pltpu.SMEM)
    return pl.pallas_call(
        conv_kernel,
        out_shape=jax.ShapeDtypeStruct((rows, LANES), bf16),
        in_specs=[in_smem, in_vmem, pl.BlockSpec(memory_space=pltpu.HBM), in_smem, in_smem],
        out_specs=in_vmem,
        scratch_shapes=[
            pltpu.VMEM((rows, 2 * LANES), bf16),
            pltpu.VMEM((rows, LANES), f32),
            pltpu.VMEM(table.shape, bf16),
            pltpu.SemaphoreType.DMA((table.shape[1] // CHUNK,)),
        ],
        compiler_params=params(16),
        cost_estimate=pl.CostEstimate(flops=1 << 31, bytes_accessed=1 << 20, transcendentals=0),
        name="long_conv",
    )(rank, value, table, short_taps, skip_gain)


def turn_kernel(weight_ref, out_ref):
    for at in range(0, weight_ref.shape[1], 256):
        out_ref[at : at + 256, :] = jnp.transpose(weight_ref[:, at : at + 256])


def turn(weight):
    return pl.pallas_call(
        turn_kernel,
        out_shape=jax.ShapeDtypeStruct(weight.shape[::-1], bf16),
        compiler_params=params(16),
        cost_estimate=pl.CostEstimate(flops=1 << 20, bytes_accessed=1 << 22, transcendentals=0),
        name="turn",
    )(weight)


def project_kernel(member_ref, q_ref, q_other_ref, mix_ref, mix_other_ref, weight_ref, weight_other_ref, out_ref):
    gated = (q_ref[...] * mix_ref[...].astype(f32)).astype(bf16)
    gated_other = (q_other_ref[...] * mix_other_ref[...].astype(f32)).astype(bf16)
    total = jnp.dot(weight_ref[...], gated, preferred_element_type=f32)
    total = total + jnp.dot(weight_other_ref[...], gated_other, preferred_element_type=f32)
    out_ref[...] = total.astype(out_ref.dtype)


def project(member, q, q_other, mix, mix_other, weight, weight_other, kind):
    channels, tokens = mix.shape
    whole = pl.BlockSpec((channels, tokens), lambda i, m: (0, 0))
    block = pl.BlockSpec((channels, channels), lambda i, m: (m[0], 0))
    return pl.pallas_call(
        project_kernel,
        out_shape=jax.ShapeDtypeStruct((channels, tokens), kind),
        grid_spec=pltpu.PrefetchScalarGridSpec(
            num_scalar_prefetch=1,
            grid=(1,),
            in_specs=[whole] * 4 + [block] * 2,
            out_specs=whole,
        ),
        compiler_params=params(16),
        cost_estimate=pl.CostEstimate(flops=1 << 27, bytes_accessed=1 << 21, transcendentals=0),
    )(member, q, q_other, mix, mix_other, weight, weight_other)


def local(features, short_taps, filters, skip_gain, out_weight):
    chan_tp, tok_local = features.shape[1:]
    ctx_count = lax.axis_size("ctx")
    chan_dev = chan_tp // ctx_count
    rank = jnp.full((1,), lax.axis_index("ctx"), jnp.int32)
    member = jnp.full((1,), lax.axis_index("tp"), jnp.int32)

    sent = features[1:].reshape(2, ctx_count, chan_dev, tok_local).transpose(1, 0, 2, 3)
    got = lax.all_to_all(sent, "ctx", 0, 0, tiled=True)
    got = got.reshape(ctx_count, 2 * chan_dev, tok_local)
    weight = turn(out_weight)
    weight_other = lax.ppermute(weight, "tp", CORE_PAIRS)
    table = make_table(rank, filters)

    mix = long_conv(rank, got, table, short_taps, skip_gain).reshape(ctx_count, chan_dev, tok_local)
    mix, late, late_taps = lax.optimization_barrier((mix, features, short_taps))
    mix = lax.all_to_all(mix, "ctx", 0, 0, tiled=True).reshape(chan_tp, tok_local)
    halo = lax.ppermute(late[0, :, tok_local - 2 :], "ctx", [(i, i + 1) for i in range(ctx_count - 1)])
    extended = jnp.concatenate([halo, late[0]], axis=1).astype(f32)
    q = sum(late_taps[j, 0][:, None] * extended[:, 2 - j : 2 - j + tok_local] for j in range(3))
    q_other = lax.ppermute(q, "tp", CORE_PAIRS)
    mix_other = lax.ppermute(mix, "tp", CORE_PAIRS)
    operands = (q, q_other, mix, mix_other, weight, weight_other)
    away = project(lax.bitwise_xor(member, 2), *operands, bf16)
    arrived = lax.ppermute(away, "tp", CHIP_PAIRS)
    home = project(member, *operands, f32)
    return (home + arrived.astype(f32)).astype(bf16)


def solution(mesh):
    placed = (P(None, "tp", "ctx"), P(None, None, "tp"), P("tp", None), P("tp"), P("tp", None))
    return jax.shard_map(
        local, mesh=mesh, in_specs=placed, out_specs=P("tp", "ctx"), check_vma=False
    )
```

time: 88.2 us -> 85.2 us (0.966)
  blocking collectives: 36 us -> 0 us
  starting transfers between devices: 19.3 us -> 46.5 us
  local copies, waits for them, and re-layouts: 4.53 us -> 6.67 us
  waiting for transfers between devices: 17.6 us -> 19.1 us
  other arithmetic: 0 us -> 1.23 us
    all_to_all x2 -> x0, blocking collectives: 36 us -> none  [the longest x1 19 us: local(): lax.all_to_all(gated, 'ctx', 0, 0, tiled=True).reshape(chan_tp, tok_local)]
    ppermute x0 -> x5, starting transfers between devices: none -> 24.7 us  [the longest x1 8.75 us: local(): weight_other = lax.ppermute(weight, 'tp', CORE_PAIRS)]
    all_to_all x0 -> x1, starting transfers between devices: none -> 8.63 us  [local(): lax.all_to_all(mix, 'ctx', 0, 0, tiled=True).reshape(chan_tp, tok_local)]
    all_to_all x1, waiting for transfers between devices: 17.6 us -> 9.08 us  [local(): got = lax.all_to_all(sent, 'ctx', 0, 0, tiled=True)]
    all_to_all x0 -> x1, waiting for transfers between devices: none -> 6.85 us  [local(): lax.all_to_all(mix, 'ctx', 0, 0, tiled=True).reshape(chan_tp, tok_local)]
    all_to_all x1, starting transfers between devices: 19.3 us -> 13.1 us  [local(): got = lax.all_to_all(sent, 'ctx', 0, 0, tiled=True)]
    unnamed x0 -> x14, local copies, waits for them, and re-layouts: none -> 5.75 us
    ppermute x0 -> x5, waiting for transfers between devices: none -> 3.2 us  [the longest x1 2.24 us: local(): arrived = lax.ppermute(away, 'tp', CHIP_PAIRS)]
  transfers between devices with their start and end apart: 1 -> 7, of which waited for: 1 -> 4; matrix products, arithmetic and copies ran while one was open for 0% -> 2% of each run, Pallas kernels for 0% -> 11%
where the time goes in v2:
time: 85.2 us; the launch traced here: 84.8 us
  starting transfers between devices  46.5 us (55%)
  waiting for transfers between devices  19.1 us (22%)
  Pallas kernels  11.1 us (13%)
  local copies, waits for them, and re-layouts  6.67 us (8%)
  other arithmetic  1.23 us (1%)
    all_to_all x1, starting transfers between devices, local(): got = lax.all_to_all(sent, 'ctx', 0, 0, tiled=True)  13.1 us
    all_to_all x1, waiting for transfers between devices, local(): got = lax.all_to_all(sent, 'ctx', 0, 0, tiled=True)  9.08 us
    ppermute x1, starting transfers between devices, local(): weight_other = lax.ppermute(weight, 'tp', CORE_PAIRS)  8.75 us
    all_to_all x1, starting transfers between devices, local(): lax.all_to_all(mix, 'ctx', 0, 0, tiled=True).reshape(chan_tp, tok_local)  8.63 us
    all_to_all x1, waiting for transfers between devices, local(): lax.all_to_all(mix, 'ctx', 0, 0, tiled=True).reshape(chan_tp, tok_local)  6.85 us
    unnamed x14, local copies, waits for them, and re-layouts  5.75 us
    pallas_call x1, Pallas kernels, long_conv(): pl.pallas_call(conv_kernel, out_shape=jax.ShapeDtypeStruct((rows, LANES),...  5.03 us
    ppermute x1, starting transfers between devices, local(): mix_other = lax.ppermute(mix, 'tp', CORE_PAIRS)  4.91 us
  transfers between devices with their start and end apart: 7, of which 4 were waited for; matrix products, arithmetic and copies ran while one was open for 2% of the time, Pallas kernels for 11%

profile of v2, /device:TPU:1, one launch (start us, length us, event | category | flops | bytes accessed | tf_op | source)
XLA Modules:
  0.0 84.8 jit_solution(6902988765998913698)
XLA Ops:
  0.0 1.6 %copy-done.2 = bf16[512,2048]{1,0:T(8,128)(2,1)S(1)} copy-done((bf16[512,2048]{1,0:T(8,128)(2,1)S(1)}, bf16[512,2048]{1,0:T(8,128)(2,1)}, u32[]{:S(2)}) %copy-start.2) | copy-done | bytes 2097176
  1.6 0.6 turn.1.weight_ref
  2.2 8.7 %collective-permute-start.3 = (bf16[2048,512]{1,0:T(8,128)(2,1)S(1)}, bf16[2048,512]{1,0:T(8,128)(2,1)}, u32[]{:S(2)}, u32[]{:S(2)}) collective-permute-start(bf16[2048,512]{1,0:T(8,128)(2,1)S(1)} %turn.1.weight_ref), channel_id=1, source_target_pairs={{0,1},{1,0},{2,3},{3,2},{4,5},{5,4},{6,7},{7,6},{8,9},{9,8},{10,11... | collective-permute-start | bytes 6291464 | tf_op jit(solution)/shard_map/ppermute | solution.py:189
  11.0 0.8 copy.8
  11.8 13.1 %all-to-all-start = ((bf16[128,2,4,128]{3,2,1,0:T(4,128)(2,1)}), bf16[128,2,4,128]{3,2,1,0:T(4,128)(2,1)S(1)}, u32[]{:S(2)}, u32[]{:S(2)}) async-start(bf16[128,2,4,128]{3,2,1,0:T(4,128)(2,1)} %bitcast.20), calls=%async_computation | async-start | bytes 524288 | tf_op jit(solution)/shard_map/all_to_all | solution.py:186
  24.9 2.5 %make_table.1.far_ref = bf16[256,8192]{1,0:T(8,128)(2,1)S(1)} custom-call(s32[1]{0:T(128)} %bitcast.1.rank_ref, bf16[32,16384]{1,0:T(8,128)(2,1)S(1)} %copy-done.3), custom_call_target="tpu_custom_call" | custom-call | flops 67108864 | bytes 8388608 | tf_op jit(solution)/shard_map/make_table/pallas_call | solution.py:46
  27.4 1.9 %copy-done = bf16[256,8192]{1,0:T(8,128)(2,1)} copy-done((bf16[256,8192]{1,0:T(8,128)(2,1)}, bf16[256,8192]{1,0:T(8,128)(2,1)S(1)}, u32[]{:S(2)}) %copy-start) | copy-done | bytes 4194328
  29.3 9.1 %all-to-all-done = bf16[128,2,4,128]{3,2,1,0:T(4,128)(2,1)S(1)} async-done(((bf16[128,2,4,128]{3,2,1,0:T(4,128)(2,1)}), bf16[128,2,4,128]{3,2,1,0:T(4,128)(2,1)S(1)}, u32[]{:S(2)}, u32[]{:S(2)}) %all-to-all-start) | async-done | bytes 262176 | tf_op jit(solution)/shard_map/all_to_all | solution.py:186
  38.4 2.2 %copy-done.1 = bf16[256,8192]{1,0:T(8,128)(2,1)S(1)} copy-done((bf16[256,8192]{1,0:T(8,128)(2,1)S(1)}, bf16[256,8192]{1,0:T(8,128)(2,1)}, u32[]{:S(2)}) %copy-start.1) | copy-done | bytes 4194328
  40.6 5.0 %long_conv.1 = bf16[512,128]{1,0:T(8,128)(2,1)} custom-call(s32[1]{0:T(128)} %bitcast.1.rank_ref, bf16[128,8,128]{2,1,0:T(8,128)(2,1)S(1)} %bitcast.19, bf16[256,8192]{1,0:T(8,128)(2,1)S(1)} %copy-done.1, f32[3,3,512]{2,1,0:T(4,128)S(1)} %copy-done.4, f32[512]{0:T(512)S(1)} %copy-done.5), custom_call_target="tpu_custom_call" | custom-call | flops 2147483648 | bytes 1048576 | tf_op jit(solution)/shard_map/long_conv/pallas_call | solution.py:120
  45.7 0.1 slice_bitcast_fusion.1
  45.8 2.9 %collective-permute-start = (bf16[512,2]{1,0:T(8,128)(2,1)S(1)}, bf16[512,2]{1,0:T(8,128)(2,1)S(1)}, u32[]{:S(2)}, u32[]{:S(2)}) collective-permute-start(bf16[512,2]{1,0:T(8,128)(2,1)S(1)} %slice_bitcast_fusion.1), channel_id=1, source_target_pairs={{0,4},{4,8},{8,12},{12,16},{16,20},{20,24},{24,28},{28,32},{32,36}... | collective-permute-start | bytes 6152 | tf_op jit(solution)/shard_map/ppermute | solution.py:195
  48.7 8.6 %all-to-all-start.1 = ((bf16[128,4,128]{2,1,0:T(4,128)(2,1)}), bf16[128,4,128]{2,1,0:T(4,128)(2,1)S(1)}, u32[]{:S(2)}, u32[]{:S(2)}) async-start(bf16[128,4,128]{2,1,0:T(4,128)(2,1)} %bitcast.5), calls=%async_computation.1 | async-start | bytes 262144 | tf_op jit(solution)/shard_map/all_to_all | solution.py:194
  57.4 0.1 maximum_convert_fusion
  57.5 0.4 fusion.q_ref
  58.0 3.8 %collective-permute-start.1 = (f32[512,128]{1,0:T(8,128)S(1)}, f32[512,128]{1,0:T(8,128)S(1)}, u32[]{:S(2)}, u32[]{:S(2)}) collective-permute-start(f32[512,128]{1,0:T(8,128)S(1)} %fusion.q_ref), channel_id=1, source_target_pairs={{0,1},{1,0},{2,3},{3,2},{4,5},{5,4},{6,7},{7,6},{8,9},{9,8},{10,11... | collective-permute-start | bytes 786440 | tf_op jit(solution)/shard_map/ppermute | solution.py:198
  61.8 6.8 %all-to-all-done.1 = bf16[128,4,128]{2,1,0:T(4,128)(2,1)S(1)} async-done(((bf16[128,4,128]{2,1,0:T(4,128)(2,1)}), bf16[128,4,128]{2,1,0:T(4,128)(2,1)S(1)}, u32[]{:S(2)}, u32[]{:S(2)}) %all-to-all-start.1) | async-done | bytes 131104 | tf_op jit(solution)/shard_map/all_to_all | solution.py:194
  68.6 4.9 %collective-permute-start.2 = (bf16[512,128]{1,0:T(8,128)(2,1)S(1)}, bf16[512,128]{1,0:T(8,128)(2,1)S(1)}, u32[]{:S(2)}, u32[]{:S(2)}) collective-permute-start(bf16[512,128]{1,0:T(8,128)(2,1)S(1)} %bitcast.16), channel_id=1, source_target_pairs={{0,1},{1,0},{2,3},{3,2},{4,5},{5,4},{6,7},{7,6},{8,9},{9,8},{10,11... | collective-permute-start | bytes 393224 | tf_op jit(solution)/shard_map/ppermute | solution.py:199
  73.5 0.9 %collective-permute-done.2.mix_other_ref = bf16[512,128]{1,0:T(8,128)(2,1)S(1)} collective-permute-done((bf16[512,128]{1,0:T(8,128)(2,1)S(1)}, bf16[512,128]{1,0:T(8,128)(2,1)S(1)}, u32[]{:S(2)}, u32[]{:S(2)}) %collective-permute-start.2) | collective-permute-done | bytes 131104 | tf_op jit(solution)/shard_map/ppermute | solution.py:199
  74.5 1.5 %shard_map.56 = bf16[512,128]{1,0:T(8,128)(2,1)S(1)} custom-call(s32[1]{0:T(128)S(6)} %xor.3.member_ref, f32[512,128]{1,0:T(8,128)S(1)} %fusion.q_ref, f32[512,128]{1,0:T(8,128)S(1)} %collective-permute-done.1.q_other_ref, bf16[512,128]{1,0:T(8,128)(2,1)S(1)} %bitcast.17, bf16[512,128]{1,0:T(8,128)(2,1)S(1)} %collective-permute-done.2.mix_other_ref, ...), custom_call_target="tpu_custom_call" | custom-call | flops 134217728 | bytes 2097152 | tf_op jit(solution)/shard_map/pallas_call | solution.py:164
  76.0 4.4 %collective-permute-start.4 = (bf16[512,128]{1,0:T(8,128)(2,1)S(1)}, bf16[512,128]{1,0:T(8,128)(2,1)S(1)}, u32[]{:S(2)}, u32[]{:S(2)}) collective-permute-start(bf16[512,128]{1,0:T(8,128)(2,1)S(1)} %shard_map.56), channel_id=1, source_target_pairs={{0,2},{2,0},{1,3},{3,1},{4,6},{6,4},{5,7},{7,5},{8,10},{10,8},{9,1... | collective-permute-start | bytes 393224 | tf_op jit(solution)/shard_map/ppermute | solution.py:202
  80.3 1.5 %shard_map.55 = f32[512,128]{1,0:T(8,128)S(1)} custom-call(s32[1]{0:T(128)} %bitcast.member_ref, f32[512,128]{1,0:T(8,128)S(1)} %fusion.q_ref, f32[512,128]{1,0:T(8,128)S(1)} %collective-permute-done.1.q_other_ref, bf16[512,128]{1,0:T(8,128)(2,1)S(1)} %bitcast.18, bf16[512,128]{1,0:T(8,128)(2,1)S(1)} %collective-permute-done.2.mix_other_ref, ...), custom_call_target="tpu_custom_call" | custom-call | flops 134217728 | bytes 2097152 | tf_op jit(solution)/shard_map/pallas_call | solution.py:164
  81.8 2.2 %collective-permute-done.4 = bf16[512,128]{1,0:T(8,128)(2,1)S(1)} collective-permute-done((bf16[512,128]{1,0:T(8,128)(2,1)S(1)}, bf16[512,128]{1,0:T(8,128)(2,1)S(1)}, u32[]{:S(2)}, u32[]{:S(2)}) %collective-permute-start.4) | collective-permute-done | bytes 131104 | tf_op jit(solution)/shard_map/ppermute | solution.py:202
  84.1 0.7 add_convert_fusion
  (18 shorter events, 0.1 us)
Async XLA Ops:
  0.0 1.6 %copy-start.2 = (bf16[512,2048]{1,0:T(8,128)(2,1)S(1)}, bf16[512,2048]{1,0:T(8,128)(2,1)}, u32[]{:S(2)}) copy-start(bf16[512,2048]{1,0:T(8,128)(2,1)} %weight_ref.1) | copy-start | bytes 6291460
  1.6 9.4 %slice-start = ((bf16[3,512,128]{2,1,0:T(8,128)(2,1)}), bf16[2,512,128]{2,1,0:T(8,128)(2,1)S(1)}, s32[]{:S(2)}) async-start(bf16[3,512,128]{2,1,0:T(8,128)(2,1)} %param.5), calls=%async_computation.2 | async-start | bytes 524288 | tf_op jit(solution)/shard_map/slice | solution.py:185
  1.6 23.3 %copy-start.3 = (bf16[32,16384]{1,0:T(8,128)(2,1)S(1)}, bf16[32,16384]{1,0:T(8,128)(2,1)}, u32[]{:S(2)}) copy-start(bf16[32,16384]{1,0:T(8,128)(2,1)} %filter_ref.1) | copy-start | bytes 3145732
  2.2 72.3 %collective-permute-start.3 = (bf16[2048,512]{1,0:T(8,128)(2,1)S(1)}, bf16[2048,512]{1,0:T(8,128)(2,1)}, u32[]{:S(2)}, u32[]{:S(2)}) collective-permute-start(bf16[2048,512]{1,0:T(8,128)(2,1)S(1)} %turn.1.weight_ref), channel_id=1, source_target_pairs={{0,1},{1,0},{2,3},{3,2},{4,5},{5,4},{6,7},{7,6},{8,9},{9,8},{10,11... | collective-permute-start | bytes 6291464 | tf_op jit(solution)/shard_map/ppermute | solution.py:189
  11.8 26.7 %all-to-all-start = ((bf16[128,2,4,128]{3,2,1,0:T(4,128)(2,1)}), bf16[128,2,4,128]{3,2,1,0:T(4,128)(2,1)S(1)}, u32[]{:S(2)}, u32[]{:S(2)}) async-start(bf16[128,2,4,128]{3,2,1,0:T(4,128)(2,1)} %bitcast.20), calls=%async_computation | async-start | bytes 524288 | tf_op jit(solution)/shard_map/all_to_all | solution.py:186
  24.9 13.5 %copy-start.4 = (f32[3,3,512]{2,1,0:T(4,128)S(1)}, f32[3,3,512]{2,1,0:T(4,128)}, u32[]{:S(2)}) copy-start(f32[3,3,512]{2,1,0:T(4,128)} %taps_ref.1) | copy-start | bytes 55300
  24.9 13.5 %copy-start.5 = (f32[512]{0:T(512)S(1)}, f32[512]{0:T(512)}, u32[]{:S(2)}) copy-start(f32[512]{0:T(512)} %skip_ref.1) | copy-start | bytes 6148
  27.4 2.0 %copy-start = (bf16[256,8192]{1,0:T(8,128)(2,1)}, bf16[256,8192]{1,0:T(8,128)(2,1)S(1)}, u32[]{:S(2)}) copy-start(bf16[256,8192]{1,0:T(8,128)(2,1)S(1)} %make_table.1.far_ref) | copy-start | bytes 12582916
  38.4 2.2 %copy-start.1 = (bf16[256,8192]{1,0:T(8,128)(2,1)S(1)}, bf16[256,8192]{1,0:T(8,128)(2,1)}, u32[]{:S(2)}) copy-start(bf16[256,8192]{1,0:T(8,128)(2,1)} %copy-done) | copy-start | bytes 12582916
  40.6 5.0 %copy-start.6 = (bf16[3,512,128]{2,1,0:T(8,128)(2,1)S(1)}, bf16[3,512,128]{2,1,0:T(8,128)(2,1)}, u32[]{:S(2)}) copy-start(bf16[3,512,128]{2,1,0:T(8,128)(2,1)} %param.5) | copy-start | bytes 1179652
  45.8 11.6 %collective-permute-start = (bf16[512,2]{1,0:T(8,128)(2,1)S(1)}, bf16[512,2]{1,0:T(8,128)(2,1)S(1)}, u32[]{:S(2)}, u32[]{:S(2)}) collective-permute-start(bf16[512,2]{1,0:T(8,128)(2,1)S(1)} %slice_bitcast_fusion.1), channel_id=1, source_target_pairs={{0,4},{4,8},{8,12},{12,16},{16,20},{20,24},{24,28},{28,32},{32,36}... | collective-permute-start | bytes 6152 | tf_op jit(solution)/shard_map/ppermute | solution.py:195
  48.7 19.9 %all-to-all-start.1 = ((bf16[128,4,128]{2,1,0:T(4,128)(2,1)}), bf16[128,4,128]{2,1,0:T(4,128)(2,1)S(1)}, u32[]{:S(2)}, u32[]{:S(2)}) async-start(bf16[128,4,128]{2,1,0:T(4,128)(2,1)} %bitcast.5), calls=%async_computation.1 | async-start | bytes 262144 | tf_op jit(solution)/shard_map/all_to_all | solution.py:194
  58.0 15.6 %collective-permute-start.1 = (f32[512,128]{1,0:T(8,128)S(1)}, f32[512,128]{1,0:T(8,128)S(1)}, u32[]{:S(2)}, u32[]{:S(2)}) collective-permute-start(f32[512,128]{1,0:T(8,128)S(1)} %fusion.q_ref), channel_id=1, source_target_pairs={{0,1},{1,0},{2,3},{3,2},{4,5},{5,4},{6,7},{7,6},{8,9},{9,8},{10,11... | collective-permute-start | bytes 786440 | tf_op jit(solution)/shard_map/ppermute | solution.py:198
  68.6 5.9 %collective-permute-start.2 = (bf16[512,128]{1,0:T(8,128)(2,1)S(1)}, bf16[512,128]{1,0:T(8,128)(2,1)S(1)}, u32[]{:S(2)}, u32[]{:S(2)}) collective-permute-start(bf16[512,128]{1,0:T(8,128)(2,1)S(1)} %bitcast.16), channel_id=1, source_target_pairs={{0,1},{1,0},{2,3},{3,2},{4,5},{5,4},{6,7},{7,6},{8,9},{9,8},{10,11... | collective-permute-start | bytes 393224 | tf_op jit(solution)/shard_map/ppermute | solution.py:199
  76.0 8.1 %collective-permute-start.4 = (bf16[512,128]{1,0:T(8,128)(2,1)S(1)}, bf16[512,128]{1,0:T(8,128)(2,1)S(1)}, u32[]{:S(2)}, u32[]{:S(2)}) collective-permute-start(bf16[512,128]{1,0:T(8,128)(2,1)S(1)} %shard_map.56), channel_id=1, source_target_pairs={{0,2},{2,0},{1,3},{3,1},{4,6},{6,4},{5,7},{7,5},{8,10},{10,8},{9,1... | collective-permute-start | bytes 393224 | tf_op jit(solution)/shard_map/ppermute | solution.py:202

commit v3 on v2

v3 whole, which is shorter than its diff:
```python
import jax
import jax.numpy as jnp
from jax import lax
from jax.experimental import pallas as pl
from jax.experimental.pallas import tpu as pltpu
from jax.sharding import PartitionSpec as P


GROUP = 16
LANES = 128
CHUNK = 1024
TABLE_STEPS = 4
LEAD = 48
CORE_PAIRS = [(0, 1), (1, 0), (2, 3), (3, 2)]
CHIP_PAIRS = [(0, 2), (2, 0), (1, 3), (3, 1)]

f32 = jnp.float32
bf16 = jnp.bfloat16


def params(mib):
    return pltpu.CompilerParams(vmem_limit_bytes=mib << 20)


def table_kernel(rank_ref, filter_ref, table_ref, line_ref):
    length = filter_ref.shape[1]
    own = (rank_ref[0] * 4 // GROUP) % 8

    @pl.when(pl.program_id(0) == 0)
    def _():
        line_ref[:, :LANES] = jnp.zeros((8, LANES), f32)

    @pl.when(pl.program_id(0) > 0)
    def _():
        line_ref[:, :LANES] = line_ref[:, length:]

    for at in range(0, length, CHUNK):
        piece = filter_ref[:, at : at + CHUNK].astype(f32)
        sub = lax.broadcasted_iota(jnp.int32, piece.shape, 0)
        chosen = jnp.sum(jnp.where(sub == own, piece, 0.0), axis=0, keepdims=True)
        line_ref[:, LANES + at : LANES + at + CHUNK] = jnp.broadcast_to(chosen, piece.shape)
    for at in range(0, length, CHUNK):
        piece = pltpu.roll(line_ref[:, at : at + CHUNK + LANES], 0, 1, stride=1, stride_axis=0)
        for tile in range(LANES // 16):
            upper = pltpu.roll(piece, 16 * tile, 1)[:, LANES:]
            lower = pltpu.roll(piece, 16 * tile + 8, 1)[:, LANES:]
            both = jnp.concatenate([upper, lower], axis=0).astype(bf16)
            for block in range(CHUNK // LANES):
                to_row = (block % 2) * LANES + 16 * tile
                to_col = (at // LANES + block) // 2 * LANES
                table_ref[to_row : to_row + 16, to_col : to_col + LANES] = both[:, block * LANES : (block + 1) * LANES]


def make_table(rank, filters):
    seq_len = filters.shape[1]
    length = seq_len // TABLE_STEPS
    return pl.pallas_call(
        table_kernel,
        out_shape=jax.ShapeDtypeStruct((2 * LANES, seq_len // 2), bf16),
        grid_spec=pltpu.PrefetchScalarGridSpec(
            num_scalar_prefetch=1,
            grid=(TABLE_STEPS,),
            in_specs=[pl.BlockSpec((8, length), lambda i, r: (r[0] * 4 // GROUP // 8, i))],
            out_specs=pl.BlockSpec((2 * LANES, length // 2), lambda i, r: (0, i)),
            scratch_shapes=[pltpu.VMEM((8, LANES + length), f32)],
        ),
        compiler_params=params(60),
        cost_estimate=pl.CostEstimate(flops=1 << 26, bytes_accessed=1 << 23, transcendentals=0),
        name="make_table",
    )(rank, filters)


def pattern(values):
    row = lax.broadcasted_iota(jnp.int32, (8, LANES), 0) % len(values)
    tile = jnp.full((8, LANES), values[-1], f32)
    for index in range(len(values) - 1):
        tile = jnp.where(row == index, values[index], tile)
    return tile


def conv_kernel(rank_ref, value_ref, far_ref, taps_ref, skip_ref, out_ref, pair_ref, sum_ref, table_ref, sems):
    pieces = [
        pltpu.make_async_copy(far_ref.at[:, at : at + CHUNK], table_ref.at[:, at : at + CHUNK], sems.at[at // CHUNK])
        for at in range(0, far_ref.shape[1], CHUNK)
    ]
    for piece in pieces:
        piece.start()
    blocks = value_ref.shape[0]
    rows = blocks * 4
    first = rank_ref[0] * 4
    value = value_ref[...].astype(f32)
    lane = lax.broadcasted_iota(jnp.int32, value.shape, 2)
    sub = lax.broadcasted_iota(jnp.int32, (blocks // 2, 8, LANES), 1)

    def delayed(array):
        return jnp.concatenate([jnp.zeros((1, 8, LANES), f32), array[:-1]], axis=0)

    def tile_of(offset):
        return pattern([taps_ref[offset, feature, first + c] for feature in (1, 2) for c in range(4)])[None]

    conv = tile_of(0) * value
    for offset in (1, 2):
        turned = pltpu.roll(value, offset, 2)
        conv = conv + tile_of(offset) * jnp.where(lane < offset, delayed(turned), turned)
    kv = (conv * pltpu.roll(conv, 4, 1)).astype(bf16).astype(f32)
    kv = kv.reshape(blocks // 2, 2, 8, LANES)
    even, odd = kv[:, 0], kv[:, 1]
    pair_ref[:LEAD, :] = jnp.zeros((LEAD, 2 * LANES), bf16)
    pair_ref[LEAD:, :LANES] = jnp.where(sub < 4, even, odd).reshape(rows, LANES).astype(bf16)
    pair_ref[LEAD:, LANES:] = jnp.where(sub < 4, delayed(odd), even).reshape(rows, LANES).astype(bf16)

    direct = pattern([skip_ref[first + c] for c in range(4)])[None]
    sum_ref[...] = (pair_ref[LEAD:, :LANES].astype(f32).reshape(rows // 8, 8, LANES) * direct).reshape(rows, LANES)
    for index, piece in enumerate(pieces):
        begin = 64 * index
        piece.wait()
        left = [pair_ref[LEAD - 16 * s : LEAD - 16 * s + rows - begin, :] for s in range(4)]
        right = [table_ref[:, index * CHUNK + 256 * s : index * CHUNK + 256 * (s + 1)] for s in range(4)]
        moved = jnp.dot(
            jnp.concatenate(left, axis=1), jnp.concatenate(right, axis=0), preferred_element_type=f32
        )
        sum_ref[begin:, :] += moved[:, :LANES]
        sum_ref[begin + 8 :, :] += moved[: rows - begin - 8, LANES:]
    out_ref[...] = sum_ref[...].astype(bf16)


def long_conv(rank, value, table, short_taps, skip_gain):
    rows = value.shape[0] * 4
    in_vmem = pl.BlockSpec(memory_space=pltpu.VMEM)
    in_smem = pl.BlockSpec(memory_space=pltpu.SMEM)
    return pl.pallas_call(
        conv_kernel,
        out_shape=jax.ShapeDtypeStruct((rows, LANES), bf16),
        in_specs=[in_smem, in_vmem, pl.BlockSpec(memory_space=pltpu.HBM), in_smem, in_smem],
        out_specs=in_vmem,
        scratch_shapes=[
            pltpu.VMEM((LEAD + rows, 2 * LANES), bf16),
            pltpu.VMEM((rows, LANES), f32),
            pltpu.VMEM(table.shape, bf16),
            pltpu.SemaphoreType.DMA((table.shape[1] // CHUNK,)),
        ],
        compiler_params=params(16),
        cost_estimate=pl.CostEstimate(flops=1 << 31, bytes_accessed=1 << 20, transcendentals=0),
        name="long_conv",
    )(rank, value, table, short_taps, skip_gain)


def turn_kernel(core_ref, weight_ref, out_ref):
    out_ref[...] = jnp.transpose(weight_ref[...])


def turn(core, weight):
    width = weight.shape[0]
    return pl.pallas_call(
        turn_kernel,
        out_shape=jax.ShapeDtypeStruct((weight.shape[1] // 2, width), bf16),
        grid_spec=pltpu.PrefetchScalarGridSpec(
            num_scalar_prefetch=1,
            grid=(2,),
            in_specs=[pl.BlockSpec((width, width), lambda i, c: (0, 2 * i + c[0]))],
            out_specs=pl.BlockSpec((width, width), lambda i, c: (i, 0)),
        ),
        compiler_params=params(16),
        cost_estimate=pl.CostEstimate(flops=1 << 20, bytes_accessed=1 << 21, transcendentals=0),
        name="turn",
    )(core, weight)


def edge_kernel(rows_ref, out_ref):
    out_ref[...] = jnp.transpose(rows_ref[0])[LANES - 16 :, :]


def edge(features):
    channels, tokens = features.shape[1:]
    return pl.pallas_call(
        edge_kernel,
        out_shape=jax.ShapeDtypeStruct((16, channels), bf16),
        grid=(1,),
        in_specs=[pl.BlockSpec((1, channels, tokens), lambda i: (0, 0, 0))],
        out_specs=pl.BlockSpec((16, channels), lambda i: (0, 0)),
        compiler_params=params(16),
        cost_estimate=pl.CostEstimate(flops=1 << 16, bytes_accessed=1 << 17, transcendentals=0),
        name="edge",
    )(features)


def query_kernel(rows_ref, halo_ref, taps_ref, out_ref):
    value = rows_ref[0].astype(f32)
    lane = lax.broadcasted_iota(jnp.int32, value.shape, 1)
    halo = jnp.transpose(halo_ref[...].astype(f32))
    taps = taps_ref[:, 0, :]
    taps = jnp.transpose(jnp.concatenate([taps, jnp.zeros((5, taps.shape[1]), f32)], axis=0))
    once = jnp.where(lane == 0, halo[:, 15:16], pltpu.roll(value, 1, 1))
    twice = jnp.where(lane == 0, halo[:, 14:15], jnp.where(lane == 1, halo[:, 15:16], pltpu.roll(value, 2, 1)))
    out_ref[...] = taps[:, 0:1] * value + taps[:, 1:2] * once + taps[:, 2:3] * twice


def query_conv(features, halo, short_taps):
    channels, tokens = features.shape[1:]
    return pl.pallas_call(
        query_kernel,
        out_shape=jax.ShapeDtypeStruct((channels, tokens), f32),
        grid=(1,),
        in_specs=[
            pl.BlockSpec((1, channels, tokens), lambda i: (0, 0, 0)),
            pl.BlockSpec(halo.shape, lambda i: (0, 0)),
            pl.BlockSpec(short_taps.shape, lambda i: (0, 0, 0)),
        ],
        out_specs=pl.BlockSpec((channels, tokens), lambda i: (0, 0)),
        compiler_params=params(16),
        cost_estimate=pl.CostEstimate(flops=1 << 20, bytes_accessed=1 << 19, transcendentals=0),
        name="query_conv",
    )(features, halo, short_taps)


def project_kernel(chip_ref, q_ref, q_other_ref, mix_ref, mix_other_ref, weight_ref, weight_other_ref, out_ref):
    width = out_ref.shape[0]
    block = pl.ds(pl.multiple_of(chip_ref[0] * width, width), width)
    gated = (q_ref[...] * mix_ref[...].astype(f32)).astype(bf16)
    gated_other = (q_other_ref[...] * mix_other_ref[...].astype(f32)).astype(bf16)
    total = jnp.dot(weight_ref[block, :], gated, preferred_element_type=f32)
    total = total + jnp.dot(weight_other_ref[block, :], gated_other, preferred_element_type=f32)
    out_ref[...] = total.astype(out_ref.dtype)


def project(chip, q, q_other, mix, mix_other, weight, weight_other, kind):
    in_vmem = pl.BlockSpec(memory_space=pltpu.VMEM)
    return pl.pallas_call(
        project_kernel,
        out_shape=jax.ShapeDtypeStruct(mix.shape, kind),
        in_specs=[pl.BlockSpec(memory_space=pltpu.SMEM)] + [in_vmem] * 6,
        out_specs=in_vmem,
        compiler_params=params(16),
        cost_estimate=pl.CostEstimate(flops=1 << 27, bytes_accessed=1 << 21, transcendentals=0),
    )(chip, q, q_other, mix, mix_other, weight, weight_other)


def local(features, short_taps, filters, skip_gain, out_weight):
    chan_tp, tok_local = features.shape[1:]
    ctx_count = lax.axis_size("ctx")
    chan_dev = chan_tp // ctx_count
    rank = jnp.full((1,), lax.axis_index("ctx"), jnp.int32)
    chip = jnp.full((1,), lax.axis_index("tp") // 2, jnp.int32)
    core = jnp.full((1,), lax.axis_index("tp") % 2, jnp.int32)

    sent = features[1:].reshape(2, ctx_count, chan_dev, tok_local).transpose(1, 0, 2, 3)
    got = lax.all_to_all(sent, "ctx", 0, 0, tiled=True)
    got = got.reshape(ctx_count, 2 * chan_dev, tok_local)
    weight_given = turn(1 - core, out_weight)
    table = pltpu.with_memory_space_constraint(make_table(rank, filters), pltpu.HBM)
    last = edge(features)
    halo = lax.ppermute(last, "ctx", [(i, i + 1) for i in range(ctx_count - 1)])
    weight_other = lax.ppermute(weight_given, "tp", CORE_PAIRS)

    mix = long_conv(rank, got, table, short_taps, skip_gain).reshape(ctx_count, chan_dev, tok_local)
    mix = lax.all_to_all(mix, "ctx", 0, 0, tiled=True).reshape(chan_tp, tok_local)
    weight = turn(core, out_weight)
    q = query_conv(features, halo, short_taps)
    q_other = lax.ppermute(q, "tp", CORE_PAIRS)
    mix_other = lax.ppermute(mix, "tp", CORE_PAIRS)
    operands = (q, q_other, mix, mix_other, weight, weight_other)
    away = project(1 - chip, *operands, bf16)
    arrived = lax.ppermute(away, "tp", CHIP_PAIRS)
    home = project(chip, *operands, f32)
    return (home + arrived.astype(f32)).astype(bf16)


def solution(mesh):
    placed = (P(None, "tp", "ctx"), P(None, None, "tp"), P("tp", None), P("tp"), P("tp", None))
    return jax.shard_map(
        local, mesh=mesh, in_specs=placed, out_specs=P("tp", "ctx"), check_vma=False
    )
```

time: 85.2 us -> 83.6 us (0.981)
  the two profiles are of different devices: /device:TPU:1 before, /device:TPU:32 now
where the time goes in v3:
time: 83.6 us; the launch traced here: 82.9 us
  starting transfers between devices  46.5 us (56%)
  Pallas kernels  17 us (20%)
  waiting for transfers between devices  11.3 us (14%)
  local copies, waits for them, and re-layouts  7.18 us (9%)
    all_to_all x1, starting transfers between devices, local(): got = lax.all_to_all(sent, 'ctx', 0, 0, tiled=True)  18.3 us
    all_to_all x1, starting transfers between devices, local(): lax.all_to_all(mix, 'ctx', 0, 0, tiled=True).reshape(chan_tp, tok_local)  14 us
    ppermute x1, waiting for transfers between devices, local(): halo = lax.ppermute(last, 'ctx', [(i, i + 1) for i in range(ctx_count - 1)])  6.47 us
    pallas_call x1, Pallas kernels, long_conv(): pl.pallas_call(conv_kernel, out_shape=jax.ShapeDtypeStruct((rows, LANES),...  5.86 us
    unnamed x18, local copies, waits for them, and re-layouts  5.39 us
    pallas_call x1, Pallas kernels, make_table(): pl.pallas_call(table_kernel, out_shape=jax.ShapeDtypeStruct((2 * LANES, s...  5.15 us
    ppermute x1, starting transfers between devices, local(): arrived = lax.ppermute(away, 'tp', CHIP_PAIRS)  4.63 us
    ppermute x1, starting transfers between devices, local(): halo = lax.ppermute(last, 'ctx', [(i, i + 1) for i in range(ctx_count - 1)])  3.38 us
  transfers between devices with their start and end apart: 7, of which 4 were waited for; matrix products, arithmetic and copies ran while one was open for 0% of the time, Pallas kernels for 19%

profile of v3, /device:TPU:32, one launch (start us, length us, event | category | flops | bytes accessed | tf_op | source)
XLA Modules:
  0.0 82.9 jit_solution(7243267230212779170)
XLA Ops:
  0.0 1.0 %slice.3 = bf16[2,512,128]{2,1,0:T(8,128)(2,1)S(1)} slice(bf16[3,512,128]{2,1,0:T(8,128)(2,1)} %rows_ref.3), slice={[1:3], [0:512], [0:128]} | slice | bytes 524288 | tf_op jit(solution)/shard_map/slice | solution.py:246
  1.0 0.8 copy.8
  1.8 18.3 %all-to-all-start = ((bf16[128,2,4,128]{3,2,1,0:T(4,128)(2,1)}), bf16[128,2,4,128]{3,2,1,0:T(4,128)(2,1)S(1)}, u32[]{:S(2)}, u32[]{:S(2)}) async-start(bf16[128,2,4,128]{3,2,1,0:T(4,128)(2,1)} %bitcast.9), calls=%async_computation | async-start | bytes 524288 | tf_op jit(solution)/shard_map/all_to_all | solution.py:247
  20.1 1.6 %copy-done = bf16[512,2048]{1,0:T(8,128)(2,1)S(1)} copy-done((bf16[512,2048]{1,0:T(8,128)(2,1)S(1)}, bf16[512,2048]{1,0:T(8,128)(2,1)}, u32[]{:S(2)}) %copy-start) | copy-done | bytes 2097176
  21.7 1.3 %turn.3 = bf16[1024,512]{1,0:T(8,128)(2,1)} custom-call(s32[1]{0:T(128)S(6)} %sub.11.core_ref, bf16[512,2048]{1,0:T(8,128)(2,1)S(1)} %copy-done), custom_call_target="tpu_custom_call" | custom-call | flops 1048576 | bytes 2097152 | tf_op jit(solution)/shard_map/turn/pallas_call | solution.py:154
  23.0 1.9 %collective-permute-start.3 = (bf16[1024,512]{1,0:T(8,128)(2,1)}, bf16[1024,512]{1,0:T(8,128)(2,1)S(1)}, u32[]{:S(2)}, u32[]{:S(2)}) collective-permute-start(bf16[1024,512]{1,0:T(8,128)(2,1)} %turn.3), channel_id=1, source_target_pairs={{0,1},{1,0},{2,3},{3,2},{4,5},{5,4},{6,7},{7,6},{8,9},{9,8},{10,11... | collective-permute-start | bytes 3145736 | tf_op jit(solution)/shard_map/ppermute | solution.py:253
  24.9 5.2 %make_table.1.far_ref = bf16[256,8192]{1,0:T(8,128)(2,1)} custom-call(s32[1]{0:T(128)} %bitcast.1.rank_ref, bf16[32,16384]{1,0:T(8,128)(2,1)} %filter_ref.1), custom_call_target="tpu_custom_call" | custom-call | flops 67108864 | bytes 8388608 | tf_op jit(solution)/shard_map/make_table/pallas_call | solution.py:57
  30.1 1.1 %all-to-all-done = bf16[128,2,4,128]{3,2,1,0:T(4,128)(2,1)S(1)} async-done(((bf16[128,2,4,128]{3,2,1,0:T(4,128)(2,1)}), bf16[128,2,4,128]{3,2,1,0:T(4,128)(2,1)S(1)}, u32[]{:S(2)}, u32[]{:S(2)}) %all-to-all-start) | async-done | bytes 262176 | tf_op jit(solution)/shard_map/all_to_all | solution.py:247
  31.2 0.7 copy-done.3
  31.9 0.9 %copy-done.4 = bf16[128,2,4,128]{3,2,1,0:T(4,128)(2,1)S(1)} copy-done((bf16[128,2,4,128]{3,2,1,0:T(4,128)(2,1)S(1)}, bf16[128,2,4,128]{3,2,1,0:T(4,128)(2,1)}, u32[]{:S(2)}) %copy-start.4) | copy-done | bytes 262168
  32.9 0.7 copy-done.6
  33.6 5.9 %long_conv.1 = bf16[512,128]{1,0:T(8,128)(2,1)S(1)} custom-call(s32[1]{0:T(128)} %bitcast.1.rank_ref, bf16[128,8,128]{2,1,0:T(8,128)(2,1)S(1)} %bitcast.10, bf16[256,8192]{1,0:T(8,128)(2,1)} %make_table.1.far_ref, f32[3,3,512]{2,1,0:T(4,128)S(1)} %copy-done.6, f32[512]{0:T(512)S(1)} %copy-done.8), custom_call_target="tpu_custom_call" | custom-call | flops 2147483648 | bytes 1048576 | tf_op jit(solution)/shard_map/long_conv/pallas_call | solution.py:131
  40.1 14.0 %all-to-all-start.1 = ((bf16[128,4,128]{2,1,0:T(4,128)(2,1)}), bf16[128,4,128]{2,1,0:T(4,128)(2,1)}, u32[]{:S(2)}, u32[]{:S(2)}) async-start(bf16[128,4,128]{2,1,0:T(4,128)(2,1)} %bitcast.11), calls=%async_computation.1 | async-start | bytes 262144 | tf_op jit(solution)/shard_map/all_to_all | solution.py:256
  54.2 3.4 %collective-permute-start = (bf16[16,512]{1,0:T(8,128)(2,1)S(1)}, bf16[16,512]{1,0:T(8,128)(2,1)S(1)}, u32[]{:S(2)}, u32[]{:S(2)}) collective-permute-start(bf16[16,512]{1,0:T(8,128)(2,1)S(1)} %edge.1), channel_id=1, source_target_pairs={{0,4},{4,8},{8,12},{12,16},{16,20},{20,24},{24,28},{28,32},{32,36}... | collective-permute-start | bytes 49160 | tf_op jit(solution)/shard_map/ppermute | solution.py:252
  57.6 6.5 %collective-permute-done.halo_ref = bf16[16,512]{1,0:T(8,128)(2,1)S(1)} collective-permute-done((bf16[16,512]{1,0:T(8,128)(2,1)S(1)}, bf16[16,512]{1,0:T(8,128)(2,1)S(1)}, u32[]{:S(2)}, u32[]{:S(2)}) %collective-permute-start) | collective-permute-done | bytes 16416 | tf_op jit(solution)/shard_map/ppermute | solution.py:252
  64.1 0.7 copy-done.7
  64.8 1.3 %query_conv.1.q_ref = f32[512,128]{1,0:T(8,128)} custom-call(bf16[3,512,128]{2,1,0:T(8,128)(2,1)S(1)} %copy-done.2, bf16[16,512]{1,0:T(8,128)(2,1)S(1)} %collective-permute-done.halo_ref, f32[3,3,512]{2,1,0:T(4,128)S(1)} %copy-done.7), custom_call_target="tpu_custom_call" | custom-call | flops 1048576 | bytes 524288 | tf_op jit(solution)/shard_map/query_conv/pallas_call | solution.py:200
  66.1 1.9 %collective-permute-start.1 = (f32[512,128]{1,0:T(8,128)}, f32[512,128]{1,0:T(8,128)S(1)}, u32[]{:S(2)}, u32[]{:S(2)}) collective-permute-start(f32[512,128]{1,0:T(8,128)} %query_conv.1.q_ref), channel_id=1, source_target_pairs={{0,1},{1,0},{2,3},{3,2},{4,5},{5,4},{6,7},{7,6},{8,9},{9,8},{10,11... | collective-permute-start | bytes 786440 | tf_op jit(solution)/shard_map/ppermute | solution.py:259
  68.0 2.4 %collective-permute-start.2 = (bf16[512,128]{1,0:T(8,128)(2,1)}, bf16[512,128]{1,0:T(8,128)(2,1)S(1)}, u32[]{:S(2)}, u32[]{:S(2)}) collective-permute-start(bf16[512,128]{1,0:T(8,128)(2,1)} %bitcast.6.mix_ref), channel_id=1, source_target_pairs={{0,1},{1,0},{2,3},{3,2},{4,5},{5,4},{6,7},{7,6},{8,9},{9,8},{10,11... | collective-permute-start | bytes 393224 | tf_op jit(solution)/shard_map/ppermute | solution.py:260
  71.6 1.4 %shard_map.56 = bf16[512,128]{1,0:T(8,128)(2,1)S(1)} custom-call(s32[1]{0:T(128)S(6)} %sub.12.chip_ref, f32[512,128]{1,0:T(8,128)} %query_conv.1.q_ref, f32[512,128]{1,0:T(8,128)S(1)} %collective-permute-done.1.q_other_ref, bf16[512,128]{1,0:T(8,128)(2,1)} %bitcast.6.mix_ref, bf16[512,128]{1,0:T(8,128)(2,1)S(1)} %collective-permute-done.2.mix_other_ref, ...), custom_call_target="tpu_custom_call" | custom-call | flops 134217728 | bytes 2097152 | tf_op jit(solution)/shard_map/pallas_call | solution.py:228
  73.0 4.6 %collective-permute-start.4 = (bf16[512,128]{1,0:T(8,128)(2,1)S(1)}, bf16[512,128]{1,0:T(8,128)(2,1)S(1)}, u32[]{:S(2)}, u32[]{:S(2)}) collective-permute-start(bf16[512,128]{1,0:T(8,128)(2,1)S(1)} %shard_map.56), channel_id=1, source_target_pairs={{0,2},{2,0},{1,3},{3,1},{4,6},{6,4},{5,7},{7,5},{8,10},{10,8},{9,1... | collective-permute-start | bytes 393224 | tf_op jit(solution)/shard_map/ppermute | solution.py:263
  77.7 1.4 %shard_map.55 = f32[512,128]{1,0:T(8,128)S(1)} custom-call(s32[1]{0:T(128)} %bitcast.chip_ref, f32[512,128]{1,0:T(8,128)} %query_conv.1.q_ref, f32[512,128]{1,0:T(8,128)S(1)} %collective-permute-done.1.q_other_ref, bf16[512,128]{1,0:T(8,128)(2,1)} %bitcast.6.mix_ref, bf16[512,128]{1,0:T(8,128)(2,1)S(1)} %collective-permute-done.2.mix_other_ref, ...), custom_call_target="tpu_custom_call" | custom-call | flops 134217728 | bytes 2097152 | tf_op jit(solution)/shard_map/pallas_call | solution.py:228
  79.1 3.1 %collective-permute-done.4 = bf16[512,128]{1,0:T(8,128)(2,1)S(1)} collective-permute-done((bf16[512,128]{1,0:T(8,128)(2,1)S(1)}, bf16[512,128]{1,0:T(8,128)(2,1)S(1)}, u32[]{:S(2)}, u32[]{:S(2)}) %collective-permute-start.4) | collective-permute-done | bytes 131104 | tf_op jit(solution)/shard_map/ppermute | solution.py:263
  82.2 0.7 add_convert_fusion
  (19 shorter events, 1.9 us)
Async XLA Ops:
  1.8 29.4 %all-to-all-start = ((bf16[128,2,4,128]{3,2,1,0:T(4,128)(2,1)}), bf16[128,2,4,128]{3,2,1,0:T(4,128)(2,1)S(1)}, u32[]{:S(2)}, u32[]{:S(2)}) async-start(bf16[128,2,4,128]{3,2,1,0:T(4,128)(2,1)} %bitcast.9), calls=%async_computation | async-start | bytes 524288 | tf_op jit(solution)/shard_map/all_to_all | solution.py:247
  20.1 1.6 %copy-start = (bf16[512,2048]{1,0:T(8,128)(2,1)S(1)}, bf16[512,2048]{1,0:T(8,128)(2,1)}, u32[]{:S(2)}) copy-start(bf16[512,2048]{1,0:T(8,128)(2,1)} %weight_ref.3) | copy-start | bytes 6291460
  21.7 10.3 %copy-start.8 = (f32[512]{0:T(512)S(1)}, f32[512]{0:T(512)}, u32[]{:S(2)}) copy-start(f32[512]{0:T(512)} %skip_ref.1) | copy-start | bytes 6148
  23.0 48.6 %collective-permute-start.3 = (bf16[1024,512]{1,0:T(8,128)(2,1)}, bf16[1024,512]{1,0:T(8,128)(2,1)S(1)}, u32[]{:S(2)}, u32[]{:S(2)}) collective-permute-start(bf16[1024,512]{1,0:T(8,128)(2,1)} %turn.3), channel_id=1, source_target_pairs={{0,1},{1,0},{2,3},{3,2},{4,5},{5,4},{6,7},{7,6},{8,9},{9,8},{10,11... | collective-permute-start | bytes 3145736 | tf_op jit(solution)/shard_map/ppermute | solution.py:253
  30.1 24.0 %copy-start.2 = (bf16[3,512,128]{2,1,0:T(8,128)(2,1)S(1)}, bf16[3,512,128]{2,1,0:T(8,128)(2,1)}, u32[]{:S(2)}) copy-start(bf16[3,512,128]{2,1,0:T(8,128)(2,1)} %rows_ref.3) | copy-start | bytes 1179652
  31.2 0.7 copy-start.3
  31.9 1.0 %copy-start.4 = (bf16[128,2,4,128]{3,2,1,0:T(4,128)(2,1)S(1)}, bf16[128,2,4,128]{3,2,1,0:T(4,128)(2,1)}, u32[]{:S(2)}) copy-start(bf16[128,2,4,128]{3,2,1,0:T(4,128)(2,1)} %copy-done.3) | copy-start | bytes 786436
  32.9 0.7 copy-start.6
  33.6 36.8 %copy-start.1 = (bf16[512,2048]{1,0:T(8,128)(2,1)S(1)}, bf16[512,2048]{1,0:T(8,128)(2,1)}, u32[]{:S(2)}) copy-start(bf16[512,2048]{1,0:T(8,128)(2,1)} %weight_ref.3) | copy-start | bytes 6291460
  39.5 0.7 copy-start.5
  40.1 27.8 %all-to-all-start.1 = ((bf16[128,4,128]{2,1,0:T(4,128)(2,1)}), bf16[128,4,128]{2,1,0:T(4,128)(2,1)}, u32[]{:S(2)}, u32[]{:S(2)}) async-start(bf16[128,4,128]{2,1,0:T(4,128)(2,1)} %bitcast.11), calls=%async_computation.1 | async-start | bytes 262144 | tf_op jit(solution)/shard_map/all_to_all | solution.py:256
  54.2 9.9 %collective-permute-start = (bf16[16,512]{1,0:T(8,128)(2,1)S(1)}, bf16[16,512]{1,0:T(8,128)(2,1)S(1)}, u32[]{:S(2)}, u32[]{:S(2)}) collective-permute-start(bf16[16,512]{1,0:T(8,128)(2,1)S(1)} %edge.1), channel_id=1, source_target_pairs={{0,4},{4,8},{8,12},{12,16},{16,20},{20,24},{24,28},{28,32},{32,36}... | collective-permute-start | bytes 49160 | tf_op jit(solution)/shard_map/ppermute | solution.py:252
  64.0 0.7 copy-start.7
  66.1 4.9 %collective-permute-start.1 = (f32[512,128]{1,0:T(8,128)}, f32[512,128]{1,0:T(8,128)S(1)}, u32[]{:S(2)}, u32[]{:S(2)}) collective-permute-start(f32[512,128]{1,0:T(8,128)} %query_conv.1.q_ref), channel_id=1, source_target_pairs={{0,1},{1,0},{2,3},{3,2},{4,5},{5,4},{6,7},{7,6},{8,9},{9,8},{10,11... | collective-permute-start | bytes 786440 | tf_op jit(solution)/shard_map/ppermute | solution.py:259
  68.0 3.6 %collective-permute-start.2 = (bf16[512,128]{1,0:T(8,128)(2,1)}, bf16[512,128]{1,0:T(8,128)(2,1)S(1)}, u32[]{:S(2)}, u32[]{:S(2)}) collective-permute-start(bf16[512,128]{1,0:T(8,128)(2,1)} %bitcast.6.mix_ref), channel_id=1, source_target_pairs={{0,1},{1,0},{2,3},{3,2},{4,5},{5,4},{6,7},{7,6},{8,9},{9,8},{10,11... | collective-permute-start | bytes 393224 | tf_op jit(solution)/shard_map/ppermute | solution.py:260
  73.0 9.2 %collective-permute-start.4 = (bf16[512,128]{1,0:T(8,128)(2,1)S(1)}, bf16[512,128]{1,0:T(8,128)(2,1)S(1)}, u32[]{:S(2)}, u32[]{:S(2)}) collective-permute-start(bf16[512,128]{1,0:T(8,128)(2,1)S(1)} %shard_map.56), channel_id=1, source_target_pairs={{0,2},{2,0},{1,3},{3,1},{4,6},{6,4},{5,7},{7,5},{8,10},{10,8},{9,1... | collective-permute-start | bytes 393224 | tf_op jit(solution)/shard_map/ppermute | solution.py:263

commit v4 on v3

v4 whole, which is shorter than its diff:
```python
import jax
import jax.numpy as jnp
from jax import lax
from jax.experimental import pallas as pl
from jax.experimental.pallas import tpu as pltpu
from jax.sharding import PartitionSpec as P


GROUP = 16
LANES = 128
CHUNK = 1024
LEAD = 48
CORE_PAIRS = [(0, 1), (1, 0), (2, 3), (3, 2)]
CHIP_PAIRS = [(0, 2), (2, 0), (1, 3), (3, 1)]

f32 = jnp.float32
bf16 = jnp.bfloat16


def params(mib):
    return pltpu.CompilerParams(vmem_limit_bytes=mib << 20)


def in_hbm(array):
    return pltpu.with_memory_space_constraint(array, pltpu.HBM)


def load_line(filter_ref, own, line_ref):
    line_ref[:, :LANES] = jnp.zeros((8, LANES), f32)
    for at in range(0, filter_ref.shape[1], CHUNK):
        piece = filter_ref[:, at : at + CHUNK].astype(f32)
        sub = lax.broadcasted_iota(jnp.int32, piece.shape, 0)
        chosen = jnp.sum(jnp.where(sub == own, piece, 0.0), axis=0, keepdims=True)
        line_ref[:, LANES + at : LANES + at + CHUNK] = jnp.broadcast_to(chosen, piece.shape)


def fill_table(line_ref, table_ref, at):
    piece = line_ref[:, at : at + CHUNK + LANES]
    piece = jnp.concatenate([pltpu.roll(piece, first, 1, stride=1, stride_axis=0) for first in (0, 8)], axis=0).astype(bf16)
    for tile in range(LANES // 16):
        moved = pltpu.roll(piece, 16 * tile, 1)[:, LANES:] if tile else piece[:, LANES:]
        for block in range(CHUNK // LANES):
            to_row = (block % 2) * LANES + 16 * tile
            to_col = (at // LANES + block) // 2 * LANES
            table_ref[to_row : to_row + 16, to_col : to_col + LANES] = moved[:, block * LANES : (block + 1) * LANES]


def pattern(values):
    row = lax.broadcasted_iota(jnp.int32, (8, LANES), 0) % len(values)
    tile = jnp.full((8, LANES), values[-1], f32)
    for index in range(len(values) - 1):
        tile = jnp.where(row == index, values[index], tile)
    return tile


def conv_kernel(rank_ref, value_ref, filter_ref, taps_ref, skip_ref, out_ref, pair_ref, sum_ref, line_ref, table_ref):
    load_line(filter_ref, (rank_ref[0] * 4 // GROUP) % 8, line_ref)
    blocks = value_ref.shape[0]
    rows = blocks * 4
    first = rank_ref[0] * 4
    value = value_ref[...].astype(f32)
    lane = lax.broadcasted_iota(jnp.int32, value.shape, 2)
    sub = lax.broadcasted_iota(jnp.int32, (blocks // 2, 8, LANES), 1)

    def delayed(array):
        return jnp.concatenate([jnp.zeros((1, 8, LANES), f32), array[:-1]], axis=0)

    def tile_of(offset):
        return pattern([taps_ref[offset, feature, first + c] for feature in (1, 2) for c in range(4)])[None]

    conv = tile_of(0) * value
    for offset in (1, 2):
        turned = pltpu.roll(value, offset, 2)
        conv = conv + tile_of(offset) * jnp.where(lane < offset, delayed(turned), turned)
    kv = (conv * pltpu.roll(conv, 4, 1)).astype(bf16).astype(f32)
    kv = kv.reshape(blocks // 2, 2, 8, LANES)
    even, odd = kv[:, 0], kv[:, 1]
    pair_ref[:LEAD, :] = jnp.zeros((LEAD, 2 * LANES), bf16)
    pair_ref[LEAD:, :LANES] = jnp.where(sub < 4, even, odd).reshape(rows, LANES).astype(bf16)
    pair_ref[LEAD:, LANES:] = jnp.where(sub < 4, delayed(odd), even).reshape(rows, LANES).astype(bf16)

    direct = pattern([skip_ref[first + c] for c in range(4)])[None]
    sum_ref[...] = (pair_ref[LEAD:, :LANES].astype(f32).reshape(rows // 8, 8, LANES) * direct).reshape(rows, LANES)
    for index in range(rows // 64):
        begin, base = 64 * index, CHUNK * index
        for at in (2 * base, 2 * base + CHUNK):
            fill_table(line_ref, table_ref, at)
        left = [pair_ref[LEAD - 16 * s : LEAD - 16 * s + rows - begin, :] for s in range(4)]
        right = [table_ref[:, base + 256 * s : base + 256 * (s + 1)] for s in range(4)]
        moved = jnp.dot(
            jnp.concatenate(left, axis=1), jnp.concatenate(right, axis=0), preferred_element_type=f32
        )
        sum_ref[begin:, :] += moved[:, :LANES]
        sum_ref[begin + 8 :, :] += moved[: rows - begin - 8, LANES:]
    out_ref[...] = sum_ref[...].astype(bf16)


def long_conv(rank, value, filters, short_taps, skip_gain):
    blocks = value.shape[0]
    rows = blocks * 4
    seq_len = filters.shape[1]
    in_smem = pl.BlockSpec(memory_space=pltpu.SMEM)
    return pl.pallas_call(
        conv_kernel,
        out_shape=jax.ShapeDtypeStruct((rows, LANES), bf16),
        grid_spec=pltpu.PrefetchScalarGridSpec(
            num_scalar_prefetch=1,
            grid=(1,),
            in_specs=[
                pl.BlockSpec(value.shape, lambda i, r: (0, 0, 0)),
                pl.BlockSpec((8, seq_len), lambda i, r: (r[0] * 4 // GROUP // 8, 0)),
                in_smem,
                in_smem,
            ],
            out_specs=pl.BlockSpec((rows, LANES), lambda i, r: (0, 0)),
            scratch_shapes=[
                pltpu.VMEM((LEAD + rows, 2 * LANES), bf16),
                pltpu.VMEM((rows, LANES), f32),
                pltpu.VMEM((8, LANES + seq_len), f32),
                pltpu.VMEM((2 * LANES, seq_len // 2), bf16),
            ],
        ),
        compiler_params=params(16),
        cost_estimate=pl.CostEstimate(flops=1 << 31, bytes_accessed=1 << 20, transcendentals=0),
        name="long_conv",
    )(rank, value, filters, short_taps, skip_gain)


def turn_kernel(weight_ref, out_ref):
    out_ref[...] = jnp.transpose(weight_ref[...])


def turn(weight):
    width, total = weight.shape
    return pl.pallas_call(
        turn_kernel,
        out_shape=jax.ShapeDtypeStruct((total, width), bf16),
        grid=(total // width,),
        in_specs=[pl.BlockSpec((width, width), lambda i: (0, i))],
        out_specs=pl.BlockSpec((width, width), lambda i: (i, 0)),
        compiler_params=params(16),
        cost_estimate=pl.CostEstimate(flops=1 << 20, bytes_accessed=1 << 22, transcendentals=0),
        name="turn",
    )(weight)


def edge_kernel(rows_ref, out_ref):
    out_ref[...] = jnp.transpose(rows_ref[0])[LANES - 16 :, :]


def edge(features):
    channels, tokens = features.shape[1:]
    return pl.pallas_call(
        edge_kernel,
        out_shape=jax.ShapeDtypeStruct((16, channels), bf16),
        grid=(1,),
        in_specs=[pl.BlockSpec((1, channels, tokens), lambda i: (0, 0, 0))],
        out_specs=pl.BlockSpec((16, channels), lambda i: (0, 0)),
        compiler_params=params(16),
        cost_estimate=pl.CostEstimate(flops=1 << 16, bytes_accessed=1 << 17, transcendentals=0),
        name="edge",
    )(features)


def query_kernel(rows_ref, halo_ref, taps_ref, out_ref):
    value = rows_ref[0].astype(f32)
    lane = lax.broadcasted_iota(jnp.int32, value.shape, 1)
    halo = jnp.transpose(halo_ref[...].astype(f32))
    taps = taps_ref[:, 0, :]
    taps = jnp.transpose(jnp.concatenate([taps, jnp.zeros((5, taps.shape[1]), f32)], axis=0))
    once = jnp.where(lane == 0, halo[:, 15:16], pltpu.roll(value, 1, 1))
    twice = jnp.where(lane == 0, halo[:, 14:15], jnp.where(lane == 1, halo[:, 15:16], pltpu.roll(value, 2, 1)))
    out_ref[...] = taps[:, 0:1] * value + taps[:, 1:2] * once + taps[:, 2:3] * twice


def query_conv(features, halo, short_taps):
    channels, tokens = features.shape[1:]
    return pl.pallas_call(
        query_kernel,
        out_shape=jax.ShapeDtypeStruct((channels, tokens), f32),
        grid=(1,),
        in_specs=[
            pl.BlockSpec((1, channels, tokens), lambda i: (0, 0, 0)),
            pl.BlockSpec(halo.shape, lambda i: (0, 0)),
            pl.BlockSpec(short_taps.shape, lambda i: (0, 0, 0)),
        ],
        out_specs=pl.BlockSpec((channels, tokens), lambda i: (0, 0)),
        compiler_params=params(16),
        cost_estimate=pl.CostEstimate(flops=1 << 20, bytes_accessed=1 << 19, transcendentals=0),
        name="query_conv",
    )(features, halo, short_taps)


def gated_of(q_ref, mix_ref):
    return (q_ref[...] * mix_ref[...].astype(f32)).astype(bf16)


def give_kernel(member_ref, q_ref, mix_ref, weight_ref, out_ref):
    gated = gated_of(q_ref, mix_ref)
    width = mix_ref.shape[0]
    for chip in range(2):
        at = (2 * chip + 1 - member_ref[0] % 2) * width
        out_ref[chip * width : (chip + 1) * width, :] = jnp.dot(
            weight_ref[pl.ds(pl.multiple_of(at, width), width), :], gated, preferred_element_type=f32
        ).astype(bf16)


def keep_kernel(member_ref, q_ref, mix_ref, weight_ref, given_ref, out_ref):
    gated = gated_of(q_ref, mix_ref)
    width = mix_ref.shape[0]
    at = pl.multiple_of(member_ref[0] * width, width)
    chip = pl.multiple_of(member_ref[0] // 2 * width, width)
    own = jnp.dot(weight_ref[pl.ds(at, width), :], gated, preferred_element_type=f32)
    out_ref[...] = (own + given_ref[pl.ds(chip, width), :].astype(f32)).astype(out_ref.dtype)


def project(kernel, member, operands, rows, kind):
    in_vmem = pl.BlockSpec(memory_space=pltpu.VMEM)
    return pl.pallas_call(
        kernel,
        out_shape=jax.ShapeDtypeStruct((rows, operands[1].shape[1]), kind),
        in_specs=[pl.BlockSpec(memory_space=pltpu.SMEM)] + [in_vmem] * len(operands),
        out_specs=in_vmem,
        compiler_params=params(16),
        cost_estimate=pl.CostEstimate(flops=1 << 27, bytes_accessed=1 << 21, transcendentals=0),
    )(member, *operands)


def local(features, short_taps, filters, skip_gain, out_weight):
    chan_tp, tok_local = features.shape[1:]
    ctx_count = lax.axis_size("ctx")
    chan_dev = chan_tp // ctx_count
    rank = jnp.full((1,), lax.axis_index("ctx"), jnp.int32)
    member = jnp.full((1,), lax.axis_index("tp"), jnp.int32)

    sent = features[1:].reshape(2, ctx_count, chan_dev, tok_local).transpose(1, 0, 2, 3)
    got = lax.all_to_all(sent, "ctx", 0, 0, tiled=True)
    got = got.reshape(ctx_count, 2 * chan_dev, tok_local)
    last = edge(in_hbm(features))
    halo = lax.ppermute(last, "ctx", [(i, i + 1) for i in range(ctx_count - 1)])
    mix = long_conv(rank, got, *map(in_hbm, (filters, short_taps, skip_gain))).reshape(ctx_count, chan_dev, tok_local)
    mix = lax.all_to_all(mix, "ctx", 0, 0, tiled=True).reshape(chan_tp, tok_local)
    q = query_conv(features, halo, short_taps)
    weight = turn(in_hbm(out_weight))
    given = project(give_kernel, member, (q, mix, weight), 2 * chan_tp, bf16)
    given = lax.ppermute(given, "tp", CORE_PAIRS)
    operands = (q, mix, weight, given)
    away = project(keep_kernel, lax.bitwise_xor(member, 2), operands, chan_tp, bf16)
    arrived = lax.ppermute(away, "tp", CHIP_PAIRS)
    home = project(keep_kernel, member, operands, chan_tp, f32)
    return (home + arrived.astype(f32)).astype(bf16)


def solution(mesh):
    placed = (P(None, "tp", "ctx"), P(None, None, "tp"), P("tp", None), P("tp"), P("tp", None))
    return jax.shard_map(
        local, mesh=mesh, in_specs=placed, out_specs=P("tp", "ctx"), check_vma=False
    )
```

time: 83.6 us -> 73.2 us (0.88)
  the two profiles are of different devices: /device:TPU:32 before, /device:TPU:1 now
where the time goes in v4:
time: 73.2 us; the launch traced here: 72.8 us
  starting transfers between devices  38.4 us (52%)
  waiting for transfers between devices  21.6 us (30%)
  Pallas kernels  10.3 us (14%)
  local copies, waits for them, and re-layouts  1.77 us (2%)
    all_to_all x1, starting transfers between devices, local(): got = lax.all_to_all(sent, 'ctx', 0, 0, tiled=True)  19.3 us
    all_to_all x1, waiting for transfers between devices, local(): got = lax.all_to_all(sent, 'ctx', 0, 0, tiled=True)  12.8 us
    all_to_all x1, starting transfers between devices, local(): lax.all_to_all(mix, 'ctx', 0, 0, tiled=True).reshape(chan_tp, tok_local)  6.97 us
    ppermute x1, starting transfers between devices, local(): given = lax.ppermute(given, 'tp', CORE_PAIRS)  5.28 us
    pallas_call x1, Pallas kernels, long_conv(): pl.pallas_call(conv_kernel, out_shape=jax.ShapeDtypeStruct((rows, LANES),...  4.89 us
    ppermute x1, starting transfers between devices, local(): arrived = lax.ppermute(away, 'tp', CHIP_PAIRS)  4.36 us
    all_to_all x1, waiting for transfers between devices, local(): lax.all_to_all(mix, 'ctx', 0, 0, tiled=True).reshape(chan_tp, tok_local)  4.29 us
    ppermute x1, waiting for transfers between devices, local(): arrived = lax.ppermute(away, 'tp', CHIP_PAIRS)  3.41 us
  transfers between devices with their start and end apart: 5, of which 4 were waited for; matrix products, arithmetic and copies ran while one was open for 0% of the time, Pallas kernels for 6%

profile of v4, /device:TPU:1, one launch (start us, length us, event | category | flops | bytes accessed | tf_op | source)
XLA Modules:
  0.0 72.8 jit_solution(2330916014539033208)
XLA Ops:
  0.0 1.0 %slice.3 = bf16[2,512,128]{2,1,0:T(8,128)(2,1)S(1)} slice(bf16[3,512,128]{2,1,0:T(8,128)(2,1)} %rows_ref.3), slice={[1:3], [0:512], [0:128]} | slice | bytes 524288 | tf_op jit(solution)/shard_map/slice | solution.py:236
  1.0 0.8 %copy.8 = bf16[2,128,4,128]{3,2,0,1:T(4,128)(2,1)} copy(bf16[2,128,4,128]{3,2,1,0:T(4,128)(2,1)S(1)} %bitcast.13) | data formatting | bytes 524288 | tf_op jit(solution)/shard_map/reshape | solution.py:236
  1.8 19.3 %all-to-all-start = ((bf16[128,2,4,128]{3,2,1,0:T(4,128)(2,1)}), bf16[128,2,4,128]{3,2,1,0:T(4,128)(2,1)S(1)}, u32[]{:S(2)}, u32[]{:S(2)}) async-start(bf16[128,2,4,128]{3,2,1,0:T(4,128)(2,1)} %bitcast.8), calls=%async_computation | async-start | bytes 524288 | tf_op jit(solution)/shard_map/all_to_all | solution.py:237
  21.0 12.8 %all-to-all-done = bf16[128,2,4,128]{3,2,1,0:T(4,128)(2,1)S(1)} async-done(((bf16[128,2,4,128]{3,2,1,0:T(4,128)(2,1)}), bf16[128,2,4,128]{3,2,1,0:T(4,128)(2,1)S(1)}, u32[]{:S(2)}, u32[]{:S(2)}) %all-to-all-start) | async-done | bytes 262176 | tf_op jit(solution)/shard_map/all_to_all | solution.py:237
  33.8 4.9 %long_conv.1 = bf16[512,128]{1,0:T(8,128)(2,1)} custom-call(s32[1]{0:T(128)} %bitcast.1.rank_ref, bf16[128,8,128]{2,1,0:T(8,128)(2,1)S(1)} %bitcast.12, bf16[32,16384]{1,0:T(8,128)(2,1)} %filter_ref.1, f32[3,3,512]{2,1,0:T(4,128)} %taps_ref.3, f32[512]{0:T(512)} %skip_ref.1), custom_call_target="tpu_custom_call" | custom-call | flops 2147483648 | bytes 1048576 | tf_op jit(solution)/shard_map/long_conv/pallas_call | solution.py:103
  38.7 7.0 %all-to-all-start.1 = ((bf16[128,4,128]{2,1,0:T(4,128)(2,1)}), bf16[128,4,128]{2,1,0:T(4,128)(2,1)S(1)}, u32[]{:S(2)}, u32[]{:S(2)}) async-start(bf16[128,4,128]{2,1,0:T(4,128)(2,1)} %bitcast.5), calls=%async_computation.1 | async-start | bytes 262144 | tf_op jit(solution)/shard_map/all_to_all | solution.py:242
  45.7 1.0 %edge.1 = bf16[16,512]{1,0:T(8,128)(2,1)S(1)} custom-call(bf16[3,512,128]{2,1,0:T(8,128)(2,1)} %rows_ref.3), custom_call_target="tpu_custom_call" | custom-call | flops 65536 | bytes 131072 | tf_op jit(solution)/shard_map/edge/pallas_call | solution.py:153
  46.7 2.5 %collective-permute-start = (bf16[16,512]{1,0:T(8,128)(2,1)S(1)}, bf16[16,512]{1,0:T(8,128)(2,1)S(1)}, u32[]{:S(2)}, u32[]{:S(2)}) collective-permute-start(bf16[16,512]{1,0:T(8,128)(2,1)S(1)} %edge.1), channel_id=1, source_target_pairs={{0,4},{4,8},{8,12},{12,16},{16,20},{20,24},{24,28},{28,32},{32,36}... | collective-permute-start | bytes 49160 | tf_op jit(solution)/shard_map/ppermute | solution.py:240
  49.2 0.0 copy-start
  49.2 0.0 copy-start.1
  49.2 2.8 %turn.1.weight_ref = bf16[2048,512]{1,0:T(8,128)(2,1)S(1)} custom-call(bf16[512,2048]{1,0:T(8,128)(2,1)} %weight_ref.1), custom_call_target="tpu_custom_call" | custom-call | flops 1048576 | bytes 4194304 | tf_op jit(solution)/shard_map/turn/pallas_call | solution.py:135
  52.0 0.0 collective-permute-done.halo_ref
  52.0 0.0 copy-done
  52.0 0.0 copy-done.1
  52.0 0.6 query_conv.1.q_ref
  52.6 4.3 %all-to-all-done.1 = bf16[128,4,128]{2,1,0:T(4,128)(2,1)S(1)} async-done(((bf16[128,4,128]{2,1,0:T(4,128)(2,1)}), bf16[128,4,128]{2,1,0:T(4,128)(2,1)S(1)}, u32[]{:S(2)}, u32[]{:S(2)}) %all-to-all-start.1) | async-done | bytes 131104 | tf_op jit(solution)/shard_map/all_to_all | solution.py:242
  56.9 0.4 shard_map.55
  57.3 5.3 %collective-permute-start.1 = (bf16[1024,128]{1,0:T(8,128)(2,1)S(1)}, bf16[1024,128]{1,0:T(8,128)(2,1)S(1)}, u32[]{:S(2)}, u32[]{:S(2)}) collective-permute-start(bf16[1024,128]{1,0:T(8,128)(2,1)S(1)} %shard_map.55), channel_id=1, source_target_pairs={{0,1},{1,0},{2,3},{3,2},{4,5},{5,4},{6,7},{7,6},{8,9},{9,8},{10,11... | collective-permute-start | bytes 786440 | tf_op jit(solution)/shard_map/ppermute | solution.py:246
  62.6 1.1 %collective-permute-done.1.given_ref = bf16[1024,128]{1,0:T(8,128)(2,1)S(1)} collective-permute-done((bf16[1024,128]{1,0:T(8,128)(2,1)S(1)}, bf16[1024,128]{1,0:T(8,128)(2,1)S(1)}, u32[]{:S(2)}, u32[]{:S(2)}) %collective-permute-start.1) | collective-permute-done | bytes 262176 | tf_op jit(solution)/shard_map/ppermute | solution.py:246
  63.8 0.3 shard_map.57
  64.1 4.4 %collective-permute-start.2 = (bf16[512,128]{1,0:T(8,128)(2,1)S(1)}, bf16[512,128]{1,0:T(8,128)(2,1)S(1)}, u32[]{:S(2)}, u32[]{:S(2)}) collective-permute-start(bf16[512,128]{1,0:T(8,128)(2,1)S(1)} %shard_map.57), channel_id=1, source_target_pairs={{0,2},{2,0},{1,3},{3,1},{4,6},{6,4},{5,7},{7,5},{8,10},{10,8},{9,1... | collective-permute-start | bytes 393224 | tf_op jit(solution)/shard_map/ppermute | solution.py:249
  68.4 0.3 shard_map.56
  68.7 3.4 %collective-permute-done.2 = bf16[512,128]{1,0:T(8,128)(2,1)S(1)} collective-permute-done((bf16[512,128]{1,0:T(8,128)(2,1)S(1)}, bf16[512,128]{1,0:T(8,128)(2,1)S(1)}, u32[]{:S(2)}, u32[]{:S(2)}) %collective-permute-start.2) | collective-permute-done | bytes 131104 | tf_op jit(solution)/shard_map/ppermute | solution.py:249
  72.1 0.7 add_convert_fusion
Async XLA Ops:
  1.8 32.1 %all-to-all-start = ((bf16[128,2,4,128]{3,2,1,0:T(4,128)(2,1)}), bf16[128,2,4,128]{3,2,1,0:T(4,128)(2,1)S(1)}, u32[]{:S(2)}, u32[]{:S(2)}) async-start(bf16[128,2,4,128]{3,2,1,0:T(4,128)(2,1)} %bitcast.8), calls=%async_computation | async-start | bytes 524288 | tf_op jit(solution)/shard_map/all_to_all | solution.py:237
  38.7 18.2 %all-to-all-start.1 = ((bf16[128,4,128]{2,1,0:T(4,128)(2,1)}), bf16[128,4,128]{2,1,0:T(4,128)(2,1)S(1)}, u32[]{:S(2)}, u32[]{:S(2)}) async-start(bf16[128,4,128]{2,1,0:T(4,128)(2,1)} %bitcast.5), calls=%async_computation.1 | async-start | bytes 262144 | tf_op jit(solution)/shard_map/all_to_all | solution.py:242
  46.7 5.3 %collective-permute-start = (bf16[16,512]{1,0:T(8,128)(2,1)S(1)}, bf16[16,512]{1,0:T(8,128)(2,1)S(1)}, u32[]{:S(2)}, u32[]{:S(2)}) collective-permute-start(bf16[16,512]{1,0:T(8,128)(2,1)S(1)} %edge.1), channel_id=1, source_target_pairs={{0,4},{4,8},{8,12},{12,16},{16,20},{20,24},{24,28},{28,32},{32,36}... | collective-permute-start | bytes 49160 | tf_op jit(solution)/shard_map/ppermute | solution.py:240
  49.2 2.8 %copy-start = (bf16[3,512,128]{2,1,0:T(8,128)(2,1)S(1)}, bf16[3,512,128]{2,1,0:T(8,128)(2,1)}, u32[]{:S(2)}) copy-start(bf16[3,512,128]{2,1,0:T(8,128)(2,1)} %rows_ref.3) | copy-start | bytes 1179652
  49.2 2.8 %copy-start.1 = (f32[3,3,512]{2,1,0:T(4,128)S(1)}, f32[3,3,512]{2,1,0:T(4,128)}, u32[]{:S(2)}) copy-start(f32[3,3,512]{2,1,0:T(4,128)} %taps_ref.3) | copy-start | bytes 55300
  57.3 6.4 %collective-permute-start.1 = (bf16[1024,128]{1,0:T(8,128)(2,1)S(1)}, bf16[1024,128]{1,0:T(8,128)(2,1)S(1)}, u32[]{:S(2)}, u32[]{:S(2)}) collective-permute-start(bf16[1024,128]{1,0:T(8,128)(2,1)S(1)} %shard_map.55), channel_id=1, source_target_pairs={{0,1},{1,0},{2,3},{3,2},{4,5},{5,4},{6,7},{7,6},{8,9},{9,8},{10,11... | collective-permute-start | bytes 786440 | tf_op jit(solution)/shard_map/ppermute | solution.py:246
  64.1 8.1 %collective-permute-start.2 = (bf16[512,128]{1,0:T(8,128)(2,1)S(1)}, bf16[512,128]{1,0:T(8,128)(2,1)S(1)}, u32[]{:S(2)}, u32[]{:S(2)}) collective-permute-start(bf16[512,128]{1,0:T(8,128)(2,1)S(1)} %shard_map.57), channel_id=1, source_target_pairs={{0,2},{2,0},{1,3},{3,1},{4,6},{6,4},{5,7},{7,5},{8,10},{10,8},{9,1... | collective-permute-start | bytes 393224 | tf_op jit(solution)/shard_map/ppermute | solution.py:249

commit v5 on v4

--- a/solution.py
+++ b/solution.py
@@ -25,18 +25,8 @@
     return pltpu.with_memory_space_constraint(array, pltpu.HBM)
 
 
-def load_line(filter_ref, own, line_ref):
-    line_ref[:, :LANES] = jnp.zeros((8, LANES), f32)
-    for at in range(0, filter_ref.shape[1], CHUNK):
-        piece = filter_ref[:, at : at + CHUNK].astype(f32)
-        sub = lax.broadcasted_iota(jnp.int32, piece.shape, 0)
-        chosen = jnp.sum(jnp.where(sub == own, piece, 0.0), axis=0, keepdims=True)
-        line_ref[:, LANES + at : LANES + at + CHUNK] = jnp.broadcast_to(chosen, piece.shape)
-
-
 def fill_table(line_ref, table_ref, at):
     piece = line_ref[:, at : at + CHUNK + LANES]
-    piece = jnp.concatenate([pltpu.roll(piece, first, 1, stride=1, stride_axis=0) for first in (0, 8)], axis=0).astype(bf16)
     for tile in range(LANES // 16):
         moved = pltpu.roll(piece, 16 * tile, 1)[:, LANES:] if tile else piece[:, LANES:]
         for block in range(CHUNK // LANES):
@@ -53,11 +43,80 @@
     return tile
 
 
-def conv_kernel(rank_ref, value_ref, filter_ref, taps_ref, skip_ref, out_ref, pair_ref, sum_ref, line_ref, table_ref):
-    load_line(filter_ref, (rank_ref[0] * 4 // GROUP) % 8, line_ref)
+def prepare_kernel(rank_ref, filter_ref, taps_ref, skip_ref, line_ref, tiles_ref, wide_ref):
+    own = (rank_ref[0] * 4 // GROUP) % 8
+    first = rank_ref[0] * 4
+    wide_ref[:, : 2 * LANES] = jnp.zeros((8, 2 * LANES), f32)
+    line_ref[:, :LANES] = jnp.zeros((16, LANES), bf16)
+    for at in range(0, filter_ref.shape[1], CHUNK):
+        piece = filter_ref[:, at : at + CHUNK].astype(f32)
+        sub = lax.broadcasted_iota(jnp.int32, piece.shape, 0)
+        chosen = jnp.sum(jnp.where(sub == own, piece, 0.0), axis=0, keepdims=True)
+        wide_ref[:, 2 * LANES + at : 2 * LANES + at + CHUNK] = jnp.broadcast_to(chosen, piece.shape)
+    for at in range(0, filter_ref.shape[1], CHUNK):
+        piece = wide_ref[:, LANES + at : 2 * LANES + at + CHUNK]
+        both = [pltpu.roll(piece, begin, 1, stride=1, stride_axis=0)[:, LANES:] for begin in (0, 8)]
+        line_ref[:, LANES + at : LANES + at + CHUNK] = jnp.concatenate(both, axis=0).astype(bf16)
+    for offset in range(3):
+        tiles_ref[offset] = pattern([taps_ref[offset, feature, first + c] for feature in (1, 2) for c in range(4)])
+    tiles_ref[3] = pattern([skip_ref[first + c] for c in range(4)])
+
+
+def prepare(rank, filters, short_taps, skip_gain):
+    seq_len = filters.shape[1]
+    in_smem = pl.BlockSpec(memory_space=pltpu.SMEM)
+    return pl.pallas_call(
+        prepare_kernel,
+        out_shape=[
+            jax.ShapeDtypeStruct((16, LANES + seq_len), bf16),
+            jax.ShapeDtypeStruct((4, 8, LANES), f32),
+        ],
+        grid_spec=pltpu.PrefetchScalarGridSpec(
+            num_scalar_prefetch=1,
+            grid=(1,),
+            in_specs=[pl.BlockSpec((8, seq_len), lambda i, r: (r[0] * 4 // GROUP // 8, 0)), in_smem, in_smem],
+            out_specs=[
+                pl.BlockSpec((16, LANES + seq_len), lambda i, r: (0, 0)),
+                pl.BlockSpec((4, 8, LANES), lambda i, r: (0, 0, 0)),
+            ],
+            scratch_shapes=[pltpu.VMEM((8, 2 * LANES + seq_len), f32)],
+        ),
+        compiler_params=params(16),
+        cost_estimate=pl.CostEstimate(flops=1 << 22, bytes_accessed=1 << 20, transcendentals=0),
+        name="prepare",
+    )(rank, filters, short_taps, skip_gain)
+
+
+def pack_kernel(k_ref, v_ref, out_ref):
+    rows = k_ref.shape[1]
+    k = k_ref[0].astype(f32).reshape(rows // 8, 8, LANES)
+    v = v_ref[0].astype(f32).reshape(rows // 8, 8, LANES)
+    upper = lax.broadcasted_iota(jnp.int32, k.shape, 1) < 4
+    even = jnp.where(upper, k, pltpu.roll(v, 4, 1))
+    odd = jnp.where(upper, pltpu.roll(k, 4, 1), v)
+    out_ref[...] = jnp.stack([even, odd], axis=1).reshape(rows // 4, 8, LANES).astype(bf16)
+
+
+def pack(features):
+    rows = features.shape[1]
+    return pl.pallas_call(
+        pack_kernel,
+        out_shape=jax.ShapeDtypeStruct((rows // 4, 8, LANES), bf16),
+        grid=(1,),
+        in_specs=[
+            pl.BlockSpec((1, rows, LANES), lambda i: (1, 0, 0)),
+            pl.BlockSpec((1, rows, LANES), lambda i: (2, 0, 0)),
+        ],
+        out_specs=pl.BlockSpec((rows // 4, 8, LANES), lambda i: (0, 0, 0)),
+        compiler_params=params(16),
+        cost_estimate=pl.CostEstimate(flops=1 << 18, bytes_accessed=1 << 19, transcendentals=0),
+        name="pack",
+    )(features, features)
+
+
+def conv_kernel(value_ref, line_ref, tiles_ref, out_ref, pair_ref, sum_ref, table_ref):
     blocks = value_ref.shape[0]
     rows = blocks * 4
-    first = rank_ref[0] * 4
     value = value_ref[...].astype(f32)
     lane = lax.broadcasted_iota(jnp.int32, value.shape, 2)
     sub = lax.broadcasted_iota(jnp.int32, (blocks // 2, 8, LANES), 1)
@@ -65,13 +124,10 @@
     def delayed(array):
         return jnp.concatenate([jnp.zeros((1, 8, LANES), f32), array[:-1]], axis=0)
 
-    def tile_of(offset):
-        return pattern([taps_ref[offset, feature, first + c] for feature in (1, 2) for c in range(4)])[None]
-
-    conv = tile_of(0) * value
+    conv = tiles_ref[0][None] * value
     for offset in (1, 2):
         turned = pltpu.roll(value, offset, 2)
-        conv = conv + tile_of(offset) * jnp.where(lane < offset, delayed(turned), turned)
+        conv = conv + tiles_ref[offset][None] * jnp.where(lane < offset, delayed(turned), turned)
     kv = (conv * pltpu.roll(conv, 4, 1)).astype(bf16).astype(f32)
     kv = kv.reshape(blocks // 2, 2, 8, LANES)
     even, odd = kv[:, 0], kv[:, 1]
@@ -79,7 +135,7 @@
     pair_ref[LEAD:, :LANES] = jnp.where(sub < 4, even, odd).reshape(rows, LANES).astype(bf16)
     pair_ref[LEAD:, LANES:] = jnp.where(sub < 4, delayed(odd), even).reshape(rows, LANES).astype(bf16)
 
-    direct = pattern([skip_ref[first + c] for c in range(4)])[None]
+    direct = tiles_ref[3][None]
     sum_ref[...] = (pair_ref[LEAD:, :LANES].astype(f32).reshape(rows // 8, 8, LANES) * direct).reshape(rows, LANES)
     for index in range(rows // 64):
         begin, base = 64 * index, CHUNK * index
@@ -95,35 +151,24 @@
     out_ref[...] = sum_ref[...].astype(bf16)
 
 
-def long_conv(rank, value, filters, short_taps, skip_gain):
-    blocks = value.shape[0]
-    rows = blocks * 4
-    seq_len = filters.shape[1]
-    in_smem = pl.BlockSpec(memory_space=pltpu.SMEM)
+def long_conv(value, line, tiles):
+    rows = value.shape[0] * 4
+    seq_len = line.shape[1] - LANES
+    in_vmem = pl.BlockSpec(memory_space=pltpu.VMEM)
     return pl.pallas_call(
         conv_kernel,
         out_shape=jax.ShapeDtypeStruct((rows, LANES), bf16),
-        grid_spec=pltpu.PrefetchScalarGridSpec(
-            num_scalar_prefetch=1,
-            grid=(1,),
-            in_specs=[
-                pl.BlockSpec(value.shape, lambda i, r: (0, 0, 0)),
-                pl.BlockSpec((8, seq_len), lambda i, r: (r[0] * 4 // GROUP // 8, 0)),
-                in_smem,
-                in_smem,
-            ],
-            out_specs=pl.BlockSpec((rows, LANES), lambda i, r: (0, 0)),
-            scratch_shapes=[
-                pltpu.VMEM((LEAD + rows, 2 * LANES), bf16),
-                pltpu.VMEM((rows, LANES), f32),
-                pltpu.VMEM((8, LANES + seq_len), f32),
-                pltpu.VMEM((2 * LANES, seq_len // 2), bf16),
-            ],
-        ),
+        in_specs=[in_vmem] * 3,
+        out_specs=in_vmem,
+        scratch_shapes=[
+            pltpu.VMEM((LEAD + rows, 2 * LANES), bf16),
+            pltpu.VMEM((rows, LANES), f32),
+            pltpu.VMEM((2 * LANES, seq_len // 2), bf16),
+        ],
         compiler_params=params(16),
         cost_estimate=pl.CostEstimate(flops=1 << 31, bytes_accessed=1 << 20, transcendentals=0),
         name="long_conv",
-    )(rank, value, filters, short_taps, skip_gain)
+    )(value, line, tiles)
 
 
 def turn_kernel(weight_ref, out_ref):
@@ -233,12 +278,12 @@
     rank = jnp.full((1,), lax.axis_index("ctx"), jnp.int32)
     member = jnp.full((1,), lax.axis_index("tp"), jnp.int32)
 
-    sent = features[1:].reshape(2, ctx_count, chan_dev, tok_local).transpose(1, 0, 2, 3)
+    sent = pack(in_hbm(features))
     got = lax.all_to_all(sent, "ctx", 0, 0, tiled=True)
-    got = got.reshape(ctx_count, 2 * chan_dev, tok_local)
+    line, tiles = prepare(rank, *map(in_hbm, (filters, short_taps, skip_gain)))
     last = edge(in_hbm(features))
     halo = lax.ppermute(last, "ctx", [(i, i + 1) for i in range(ctx_count - 1)])
-    mix = long_conv(rank, got, *map(in_hbm, (filters, short_taps, skip_gain))).reshape(ctx_count, chan_dev, tok_local)
+    mix = long_conv(got, line, tiles).reshape(ctx_count, chan_dev, tok_local)
     mix = lax.all_to_all(mix, "ctx", 0, 0, tiled=True).reshape(chan_tp, tok_local)
     q = query_conv(features, halo, short_taps)
     weight = turn(in_hbm(out_weight))

time: 73.2 us -> 70.8 us (0.967)
  local copies, waits for them, and re-layouts: 1.77 us -> 0.01 us
  waiting for transfers between devices: 21.6 us -> 20.2 us
    pallas_call x0 -> x2, Pallas kernels: none -> 3.11 us  [the longest x1 1.73 us: pack(): pl.pallas_call(pack_kernel, out_shape=jax.ShapeDtypeStruct((rows // 4, 8,...]
    pallas_call x1, Pallas kernels: 4.89 us -> 2.48 us  [long_conv(): pl.pallas_call(conv_kernel, out_shape=jax.ShapeDtypeStruct((rows, LANES),...]
    all_to_all x1, waiting for transfers between devices: 12.8 us -> 11.4 us  [local(): got = lax.all_to_all(sent, 'ctx', 0, 0, tiled=True)]
    slice x1 -> x0, local copies, waits for them, and re-layouts: 0.97 us -> none  [local(): features[1:].reshape(2, ctx_count, chan_dev, tok_local)]
    reshape x1 -> x0, local copies, waits for them, and re-layouts: 0.79 us -> none  [local(): features[1:].reshape(2, ctx_count, chan_dev, tok_local)]
  transfers between devices with their start and end apart: 5 -> 5, of which waited for: 4 -> 4; matrix products, arithmetic and copies ran while one was open for 0% -> 0% of each run, Pallas kernels for 6% -> 9%
where the time goes in v5:
time: 70.8 us; the launch traced here: 70.4 us
  starting transfers between devices  38.4 us (54%)
  waiting for transfers between devices  20.2 us (29%)
  Pallas kernels  11 us (16%)
    all_to_all x1, starting transfers between devices, local(): got = lax.all_to_all(sent, 'ctx', 0, 0, tiled=True)  19.3 us
    all_to_all x1, waiting for transfers between devices, local(): got = lax.all_to_all(sent, 'ctx', 0, 0, tiled=True)  11.4 us
    all_to_all x1, starting transfers between devices, local(): lax.all_to_all(mix, 'ctx', 0, 0, tiled=True).reshape(chan_tp, tok_local)  6.97 us
    ppermute x1, starting transfers between devices, local(): given = lax.ppermute(given, 'tp', CORE_PAIRS)  5.29 us
    ppermute x1, starting transfers between devices, local(): arrived = lax.ppermute(away, 'tp', CHIP_PAIRS)  4.36 us
    all_to_all x1, waiting for transfers between devices, local(): lax.all_to_all(mix, 'ctx', 0, 0, tiled=True).reshape(chan_tp, tok_local)  4.29 us
    ppermute x1, waiting for transfers between devices, local(): arrived = lax.ppermute(away, 'tp', CHIP_PAIRS)  3.4 us
    pallas_call x1, Pallas kernels, turn(): pl.pallas_call(turn_kernel, out_shape=jax.ShapeDtypeStruct((total, width)...  2.77 us
  transfers between devices with their start and end apart: 5, of which 4 were waited for; matrix products, arithmetic and copies ran while one was open for 0% of the time, Pallas kernels for 9%

profile of v5, /device:TPU:1, one launch (start us, length us, event | category | flops | bytes accessed | tf_op | source)
XLA Modules:
  0.0 70.4 jit_solution(7540709523245066169)
XLA Ops:
  0.0 1.7 %pack.1 = bf16[128,8,128]{2,1,0:T(8,128)(2,1)} custom-call(bf16[3,512,128]{2,1,0:T(8,128)(2,1)} %v_ref.1, bf16[3,512,128]{2,1,0:T(8,128)(2,1)} %v_ref.1), custom_call_target="tpu_custom_call" | custom-call | flops 262144 | bytes 524288 | tf_op jit(solution)/shard_map/pack/pallas_call | solution.py:102
  1.7 19.3 %all-to-all-start = ((bf16[128,8,128]{2,1,0:T(8,128)(2,1)}), bf16[128,8,128]{2,1,0:T(8,128)(2,1)S(1)}, u32[]{:S(2)}, u32[]{:S(2)}) async-start(bf16[128,8,128]{2,1,0:T(8,128)(2,1)} %pack.1), calls=%async_computation | async-start | bytes 524288 | tf_op jit(solution)/shard_map/all_to_all | solution.py:282
  21.0 1.4 %prepare.1 = (bf16[16,16512]{1,0:T(8,128)(2,1)S(1)}, f32[4,8,128]{2,1,0:T(8,128)S(1)}) custom-call(s32[1]{0:T(128)} %bitcast.1.rank_ref, bf16[32,16384]{1,0:T(8,128)(2,1)} %filter_ref.1, f32[3,3,512]{2,1,0:T(4,128)} %taps_ref.3, f32[512]{0:T(512)} %skip_ref.1), custom_call_target="tpu_custom_call" | custom-call | flops 4194304 | bytes 1048576 | tf_op jit(solution)/shard_map/prepare/pallas_call | solution.py:68
  22.4 11.4 %all-to-all-done.value_ref = bf16[128,8,128]{2,1,0:T(8,128)(2,1)S(1)} async-done(((bf16[128,8,128]{2,1,0:T(8,128)(2,1)}), bf16[128,8,128]{2,1,0:T(8,128)(2,1)S(1)}, u32[]{:S(2)}, u32[]{:S(2)}) %all-to-all-start) | async-done | bytes 262176 | tf_op jit(solution)/shard_map/all_to_all | solution.py:282
  33.8 2.5 %long_conv.1 = bf16[512,128]{1,0:T(8,128)(2,1)} custom-call(bf16[128,8,128]{2,1,0:T(8,128)(2,1)S(1)} %all-to-all-done.value_ref, bf16[16,16512]{1,0:T(8,128)(2,1)S(1)} %get-tuple-element.7.line_ref, f32[4,8,128]{2,1,0:T(8,128)S(1)} %get-tuple-element.8.tiles_ref), custom_call_target="tpu_custom_call" | custom-call | flops 2147483648 | bytes 1048576 | tf_op jit(solution)/shard_map/long_conv/pallas_call | solution.py:158
  36.3 7.0 %all-to-all-start.1 = ((bf16[128,4,128]{2,1,0:T(4,128)(2,1)}), bf16[128,4,128]{2,1,0:T(4,128)(2,1)S(1)}, u32[]{:S(2)}, u32[]{:S(2)}) async-start(bf16[128,4,128]{2,1,0:T(4,128)(2,1)} %bitcast.2), calls=%async_computation.1 | async-start | bytes 262144 | tf_op jit(solution)/shard_map/all_to_all | solution.py:287
  43.2 1.0 %edge.1 = bf16[16,512]{1,0:T(8,128)(2,1)S(1)} custom-call(bf16[3,512,128]{2,1,0:T(8,128)(2,1)} %v_ref.1), custom_call_target="tpu_custom_call" | custom-call | flops 65536 | bytes 131072 | tf_op jit(solution)/shard_map/edge/pallas_call | solution.py:198
  44.2 2.5 %collective-permute-start = (bf16[16,512]{1,0:T(8,128)(2,1)S(1)}, bf16[16,512]{1,0:T(8,128)(2,1)S(1)}, u32[]{:S(2)}, u32[]{:S(2)}) collective-permute-start(bf16[16,512]{1,0:T(8,128)(2,1)S(1)} %edge.1), channel_id=1, source_target_pairs={{0,4},{4,8},{8,12},{12,16},{16,20},{20,24},{24,28},{28,32},{32,36}... | collective-permute-start | bytes 49160 | tf_op jit(solution)/shard_map/ppermute | solution.py:285
  46.7 0.0 copy-start
  46.7 0.0 copy-start.1
  46.8 2.8 %turn.1.weight_ref = bf16[2048,512]{1,0:T(8,128)(2,1)S(1)} custom-call(bf16[512,2048]{1,0:T(8,128)(2,1)} %weight_ref.1), custom_call_target="tpu_custom_call" | custom-call | flops 1048576 | bytes 4194304 | tf_op jit(solution)/shard_map/turn/pallas_call | solution.py:180
  49.5 0.0 collective-permute-done.halo_ref
  49.5 0.0 copy-done
  49.6 0.0 copy-done.1
  49.6 0.6 query_conv.1.q_ref
  50.2 4.3 %all-to-all-done.1 = bf16[128,4,128]{2,1,0:T(4,128)(2,1)S(1)} async-done(((bf16[128,4,128]{2,1,0:T(4,128)(2,1)}), bf16[128,4,128]{2,1,0:T(4,128)(2,1)S(1)}, u32[]{:S(2)}, u32[]{:S(2)}) %all-to-all-start.1) | async-done | bytes 131104 | tf_op jit(solution)/shard_map/all_to_all | solution.py:287
  54.4 0.4 shard_map.55
  54.9 5.3 %collective-permute-start.1 = (bf16[1024,128]{1,0:T(8,128)(2,1)S(1)}, bf16[1024,128]{1,0:T(8,128)(2,1)S(1)}, u32[]{:S(2)}, u32[]{:S(2)}) collective-permute-start(bf16[1024,128]{1,0:T(8,128)(2,1)S(1)} %shard_map.55), channel_id=1, source_target_pairs={{0,1},{1,0},{2,3},{3,2},{4,5},{5,4},{6,7},{7,6},{8,9},{9,8},{10,11... | collective-permute-start | bytes 786440 | tf_op jit(solution)/shard_map/ppermute | solution.py:291
  60.2 1.1 %collective-permute-done.1.given_ref = bf16[1024,128]{1,0:T(8,128)(2,1)S(1)} collective-permute-done((bf16[1024,128]{1,0:T(8,128)(2,1)S(1)}, bf16[1024,128]{1,0:T(8,128)(2,1)S(1)}, u32[]{:S(2)}, u32[]{:S(2)}) %collective-permute-start.1) | collective-permute-done | bytes 262176 | tf_op jit(solution)/shard_map/ppermute | solution.py:291
  61.3 0.3 shard_map.57
  61.6 4.4 %collective-permute-start.2 = (bf16[512,128]{1,0:T(8,128)(2,1)S(1)}, bf16[512,128]{1,0:T(8,128)(2,1)S(1)}, u32[]{:S(2)}, u32[]{:S(2)}) collective-permute-start(bf16[512,128]{1,0:T(8,128)(2,1)S(1)} %shard_map.57), channel_id=1, source_target_pairs={{0,2},{2,0},{1,3},{3,1},{4,6},{6,4},{5,7},{7,5},{8,10},{10,8},{9,1... | collective-permute-start | bytes 393224 | tf_op jit(solution)/shard_map/ppermute | solution.py:294
  66.0 0.3 shard_map.56
  66.3 3.4 %collective-permute-done.2 = bf16[512,128]{1,0:T(8,128)(2,1)S(1)} collective-permute-done((bf16[512,128]{1,0:T(8,128)(2,1)S(1)}, bf16[512,128]{1,0:T(8,128)(2,1)S(1)}, u32[]{:S(2)}, u32[]{:S(2)}) %collective-permute-start.2) | collective-permute-done | bytes 131104 | tf_op jit(solution)/shard_map/ppermute | solution.py:294
  69.7 0.7 add_convert_fusion
Async XLA Ops:
  1.7 32.1 %all-to-all-start = ((bf16[128,8,128]{2,1,0:T(8,128)(2,1)}), bf16[128,8,128]{2,1,0:T(8,128)(2,1)S(1)}, u32[]{:S(2)}, u32[]{:S(2)}) async-start(bf16[128,8,128]{2,1,0:T(8,128)(2,1)} %pack.1), calls=%async_computation | async-start | bytes 524288 | tf_op jit(solution)/shard_map/all_to_all | solution.py:282
  36.3 18.2 %all-to-all-start.1 = ((bf16[128,4,128]{2,1,0:T(4,128)(2,1)}), bf16[128,4,128]{2,1,0:T(4,128)(2,1)S(1)}, u32[]{:S(2)}, u32[]{:S(2)}) async-start(bf16[128,4,128]{2,1,0:T(4,128)(2,1)} %bitcast.2), calls=%async_computation.1 | async-start | bytes 262144 | tf_op jit(solution)/shard_map/all_to_all | solution.py:287
  44.2 5.3 %collective-permute-start = (bf16[16,512]{1,0:T(8,128)(2,1)S(1)}, bf16[16,512]{1,0:T(8,128)(2,1)S(1)}, u32[]{:S(2)}, u32[]{:S(2)}) collective-permute-start(bf16[16,512]{1,0:T(8,128)(2,1)S(1)} %edge.1), channel_id=1, source_target_pairs={{0,4},{4,8},{8,12},{12,16},{16,20},{20,24},{24,28},{28,32},{32,36}... | collective-permute-start | bytes 49160 | tf_op jit(solution)/shard_map/ppermute | solution.py:285
  46.7 2.8 %copy-start = (bf16[3,512,128]{2,1,0:T(8,128)(2,1)S(1)}, bf16[3,512,128]{2,1,0:T(8,128)(2,1)}, u32[]{:S(2)}) copy-start(bf16[3,512,128]{2,1,0:T(8,128)(2,1)} %v_ref.1) | copy-start | bytes 1179652
  46.7 2.8 %copy-start.1 = (f32[3,3,512]{2,1,0:T(4,128)S(1)}, f32[3,3,512]{2,1,0:T(4,128)}, u32[]{:S(2)}) copy-start(f32[3,3,512]{2,1,0:T(4,128)} %taps_ref.3) | copy-start | bytes 55300
  54.9 6.4 %collective-permute-start.1 = (bf16[1024,128]{1,0:T(8,128)(2,1)S(1)}, bf16[1024,128]{1,0:T(8,128)(2,1)S(1)}, u32[]{:S(2)}, u32[]{:S(2)}) collective-permute-start(bf16[1024,128]{1,0:T(8,128)(2,1)S(1)} %shard_map.55), channel_id=1, source_target_pairs={{0,1},{1,0},{2,3},{3,2},{4,5},{5,4},{6,7},{7,6},{8,9},{9,8},{10,11... | collective-permute-start | bytes 786440 | tf_op jit(solution)/shard_map/ppermute | solution.py:291
  61.6 8.1 %collective-permute-start.2 = (bf16[512,128]{1,0:T(8,128)(2,1)S(1)}, bf16[512,128]{1,0:T(8,128)(2,1)S(1)}, u32[]{:S(2)}, u32[]{:S(2)}) collective-permute-start(bf16[512,128]{1,0:T(8,128)(2,1)S(1)} %shard_map.57), channel_id=1, source_target_pairs={{0,2},{2,0},{1,3},{3,1},{4,6},{6,4},{5,7},{7,5},{8,10},{10,8},{9,1... | collective-permute-start | bytes 393224 | tf_op jit(solution)/shard_map/ppermute | solution.py:294

commit v6 on v5

--- a/solution.py
+++ b/solution.py
@@ -10,6 +10,7 @@
 LANES = 128
 CHUNK = 1024
 LEAD = 48
+PACK_STEPS = 4
 CORE_PAIRS = [(0, 1), (1, 0), (2, 3), (3, 2)]
 CHIP_PAIRS = [(0, 2), (2, 0), (1, 3), (3, 1)]
 
@@ -43,75 +44,105 @@
     return tile
 
 
-def prepare_kernel(rank_ref, filter_ref, taps_ref, skip_ref, line_ref, tiles_ref, wide_ref):
-    own = (rank_ref[0] * 4 // GROUP) % 8
+def prepare_kernel(rank_ref, filters_ref, weight_ref, taps_ref, skip_ref, line_ref, tiles_ref, turned_ref, filter_ref, near_ref, wide_ref, sems):
+    width = near_ref.shape[0]
+    group = rank_ref[0] * 4 // GROUP
     first = rank_ref[0] * 4
+    fetch = pltpu.make_async_copy(filters_ref.at[pl.ds(pl.multiple_of(group // 8 * 8, 8), 8)], filter_ref, sems.at[0])
+    fetch.start()
+    pieces = []
+    for at in range(0, near_ref.shape[1], width):
+        here = slice(at, at + width)
+        pieces.append(pltpu.make_async_copy(weight_ref.at[:, here], near_ref.at[:, here], sems.at[1 + at // width]))
+        pieces[-1].start()
+    for offset in range(3):
+        tiles_ref[offset] = pattern([taps_ref[offset, feature, first + c] for feature in (1, 2) for c in range(4)])
+    tiles_ref[3] = pattern([skip_ref[first + c] for c in range(4)])
     wide_ref[:, : 2 * LANES] = jnp.zeros((8, 2 * LANES), f32)
     line_ref[:, :LANES] = jnp.zeros((16, LANES), bf16)
+    fetch.wait()
     for at in range(0, filter_ref.shape[1], CHUNK):
         piece = filter_ref[:, at : at + CHUNK].astype(f32)
         sub = lax.broadcasted_iota(jnp.int32, piece.shape, 0)
-        chosen = jnp.sum(jnp.where(sub == own, piece, 0.0), axis=0, keepdims=True)
+        chosen = jnp.sum(jnp.where(sub == group % 8, piece, 0.0), axis=0, keepdims=True)
         wide_ref[:, 2 * LANES + at : 2 * LANES + at + CHUNK] = jnp.broadcast_to(chosen, piece.shape)
     for at in range(0, filter_ref.shape[1], CHUNK):
         piece = wide_ref[:, LANES + at : 2 * LANES + at + CHUNK]
         both = [pltpu.roll(piece, begin, 1, stride=1, stride_axis=0)[:, LANES:] for begin in (0, 8)]
         line_ref[:, LANES + at : LANES + at + CHUNK] = jnp.concatenate(both, axis=0).astype(bf16)
-    for offset in range(3):
-        tiles_ref[offset] = pattern([taps_ref[offset, feature, first + c] for feature in (1, 2) for c in range(4)])
-    tiles_ref[3] = pattern([skip_ref[first + c] for c in range(4)])
-
-
-def prepare(rank, filters, short_taps, skip_gain):
+    for index, piece in enumerate(pieces):
+        piece.wait()
+        here = slice(index * width, (index + 1) * width)
+        turned_ref[here, :] = jnp.transpose(near_ref[:, here])
+
+
+def prepare(rank, filters, weight, short_taps, skip_gain):
     seq_len = filters.shape[1]
     in_smem = pl.BlockSpec(memory_space=pltpu.SMEM)
+    in_place = pl.BlockSpec(memory_space=pltpu.HBM)
+    in_vmem = pl.BlockSpec(memory_space=pltpu.VMEM)
     return pl.pallas_call(
         prepare_kernel,
         out_shape=[
             jax.ShapeDtypeStruct((16, LANES + seq_len), bf16),
             jax.ShapeDtypeStruct((4, 8, LANES), f32),
-        ],
-        grid_spec=pltpu.PrefetchScalarGridSpec(
-            num_scalar_prefetch=1,
-            grid=(1,),
-            in_specs=[pl.BlockSpec((8, seq_len), lambda i, r: (r[0] * 4 // GROUP // 8, 0)), in_smem, in_smem],
-            out_specs=[
-                pl.BlockSpec((16, LANES + seq_len), lambda i, r: (0, 0)),
-                pl.BlockSpec((4, 8, LANES), lambda i, r: (0, 0, 0)),
-            ],
-            scratch_shapes=[pltpu.VMEM((8, 2 * LANES + seq_len), f32)],
-        ),
-        compiler_params=params(16),
-        cost_estimate=pl.CostEstimate(flops=1 << 22, bytes_accessed=1 << 20, transcendentals=0),
+            jax.ShapeDtypeStruct(weight.shape[::-1], bf16),
+        ],
+        in_specs=[in_smem, in_place, in_place, in_smem, in_smem],
+        out_specs=[in_vmem] * 3,
+        scratch_shapes=[
+            pltpu.VMEM((8, seq_len), bf16),
+            pltpu.VMEM(weight.shape, bf16),
+            pltpu.VMEM((8, 2 * LANES + seq_len), f32),
+            pltpu.SemaphoreType.DMA((1 + weight.shape[1] // weight.shape[0],)),
+        ],
+        compiler_params=params(16),
+        cost_estimate=pl.CostEstimate(flops=1 << 22, bytes_accessed=1 << 22, transcendentals=0),
         name="prepare",
-    )(rank, filters, short_taps, skip_gain)
-
-
-def pack_kernel(k_ref, v_ref, out_ref):
-    rows = k_ref.shape[1]
-    k = k_ref[0].astype(f32).reshape(rows // 8, 8, LANES)
-    v = v_ref[0].astype(f32).reshape(rows // 8, 8, LANES)
-    upper = lax.broadcasted_iota(jnp.int32, k.shape, 1) < 4
-    even = jnp.where(upper, k, pltpu.roll(v, 4, 1))
-    odd = jnp.where(upper, pltpu.roll(k, 4, 1), v)
-    out_ref[...] = jnp.stack([even, odd], axis=1).reshape(rows // 4, 8, LANES).astype(bf16)
+    )(rank, filters, weight, short_taps, skip_gain)
+
+
+def pack_kernel(features_ref, out_ref, rows_ref, packed_ref, in_sems, out_sems):
+    rows = features_ref.shape[1] // PACK_STEPS
+    fetches, stores = [], []
+    for step in range(PACK_STEPS):
+        here = slice(step * rows, (step + 1) * rows)
+        fetches.append(pltpu.make_async_copy(features_ref.at[1:, here], rows_ref.at[:, here], in_sems.at[step]))
+        fetches[-1].start()
+    for step in range(PACK_STEPS):
+        fetches[step].wait()
+        k, v = (
+            rows_ref[index, step * rows : (step + 1) * rows].astype(f32).reshape(rows // 8, 8, LANES) for index in range(2)
+        )
+        upper = lax.broadcasted_iota(jnp.int32, k.shape, 1) < 4
+        even = jnp.where(upper, k, pltpu.roll(v, 4, 1))
+        odd = jnp.where(upper, pltpu.roll(k, 4, 1), v)
+        there = slice(step * rows // 4, (step + 1) * rows // 4)
+        packed_ref[there] = jnp.stack([even, odd], axis=1).reshape(rows // 4, 8, LANES).astype(bf16)
+        stores.append(pltpu.make_async_copy(packed_ref.at[there], out_ref.at[there], out_sems.at[step]))
+        stores[-1].start()
+    for store in stores:
+        store.wait()
 
 
 def pack(features):
     rows = features.shape[1]
+    in_place = pl.BlockSpec(memory_space=pltpu.HBM)
     return pl.pallas_call(
         pack_kernel,
         out_shape=jax.ShapeDtypeStruct((rows // 4, 8, LANES), bf16),
-        grid=(1,),
-        in_specs=[
-            pl.BlockSpec((1, rows, LANES), lambda i: (1, 0, 0)),
-            pl.BlockSpec((1, rows, LANES), lambda i: (2, 0, 0)),
-        ],
-        out_specs=pl.BlockSpec((rows // 4, 8, LANES), lambda i: (0, 0, 0)),
+        in_specs=[in_place],
+        out_specs=in_place,
+        scratch_shapes=[
+            pltpu.VMEM((2, rows, LANES), bf16),
+            pltpu.VMEM((rows // 4, 8, LANES), bf16),
+            pltpu.SemaphoreType.DMA((PACK_STEPS,)),
+            pltpu.SemaphoreType.DMA((PACK_STEPS,)),
+        ],
         compiler_params=params(16),
         cost_estimate=pl.CostEstimate(flops=1 << 18, bytes_accessed=1 << 19, transcendentals=0),
         name="pack",
-    )(features, features)
+    )(features)
 
 
 def conv_kernel(value_ref, line_ref, tiles_ref, out_ref, pair_ref, sum_ref, table_ref):
@@ -171,24 +202,6 @@
     )(value, line, tiles)
 
 
-def turn_kernel(weight_ref, out_ref):
-    out_ref[...] = jnp.transpose(weight_ref[...])
-
-
-def turn(weight):
-    width, total = weight.shape
-    return pl.pallas_call(
-        turn_kernel,
-        out_shape=jax.ShapeDtypeStruct((total, width), bf16),
-        grid=(total // width,),
-        in_specs=[pl.BlockSpec((width, width), lambda i: (0, i))],
-        out_specs=pl.BlockSpec((width, width), lambda i: (i, 0)),
-        compiler_params=params(16),
-        cost_estimate=pl.CostEstimate(flops=1 << 20, bytes_accessed=1 << 22, transcendentals=0),
-        name="turn",
-    )(weight)
-
-
 def edge_kernel(rows_ref, out_ref):
     out_ref[...] = jnp.transpose(rows_ref[0])[LANES - 16 :, :]
 
@@ -280,13 +293,14 @@
 
     sent = pack(in_hbm(features))
     got = lax.all_to_all(sent, "ctx", 0, 0, tiled=True)
-    line, tiles = prepare(rank, *map(in_hbm, (filters, short_taps, skip_gain)))
     last = edge(in_hbm(features))
     halo = lax.ppermute(last, "ctx", [(i, i + 1) for i in range(ctx_count - 1)])
+    line, tiles, weight = prepare(rank, *map(in_hbm, (filters, out_weight, short_taps, skip_gain)))
+    q = query_conv(in_hbm(features), halo, short_taps)
+
     mix = long_conv(got, line, tiles).reshape(ctx_count, chan_dev, tok_local)
+    mix, member = lax.optimization_barrier((mix, member))
     mix = lax.all_to_all(mix, "ctx", 0, 0, tiled=True).reshape(chan_tp, tok_local)
-    q = query_conv(features, halo, short_taps)
-    weight = turn(in_hbm(out_weight))
     given = project(give_kernel, member, (q, mix, weight), 2 * chan_tp, bf16)
     given = lax.ppermute(given, "tp", CORE_PAIRS)
     operands = (q, mix, weight, given)

time: 70.8 us -> 70.8 us (level)
    pallas_call x1 -> x0, Pallas kernels: 2.77 us -> none  [turn(): pl.pallas_call(turn_kernel, out_shape=jax.ShapeDtypeStruct((total, width)...]
    all_to_all x1, waiting for transfers between devices: 11.4 us -> 9.62 us  [local(): got = lax.all_to_all(sent, 'ctx', 0, 0, tiled=True)]
    pallas_call x1, Pallas kernels: 1.39 us -> 3.15 us  [prepare(): pl.pallas_call(prepare_kernel, out_shape=[jax.ShapeDtypeStruct((16, LANES...]
    all_to_all x1, waiting for transfers between devices: 4.29 us -> 5.37 us  [local(): lax.all_to_all(mix, 'ctx', 0, 0, tiled=True).reshape(chan_tp, tok_local)]
    pallas_call x1, Pallas kernels: 0.59 us -> 1.49 us  [query_conv(): pl.pallas_call(query_kernel, out_shape=jax.ShapeDtypeStruct((channels, to...]
    ppermute x1, waiting for transfers between devices: 0.01 us -> 0.85 us  [local(): halo = lax.ppermute(last, 'ctx', [(i, i + 1) for i in range(ctx_count - 1)])]
  transfers between devices with their start and end apart: 5 -> 5, of which waited for: 4 -> 5; matrix products, arithmetic and copies ran while one was open for 0% -> 0% of each run, Pallas kernels for 9% -> 8%
where the time goes in v6:
time: 70.8 us; the launch traced here: 70.3 us
  starting transfers between devices  38.4 us (54%)
  waiting for transfers between devices  20.4 us (29%)
  Pallas kernels  10.8 us (15%)
    all_to_all x1, starting transfers between devices, local(): got = lax.all_to_all(sent, 'ctx', 0, 0, tiled=True)  19.3 us
    all_to_all x1, waiting for transfers between devices, local(): got = lax.all_to_all(sent, 'ctx', 0, 0, tiled=True)  9.62 us
    all_to_all x1, starting transfers between devices, local(): lax.all_to_all(mix, 'ctx', 0, 0, tiled=True).reshape(chan_tp, tok_local)  6.97 us
    all_to_all x1, waiting for transfers between devices, local(): lax.all_to_all(mix, 'ctx', 0, 0, tiled=True).reshape(chan_tp, tok_local)  5.37 us
    ppermute x1, starting transfers between devices, local(): given = lax.ppermute(given, 'tp', CORE_PAIRS)  5.28 us
    ppermute x1, starting transfers between devices, local(): arrived = lax.ppermute(away, 'tp', CHIP_PAIRS)  4.36 us
    ppermute x1, waiting for transfers between devices, local(): arrived = lax.ppermute(away, 'tp', CHIP_PAIRS)  3.4 us
    pallas_call x1, Pallas kernels, prepare(): pl.pallas_call(prepare_kernel, out_shape=[jax.ShapeDtypeStruct((16, LANES...  3.15 us
  transfers between devices with their start and end apart: 5, of which 5 were waited for; matrix products, arithmetic and copies ran while one was open for 0% of the time, Pallas kernels for 8%

profile of v6, /device:TPU:1, one launch (start us, length us, event | category | flops | bytes accessed | tf_op | source)
XLA Modules:
  0.0 70.3 jit_solution(6944240770448476820)
XLA Ops:
  0.0 1.6 %pack.1 = bf16[128,8,128]{2,1,0:T(8,128)(2,1)} custom-call(bf16[3,512,128]{2,1,0:T(8,128)(2,1)} %rows_ref.3), custom_call_target="tpu_custom_call" | custom-call | flops 262144 | bytes 524288 | tf_op jit(solution)/shard_map/pack/pallas_call | solution.py:131
  1.7 19.3 %all-to-all-start = ((bf16[128,8,128]{2,1,0:T(8,128)(2,1)}), bf16[128,8,128]{2,1,0:T(8,128)(2,1)S(1)}, u32[]{:S(2)}, u32[]{:S(2)}) async-start(bf16[128,8,128]{2,1,0:T(8,128)(2,1)} %pack.1), calls=%async_computation | async-start | bytes 524288 | tf_op jit(solution)/shard_map/all_to_all | solution.py:295
  21.0 3.2 %prepare.1 = (bf16[16,16512]{1,0:T(8,128)(2,1)S(1)}, f32[4,8,128]{2,1,0:T(8,128)S(1)}, bf16[2048,512]{1,0:T(8,128)(2,1)S(1)}) custom-call(s32[1]{0:T(128)} %bitcast.rank_ref, bf16[32,16384]{1,0:T(8,128)(2,1)} %filters_ref.1, bf16[512,2048]{1,0:T(8,128)(2,1)} %weight_ref.1, f32[3,3,512]{2,1,0:T(4,128)} %taps_ref.3, f32[512]{0:T(512)} %skip_ref.1), custom_call_target="tpu_custom_call" | custom-call | flops 4194304 | bytes 4194304 | tf_op jit(solution)/shard_map/prepare/pallas_call | solution.py:84
  24.1 9.6 %all-to-all-done.value_ref = bf16[128,8,128]{2,1,0:T(8,128)(2,1)S(1)} async-done(((bf16[128,8,128]{2,1,0:T(8,128)(2,1)}), bf16[128,8,128]{2,1,0:T(8,128)(2,1)S(1)}, u32[]{:S(2)}, u32[]{:S(2)}) %all-to-all-start) | async-done | bytes 262176 | tf_op jit(solution)/shard_map/all_to_all | solution.py:295
  33.7 0.0 copy-start
  33.7 2.5 %long_conv.1 = bf16[512,128]{1,0:T(8,128)(2,1)} custom-call(bf16[128,8,128]{2,1,0:T(8,128)(2,1)S(1)} %all-to-all-done.value_ref, bf16[16,16512]{1,0:T(8,128)(2,1)S(1)} %get-tuple-element.10.line_ref, f32[4,8,128]{2,1,0:T(8,128)S(1)} %get-tuple-element.11.tiles_ref), custom_call_target="tpu_custom_call" | custom-call | flops 2147483648 | bytes 1048576 | tf_op jit(solution)/shard_map/long_conv/pallas_call | solution.py:189
  36.2 7.0 %all-to-all-start.1 = ((bf16[128,4,128]{2,1,0:T(4,128)(2,1)}), bf16[128,4,128]{2,1,0:T(4,128)(2,1)S(1)}, u32[]{:S(2)}, u32[]{:S(2)}) async-start(bf16[128,4,128]{2,1,0:T(4,128)(2,1)} %bitcast.1), calls=%async_computation.1 | async-start | bytes 262144 | tf_op jit(solution)/shard_map/all_to_all | solution.py:303
  43.2 1.0 %edge.1 = bf16[16,512]{1,0:T(8,128)(2,1)S(1)} custom-call(bf16[3,512,128]{2,1,0:T(8,128)(2,1)} %rows_ref.3), custom_call_target="tpu_custom_call" | custom-call | flops 65536 | bytes 131072 | tf_op jit(solution)/shard_map/edge/pallas_call | solution.py:211
  44.2 2.5 %collective-permute-start = (bf16[16,512]{1,0:T(8,128)(2,1)S(1)}, bf16[16,512]{1,0:T(8,128)(2,1)S(1)}, u32[]{:S(2)}, u32[]{:S(2)}) collective-permute-start(bf16[16,512]{1,0:T(8,128)(2,1)S(1)} %edge.1), channel_id=1, source_target_pairs={{0,4},{4,8},{8,12},{12,16},{16,20},{20,24},{24,28},{28,32},{32,36}... | collective-permute-start | bytes 49160 | tf_op jit(solution)/shard_map/ppermute | solution.py:297
  46.7 0.9 %collective-permute-done.halo_ref = bf16[16,512]{1,0:T(8,128)(2,1)S(1)} collective-permute-done((bf16[16,512]{1,0:T(8,128)(2,1)S(1)}, bf16[16,512]{1,0:T(8,128)(2,1)S(1)}, u32[]{:S(2)}, u32[]{:S(2)}) %collective-permute-start) | collective-permute-done | bytes 16416 | tf_op jit(solution)/shard_map/ppermute | solution.py:297
  47.5 0.0 copy-done
  47.5 1.5 %query_conv.1.q_ref = f32[512,128]{1,0:T(8,128)S(1)} custom-call(bf16[3,512,128]{2,1,0:T(8,128)(2,1)} %rows_ref.3, bf16[16,512]{1,0:T(8,128)(2,1)S(1)} %collective-permute-done.halo_ref, f32[3,3,512]{2,1,0:T(4,128)S(1)} %copy-done), custom_call_target="tpu_custom_call" | custom-call | flops 1048576 | bytes 524288 | tf_op jit(solution)/shard_map/query_conv/pallas_call | solution.py:236
  49.0 5.4 %all-to-all-done.1 = bf16[128,4,128]{2,1,0:T(4,128)(2,1)S(1)} async-done(((bf16[128,4,128]{2,1,0:T(4,128)(2,1)}), bf16[128,4,128]{2,1,0:T(4,128)(2,1)S(1)}, u32[]{:S(2)}, u32[]{:S(2)}) %all-to-all-start.1) | async-done | bytes 131104 | tf_op jit(solution)/shard_map/all_to_all | solution.py:303
  54.4 0.4 shard_map.55
  54.8 5.3 %collective-permute-start.1 = (bf16[1024,128]{1,0:T(8,128)(2,1)S(1)}, bf16[1024,128]{1,0:T(8,128)(2,1)S(1)}, u32[]{:S(2)}, u32[]{:S(2)}) collective-permute-start(bf16[1024,128]{1,0:T(8,128)(2,1)S(1)} %shard_map.55), channel_id=1, source_target_pairs={{0,1},{1,0},{2,3},{3,2},{4,5},{5,4},{6,7},{7,6},{8,9},{9,8},{10,11... | collective-permute-start | bytes 786440 | tf_op jit(solution)/shard_map/ppermute | solution.py:305
  60.1 1.1 %collective-permute-done.1.given_ref = bf16[1024,128]{1,0:T(8,128)(2,1)S(1)} collective-permute-done((bf16[1024,128]{1,0:T(8,128)(2,1)S(1)}, bf16[1024,128]{1,0:T(8,128)(2,1)S(1)}, u32[]{:S(2)}, u32[]{:S(2)}) %collective-permute-start.1) | collective-permute-done | bytes 262176 | tf_op jit(solution)/shard_map/ppermute | solution.py:305
  61.3 0.3 shard_map.57
  61.6 4.4 %collective-permute-start.2 = (bf16[512,128]{1,0:T(8,128)(2,1)S(1)}, bf16[512,128]{1,0:T(8,128)(2,1)S(1)}, u32[]{:S(2)}, u32[]{:S(2)}) collective-permute-start(bf16[512,128]{1,0:T(8,128)(2,1)S(1)} %shard_map.57), channel_id=1, source_target_pairs={{0,2},{2,0},{1,3},{3,1},{4,6},{6,4},{5,7},{7,5},{8,10},{10,8},{9,1... | collective-permute-start | bytes 393224 | tf_op jit(solution)/shard_map/ppermute | solution.py:308
  65.9 0.3 shard_map.56
  66.3 3.4 %collective-permute-done.2 = bf16[512,128]{1,0:T(8,128)(2,1)S(1)} collective-permute-done((bf16[512,128]{1,0:T(8,128)(2,1)S(1)}, bf16[512,128]{1,0:T(8,128)(2,1)S(1)}, u32[]{:S(2)}, u32[]{:S(2)}) %collective-permute-start.2) | collective-permute-done | bytes 131104 | tf_op jit(solution)/shard_map/ppermute | solution.py:308
  69.7 0.7 add_convert_fusion
Async XLA Ops:
  1.7 32.1 %all-to-all-start = ((bf16[128,8,128]{2,1,0:T(8,128)(2,1)}), bf16[128,8,128]{2,1,0:T(8,128)(2,1)S(1)}, u32[]{:S(2)}, u32[]{:S(2)}) async-start(bf16[128,8,128]{2,1,0:T(8,128)(2,1)} %pack.1), calls=%async_computation | async-start | bytes 524288 | tf_op jit(solution)/shard_map/all_to_all | solution.py:295
  33.7 13.8 %copy-start = (f32[3,3,512]{2,1,0:T(4,128)S(1)}, f32[3,3,512]{2,1,0:T(4,128)}, u32[]{:S(2)}) copy-start(f32[3,3,512]{2,1,0:T(4,128)} %taps_ref.3) | copy-start | bytes 55300
  36.2 18.2 %all-to-all-start.1 = ((bf16[128,4,128]{2,1,0:T(4,128)(2,1)}), bf16[128,4,128]{2,1,0:T(4,128)(2,1)S(1)}, u32[]{:S(2)}, u32[]{:S(2)}) async-start(bf16[128,4,128]{2,1,0:T(4,128)(2,1)} %bitcast.1), calls=%async_computation.1 | async-start | bytes 262144 | tf_op jit(solution)/shard_map/all_to_all | solution.py:303
  44.2 3.3 %collective-permute-start = (bf16[16,512]{1,0:T(8,128)(2,1)S(1)}, bf16[16,512]{1,0:T(8,128)(2,1)S(1)}, u32[]{:S(2)}, u32[]{:S(2)}) collective-permute-start(bf16[16,512]{1,0:T(8,128)(2,1)S(1)} %edge.1), channel_id=1, source_target_pairs={{0,4},{4,8},{8,12},{12,16},{16,20},{20,24},{24,28},{28,32},{32,36}... | collective-permute-start | bytes 49160 | tf_op jit(solution)/shard_map/ppermute | solution.py:297
  54.8 6.4 %collective-permute-start.1 = (bf16[1024,128]{1,0:T(8,128)(2,1)S(1)}, bf16[1024,128]{1,0:T(8,128)(2,1)S(1)}, u32[]{:S(2)}, u32[]{:S(2)}) collective-permute-start(bf16[1024,128]{1,0:T(8,128)(2,1)S(1)} %shard_map.55), channel_id=1, source_target_pairs={{0,1},{1,0},{2,3},{3,2},{4,5},{5,4},{6,7},{7,6},{8,9},{9,8},{10,11... | collective-permute-start | bytes 786440 | tf_op jit(solution)/shard_map/ppermute | solution.py:305
  61.6 8.1 %collective-permute-start.2 = (bf16[512,128]{1,0:T(8,128)(2,1)S(1)}, bf16[512,128]{1,0:T(8,128)(2,1)S(1)}, u32[]{:S(2)}, u32[]{:S(2)}) collective-permute-start(bf16[512,128]{1,0:T(8,128)(2,1)S(1)} %shard_map.57), channel_id=1, source_target_pairs={{0,2},{2,0},{1,3},{3,1},{4,6},{6,4},{5,7},{7,5},{8,10},{10,8},{9,1... | collective-permute-start | bytes 393224 | tf_op jit(solution)/shard_map/ppermute | solution.py:308

commit v7 on v5

--- a/solution.py
+++ b/solution.py
@@ -10,6 +10,8 @@
 LANES = 128
 CHUNK = 1024
 LEAD = 48
+PACK_STEPS = 4
+OUT_STEPS = 4
 CORE_PAIRS = [(0, 1), (1, 0), (2, 3), (3, 2)]
 CHIP_PAIRS = [(0, 2), (2, 0), (1, 3), (3, 1)]
 
@@ -87,34 +89,50 @@
     )(rank, filters, short_taps, skip_gain)
 
 
-def pack_kernel(k_ref, v_ref, out_ref):
-    rows = k_ref.shape[1]
-    k = k_ref[0].astype(f32).reshape(rows // 8, 8, LANES)
-    v = v_ref[0].astype(f32).reshape(rows // 8, 8, LANES)
-    upper = lax.broadcasted_iota(jnp.int32, k.shape, 1) < 4
-    even = jnp.where(upper, k, pltpu.roll(v, 4, 1))
-    odd = jnp.where(upper, pltpu.roll(k, 4, 1), v)
-    out_ref[...] = jnp.stack([even, odd], axis=1).reshape(rows // 4, 8, LANES).astype(bf16)
+def pack_kernel(features_ref, out_ref, rows_ref, packed_ref, in_sems, out_sems):
+    rows = features_ref.shape[1] // PACK_STEPS
+    fetches, stores = [], []
+    for step in range(PACK_STEPS):
+        here = slice(step * rows, (step + 1) * rows)
+        fetches.append(pltpu.make_async_copy(features_ref.at[1:, here], rows_ref.at[:, here], in_sems.at[step]))
+        fetches[-1].start()
+    for step in range(PACK_STEPS):
+        fetches[step].wait()
+        k, v = (
+            rows_ref[index, step * rows : (step + 1) * rows].astype(f32).reshape(rows // 8, 8, LANES) for index in range(2)
+        )
+        upper = lax.broadcasted_iota(jnp.int32, k.shape, 1) < 4
+        even = jnp.where(upper, k, pltpu.roll(v, 4, 1))
+        odd = jnp.where(upper, pltpu.roll(k, 4, 1), v)
+        there = slice(step * rows // 4, (step + 1) * rows // 4)
+        packed_ref[there] = jnp.stack([even, odd], axis=1).reshape(rows // 4, 8, LANES).astype(bf16)
+        stores.append(pltpu.make_async_copy(packed_ref.at[there], out_ref.at[there], out_sems.at[step]))
+        stores[-1].start()
+    for store in stores:
+        store.wait()
 
 
 def pack(features):
     rows = features.shape[1]
+    in_place = pl.BlockSpec(memory_space=pltpu.HBM)
     return pl.pallas_call(
         pack_kernel,
         out_shape=jax.ShapeDtypeStruct((rows // 4, 8, LANES), bf16),
-        grid=(1,),
-        in_specs=[
-            pl.BlockSpec((1, rows, LANES), lambda i: (1, 0, 0)),
-            pl.BlockSpec((1, rows, LANES), lambda i: (2, 0, 0)),
+        in_specs=[in_place],
+        out_specs=in_place,
+        scratch_shapes=[
+            pltpu.VMEM((2, rows, LANES), bf16),
+            pltpu.VMEM((rows // 4, 8, LANES), bf16),
+            pltpu.SemaphoreType.DMA((PACK_STEPS,)),
+            pltpu.SemaphoreType.DMA((PACK_STEPS,)),
         ],
-        out_specs=pl.BlockSpec((rows // 4, 8, LANES), lambda i: (0, 0, 0)),
         compiler_params=params(16),
         cost_estimate=pl.CostEstimate(flops=1 << 18, bytes_accessed=1 << 19, transcendentals=0),
         name="pack",
-    )(features, features)
-
-
-def conv_kernel(value_ref, line_ref, tiles_ref, out_ref, pair_ref, sum_ref, table_ref):
+    )(features)
+
+
+def conv_kernel(value_ref, line_ref, tiles_ref, out_ref, pair_ref, sum_ref, table_ref, mix_ref, sems):
     blocks = value_ref.shape[0]
     rows = blocks * 4
     value = value_ref[...].astype(f32)
@@ -138,17 +156,32 @@
     direct = tiles_ref[3][None]
     sum_ref[...] = (pair_ref[LEAD:, :LANES].astype(f32).reshape(rows // 8, 8, LANES) * direct).reshape(rows, LANES)
     for index in range(rows // 64):
-        begin, base = 64 * index, CHUNK * index
-        for at in (2 * base, 2 * base + CHUNK):
+        for at in (2 * CHUNK * index, 2 * CHUNK * index + CHUNK):
             fill_table(line_ref, table_ref, at)
-        left = [pair_ref[LEAD - 16 * s : LEAD - 16 * s + rows - begin, :] for s in range(4)]
-        right = [table_ref[:, base + 256 * s : base + 256 * (s + 1)] for s in range(4)]
-        moved = jnp.dot(
-            jnp.concatenate(left, axis=1), jnp.concatenate(right, axis=0), preferred_element_type=f32
-        )
-        sum_ref[begin:, :] += moved[:, :LANES]
-        sum_ref[begin + 8 :, :] += moved[: rows - begin - 8, LANES:]
-    out_ref[...] = sum_ref[...].astype(bf16)
+        if index:
+            add_shifted(pair_ref, table_ref, sum_ref, index, 0, rows - 64 * index)
+    stretch = rows // OUT_STEPS
+    leaving = []
+    for begin in range(0, rows, stretch):
+        add_shifted(pair_ref, table_ref, sum_ref, 0, begin, min(stretch, rows - begin))
+        here = slice(begin, begin + stretch)
+        mix_ref[here, :] = sum_ref[here, :].astype(bf16)
+        leaving.append(pltpu.make_async_copy(mix_ref.at[here], out_ref.at[here], sems.at[begin // stretch]))
+        leaving[-1].start()
+    for copy in leaving:
+        copy.wait()
+
+
+def add_shifted(pair_ref, table_ref, sum_ref, index, first, count):
+    base = CHUNK * index
+    left = [pair_ref[LEAD + first - 16 * s : LEAD + first - 16 * s + count, :] for s in range(4)]
+    right = [table_ref[:, base + 256 * s : base + 256 * (s + 1)] for s in range(4)]
+    moved = jnp.dot(jnp.concatenate(left, axis=1), jnp.concatenate(right, axis=0), preferred_element_type=f32)
+    begin = 64 * index + first
+    rows = sum_ref.shape[0]
+    sum_ref[begin : begin + count, :] += moved[:, :LANES]
+    count = min(count, rows - begin - 8)
+    sum_ref[begin + 8 : begin + 8 + count, :] += moved[:count, LANES:]
 
 
 def long_conv(value, line, tiles):
@@ -159,11 +192,13 @@
         conv_kernel,
         out_shape=jax.ShapeDtypeStruct((rows, LANES), bf16),
         in_specs=[in_vmem] * 3,
-        out_specs=in_vmem,
+        out_specs=pl.BlockSpec(memory_space=pltpu.HBM),
         scratch_shapes=[
             pltpu.VMEM((LEAD + rows, 2 * LANES), bf16),
             pltpu.VMEM((rows, LANES), f32),
             pltpu.VMEM((2 * LANES, seq_len // 2), bf16),
+            pltpu.VMEM((rows, LANES), bf16),
+            pltpu.SemaphoreType.DMA((OUT_STEPS,)),
         ],
         compiler_params=params(16),
         cost_estimate=pl.CostEstimate(flops=1 << 31, bytes_accessed=1 << 20, transcendentals=0),
@@ -240,23 +275,19 @@
     return (q_ref[...] * mix_ref[...].astype(f32)).astype(bf16)
 
 
+def own_part(member, q_ref, mix_ref, weight_ref):
+    width = mix_ref.shape[0]
+    at = pl.multiple_of(member * width, width)
+    return jnp.dot(weight_ref[pl.ds(at, width), :], gated_of(q_ref, mix_ref), preferred_element_type=f32)
+
+
 def give_kernel(member_ref, q_ref, mix_ref, weight_ref, out_ref):
-    gated = gated_of(q_ref, mix_ref)
-    width = mix_ref.shape[0]
-    for chip in range(2):
-        at = (2 * chip + 1 - member_ref[0] % 2) * width
-        out_ref[chip * width : (chip + 1) * width, :] = jnp.dot(
-            weight_ref[pl.ds(pl.multiple_of(at, width), width), :], gated, preferred_element_type=f32
-        ).astype(bf16)
+    out_ref[...] = own_part(member_ref[0], q_ref, mix_ref, weight_ref).astype(bf16)
 
 
 def keep_kernel(member_ref, q_ref, mix_ref, weight_ref, given_ref, out_ref):
-    gated = gated_of(q_ref, mix_ref)
-    width = mix_ref.shape[0]
-    at = pl.multiple_of(member_ref[0] * width, width)
-    chip = pl.multiple_of(member_ref[0] // 2 * width, width)
-    own = jnp.dot(weight_ref[pl.ds(at, width), :], gated, preferred_element_type=f32)
-    out_ref[...] = (own + given_ref[pl.ds(chip, width), :].astype(f32)).astype(out_ref.dtype)
+    own = own_part(member_ref[0], q_ref, mix_ref, weight_ref)
+    out_ref[...] = (own + given_ref[...].astype(f32)).astype(out_ref.dtype)
 
 
 def project(kernel, member, operands, rows, kind):
@@ -287,12 +318,15 @@
     mix = lax.all_to_all(mix, "ctx", 0, 0, tiled=True).reshape(chan_tp, tok_local)
     q = query_conv(features, halo, short_taps)
     weight = turn(in_hbm(out_weight))
-    given = project(give_kernel, member, (q, mix, weight), 2 * chan_tp, bf16)
+    operands = (q, mix, weight)
+    rows = chan_tp
+    given = project(give_kernel, lax.bitwise_xor(member, 3), operands, rows, bf16)
     given = lax.ppermute(given, "tp", CORE_PAIRS)
-    operands = (q, mix, weight, given)
-    away = project(keep_kernel, lax.bitwise_xor(member, 2), operands, chan_tp, bf16)
+    away = project(keep_kernel, lax.bitwise_xor(member, 2), (*operands, given), rows, bf16)
     arrived = lax.ppermute(away, "tp", CHIP_PAIRS)
-    home = project(keep_kernel, member, operands, chan_tp, f32)
+    given_home = project(give_kernel, lax.bitwise_xor(member, 1), operands, rows, bf16)
+    given_home = lax.ppermute(given_home, "tp", CORE_PAIRS)
+    home = project(keep_kernel, member, (*operands, given_home), rows, f32)
     return (home + arrived.astype(f32)).astype(bf16)
 
 

time: 70.8 us -> 71.7 us (1.013)
  starting transfers between devices: 38.4 us -> 40.3 us
  waiting for transfers between devices: 20.2 us -> 19 us
    ppermute x0 -> x1, starting transfers between devices: none -> 1.92 us  [local(): given_home = lax.ppermute(given_home, 'tp', CORE_PAIRS)]
    ppermute x1, waiting for transfers between devices: 1.14 us -> 0.01 us  [local(): given = lax.ppermute(given, 'tp', CORE_PAIRS)]
  transfers between devices with their start and end apart: 5 -> 6, of which waited for: 4 -> 3; matrix products, arithmetic and copies ran while one was open for 0% -> 0% of each run, Pallas kernels for 9% -> 9%
where the time goes in v7:
time: 71.7 us; the launch traced here: 71.3 us
  starting transfers between devices  40.3 us (56%)
  waiting for transfers between devices  19 us (26%)
  Pallas kernels  11.1 us (15%)
    all_to_all x1, starting transfers between devices, local(): got = lax.all_to_all(sent, 'ctx', 0, 0, tiled=True)  19.3 us
    all_to_all x1, waiting for transfers between devices, local(): got = lax.all_to_all(sent, 'ctx', 0, 0, tiled=True)  11.4 us
    all_to_all x1, starting transfers between devices, local(): lax.all_to_all(mix, 'ctx', 0, 0, tiled=True).reshape(chan_tp, tok_local)  6.98 us
    ppermute x1, starting transfers between devices, local(): given = lax.ppermute(given, 'tp', CORE_PAIRS)  5.28 us
    ppermute x1, starting transfers between devices, local(): arrived = lax.ppermute(away, 'tp', CHIP_PAIRS)  4.36 us
    all_to_all x1, waiting for transfers between devices, local(): lax.all_to_all(mix, 'ctx', 0, 0, tiled=True).reshape(chan_tp, tok_local)  4.29 us
    ppermute x1, waiting for transfers between devices, local(): arrived = lax.ppermute(away, 'tp', CHIP_PAIRS)  3.27 us
    pallas_call x1, Pallas kernels, turn(): pl.pallas_call(turn_kernel, out_shape=jax.ShapeDtypeStruct((total, width)...  2.77 us
  transfers between devices with their start and end apart: 6, of which 3 were waited for; matrix products, arithmetic and copies ran while one was open for 0% of the time, Pallas kernels for 9%

profile of v7, /device:TPU:1, one launch (start us, length us, event | category | flops | bytes accessed | tf_op | source)
XLA Modules:
  0.0 71.3 jit_solution(12531689287880394204)
XLA Ops:
  0.0 1.7 %pack.1 = bf16[128,8,128]{2,1,0:T(8,128)(2,1)} custom-call(bf16[3,512,128]{2,1,0:T(8,128)(2,1)} %features_ref.1), custom_call_target="tpu_custom_call" | custom-call | flops 262144 | bytes 524288 | tf_op jit(solution)/shard_map/pack/pallas_call | solution.py:118
  1.7 19.3 %all-to-all-start = ((bf16[128,8,128]{2,1,0:T(8,128)(2,1)}), bf16[128,8,128]{2,1,0:T(8,128)(2,1)S(1)}, u32[]{:S(2)}, u32[]{:S(2)}) async-start(bf16[128,8,128]{2,1,0:T(8,128)(2,1)} %pack.1), calls=%async_computation | async-start | bytes 524288 | tf_op jit(solution)/shard_map/all_to_all | solution.py:313
  21.0 1.4 %prepare.1 = (bf16[16,16512]{1,0:T(8,128)(2,1)S(1)}, f32[4,8,128]{2,1,0:T(8,128)S(1)}) custom-call(s32[1]{0:T(128)} %bitcast.1.rank_ref, bf16[32,16384]{1,0:T(8,128)(2,1)} %filter_ref.1, f32[3,3,512]{2,1,0:T(4,128)} %taps_ref.3, f32[512]{0:T(512)} %skip_ref.1), custom_call_target="tpu_custom_call" | custom-call | flops 4194304 | bytes 1048576 | tf_op jit(solution)/shard_map/prepare/pallas_call | solution.py:70
  22.4 11.4 %all-to-all-done.value_ref = bf16[128,8,128]{2,1,0:T(8,128)(2,1)S(1)} async-done(((bf16[128,8,128]{2,1,0:T(8,128)(2,1)}), bf16[128,8,128]{2,1,0:T(8,128)(2,1)S(1)}, u32[]{:S(2)}, u32[]{:S(2)}) %all-to-all-start) | async-done | bytes 262176 | tf_op jit(solution)/shard_map/all_to_all | solution.py:313
  33.7 2.6 %long_conv.1 = bf16[512,128]{1,0:T(8,128)(2,1)} custom-call(bf16[128,8,128]{2,1,0:T(8,128)(2,1)S(1)} %all-to-all-done.value_ref, bf16[16,16512]{1,0:T(8,128)(2,1)S(1)} %get-tuple-element.7.line_ref, f32[4,8,128]{2,1,0:T(8,128)S(1)} %get-tuple-element.8.tiles_ref), custom_call_target="tpu_custom_call" | custom-call | flops 2147483648 | bytes 1048576 | tf_op jit(solution)/shard_map/long_conv/pallas_call | solution.py:191
  36.3 7.0 %all-to-all-start.1 = ((bf16[128,4,128]{2,1,0:T(4,128)(2,1)}), bf16[128,4,128]{2,1,0:T(4,128)(2,1)S(1)}, u32[]{:S(2)}, u32[]{:S(2)}) async-start(bf16[128,4,128]{2,1,0:T(4,128)(2,1)} %bitcast.2), calls=%async_computation.1 | async-start | bytes 262144 | tf_op jit(solution)/shard_map/all_to_all | solution.py:318
  43.3 1.0 %edge.1 = bf16[16,512]{1,0:T(8,128)(2,1)S(1)} custom-call(bf16[3,512,128]{2,1,0:T(8,128)(2,1)} %features_ref.1), custom_call_target="tpu_custom_call" | custom-call | flops 65536 | bytes 131072 | tf_op jit(solution)/shard_map/edge/pallas_call | solution.py:233
  44.3 2.5 %collective-permute-start = (bf16[16,512]{1,0:T(8,128)(2,1)S(1)}, bf16[16,512]{1,0:T(8,128)(2,1)S(1)}, u32[]{:S(2)}, u32[]{:S(2)}) collective-permute-start(bf16[16,512]{1,0:T(8,128)(2,1)S(1)} %edge.1), channel_id=1, source_target_pairs={{0,4},{4,8},{8,12},{12,16},{16,20},{20,24},{24,28},{28,32},{32,36}... | collective-permute-start | bytes 49160 | tf_op jit(solution)/shard_map/ppermute | solution.py:316
  46.8 0.0 copy-start
  46.8 0.0 copy-start.1
  46.8 2.8 %turn.1.weight_ref = bf16[2048,512]{1,0:T(8,128)(2,1)S(1)} custom-call(bf16[512,2048]{1,0:T(8,128)(2,1)} %weight_ref.1), custom_call_target="tpu_custom_call" | custom-call | flops 1048576 | bytes 4194304 | tf_op jit(solution)/shard_map/turn/pallas_call | solution.py:215
  49.6 0.0 collective-permute-done.halo_ref
  49.6 0.6 query_conv.1.q_ref
  50.2 4.3 %all-to-all-done.1 = bf16[128,4,128]{2,1,0:T(4,128)(2,1)S(1)} async-done(((bf16[128,4,128]{2,1,0:T(4,128)(2,1)}), bf16[128,4,128]{2,1,0:T(4,128)(2,1)S(1)}, u32[]{:S(2)}, u32[]{:S(2)}) %all-to-all-start.1) | async-done | bytes 131104 | tf_op jit(solution)/shard_map/all_to_all | solution.py:318
  54.5 0.3 shard_map.57
  54.8 5.3 %collective-permute-start.2 = (bf16[512,128]{1,0:T(8,128)(2,1)S(1)}, bf16[512,128]{1,0:T(8,128)(2,1)S(1)}, u32[]{:S(2)}, u32[]{:S(2)}) collective-permute-start(bf16[512,128]{1,0:T(8,128)(2,1)S(1)} %shard_map.57), channel_id=1, source_target_pairs={{0,1},{1,0},{2,3},{3,2},{4,5},{5,4},{6,7},{7,6},{8,9},{9,8},{10,11... | collective-permute-start | bytes 393224 | tf_op jit(solution)/shard_map/ppermute | solution.py:324
  60.1 0.3 shard_map.55
  60.4 1.9 %collective-permute-start.1 = (bf16[512,128]{1,0:T(8,128)(2,1)S(1)}, bf16[512,128]{1,0:T(8,128)(2,1)S(1)}, u32[]{:S(2)}, u32[]{:S(2)}) collective-permute-start(bf16[512,128]{1,0:T(8,128)(2,1)S(1)} %shard_map.55), channel_id=1, source_target_pairs={{0,1},{1,0},{2,3},{3,2},{4,5},{5,4},{6,7},{7,6},{8,9},{9,8},{10,11... | collective-permute-start | bytes 393224 | tf_op jit(solution)/shard_map/ppermute | solution.py:328
  62.3 0.0 collective-permute-done.2.given_ref
  62.3 0.3 shard_map.58
  62.6 4.4 %collective-permute-start.3 = (bf16[512,128]{1,0:T(8,128)(2,1)S(1)}, bf16[512,128]{1,0:T(8,128)(2,1)S(1)}, u32[]{:S(2)}, u32[]{:S(2)}) collective-permute-start(bf16[512,128]{1,0:T(8,128)(2,1)S(1)} %shard_map.58), channel_id=1, source_target_pairs={{0,2},{2,0},{1,3},{3,1},{4,6},{6,4},{5,7},{7,5},{8,10},{10,8},{9,1... | collective-permute-start | bytes 393224 | tf_op jit(solution)/shard_map/ppermute | solution.py:326
  67.0 0.3 shard_map.56
  67.3 3.3 %collective-permute-done.3 = bf16[512,128]{1,0:T(8,128)(2,1)S(1)} collective-permute-done((bf16[512,128]{1,0:T(8,128)(2,1)S(1)}, bf16[512,128]{1,0:T(8,128)(2,1)S(1)}, u32[]{:S(2)}, u32[]{:S(2)}) %collective-permute-start.3) | collective-permute-done | bytes 131104 | tf_op jit(solution)/shard_map/ppermute | solution.py:326
  70.6 0.7 add_convert_fusion
  (3 shorter events, 0.0 us)
Async XLA Ops:
  1.7 32.1 %all-to-all-start = ((bf16[128,8,128]{2,1,0:T(8,128)(2,1)}), bf16[128,8,128]{2,1,0:T(8,128)(2,1)S(1)}, u32[]{:S(2)}, u32[]{:S(2)}) async-start(bf16[128,8,128]{2,1,0:T(8,128)(2,1)} %pack.1), calls=%async_computation | async-start | bytes 524288 | tf_op jit(solution)/shard_map/all_to_all | solution.py:313
  36.3 18.2 %all-to-all-start.1 = ((bf16[128,4,128]{2,1,0:T(4,128)(2,1)}), bf16[128,4,128]{2,1,0:T(4,128)(2,1)S(1)}, u32[]{:S(2)}, u32[]{:S(2)}) async-start(bf16[128,4,128]{2,1,0:T(4,128)(2,1)} %bitcast.2), calls=%async_computation.1 | async-start | bytes 262144 | tf_op jit(solution)/shard_map/all_to_all | solution.py:318
  44.3 5.3 %collective-permute-start = (bf16[16,512]{1,0:T(8,128)(2,1)S(1)}, bf16[16,512]{1,0:T(8,128)(2,1)S(1)}, u32[]{:S(2)}, u32[]{:S(2)}) collective-permute-start(bf16[16,512]{1,0:T(8,128)(2,1)S(1)} %edge.1), channel_id=1, source_target_pairs={{0,4},{4,8},{8,12},{12,16},{16,20},{20,24},{24,28},{28,32},{32,36}... | collective-permute-start | bytes 49160 | tf_op jit(solution)/shard_map/ppermute | solution.py:316
  46.8 2.8 %copy-start = (bf16[3,512,128]{2,1,0:T(8,128)(2,1)S(1)}, bf16[3,512,128]{2,1,0:T(8,128)(2,1)}, u32[]{:S(2)}) copy-start(bf16[3,512,128]{2,1,0:T(8,128)(2,1)} %features_ref.1) | copy-start | bytes 1179652
  46.8 2.8 %copy-start.1 = (f32[3,3,512]{2,1,0:T(4,128)S(1)}, f32[3,3,512]{2,1,0:T(4,128)}, u32[]{:S(2)}) copy-start(f32[3,3,512]{2,1,0:T(4,128)} %taps_ref.3) | copy-start | bytes 55300
  54.8 7.5 %collective-permute-start.2 = (bf16[512,128]{1,0:T(8,128)(2,1)S(1)}, bf16[512,128]{1,0:T(8,128)(2,1)S(1)}, u32[]{:S(2)}, u32[]{:S(2)}) collective-permute-start(bf16[512,128]{1,0:T(8,128)(2,1)S(1)} %shard_map.57), channel_id=1, source_target_pairs={{0,1},{1,0},{2,3},{3,2},{4,5},{5,4},{6,7},{7,6},{8,9},{9,8},{10,11... | collective-permute-start | bytes 393224 | tf_op jit(solution)/shard_map/ppermute | solution.py:324
  60.4 6.6 %collective-permute-start.1 = (bf16[512,128]{1,0:T(8,128)(2,1)S(1)}, bf16[512,128]{1,0:T(8,128)(2,1)S(1)}, u32[]{:S(2)}, u32[]{:S(2)}) collective-permute-start(bf16[512,128]{1,0:T(8,128)(2,1)S(1)} %shard_map.55), channel_id=1, source_target_pairs={{0,1},{1,0},{2,3},{3,2},{4,5},{5,4},{6,7},{7,6},{8,9},{9,8},{10,11... | collective-permute-start | bytes 393224 | tf_op jit(solution)/shard_map/ppermute | solution.py:328
  62.6 8.0 %collective-permute-start.3 = (bf16[512,128]{1,0:T(8,128)(2,1)S(1)}, bf16[512,128]{1,0:T(8,128)(2,1)S(1)}, u32[]{:S(2)}, u32[]{:S(2)}) collective-permute-start(bf16[512,128]{1,0:T(8,128)(2,1)S(1)} %shard_map.58), channel_id=1, source_target_pairs={{0,2},{2,0},{1,3},{3,1},{4,6},{6,4},{5,7},{7,5},{8,10},{10,8},{9,1... | collective-permute-start | bytes 393224 | tf_op jit(solution)/shard_map/ppermute | solution.py:326

commit v8 on v5

--- a/solution.py
+++ b/solution.py
@@ -10,6 +10,7 @@
 LANES = 128
 CHUNK = 1024
 LEAD = 48
+PACK_STEPS = 4
 CORE_PAIRS = [(0, 1), (1, 0), (2, 3), (3, 2)]
 CHIP_PAIRS = [(0, 2), (2, 0), (1, 3), (3, 1)]
 
@@ -87,31 +88,35 @@
     )(rank, filters, short_taps, skip_gain)
 
 
-def pack_kernel(k_ref, v_ref, out_ref):
-    rows = k_ref.shape[1]
-    k = k_ref[0].astype(f32).reshape(rows // 8, 8, LANES)
-    v = v_ref[0].astype(f32).reshape(rows // 8, 8, LANES)
-    upper = lax.broadcasted_iota(jnp.int32, k.shape, 1) < 4
-    even = jnp.where(upper, k, pltpu.roll(v, 4, 1))
-    odd = jnp.where(upper, pltpu.roll(k, 4, 1), v)
-    out_ref[...] = jnp.stack([even, odd], axis=1).reshape(rows // 4, 8, LANES).astype(bf16)
+def pack_kernel(features_ref, out_ref, sems):
+    blocks = out_ref.shape[0] // PACK_STEPS
+    copies = []
+    for row in range(2):
+        for step in range(PACK_STEPS):
+            here = slice(step * blocks, (step + 1) * blocks)
+            copies.append(
+                pltpu.make_async_copy(
+                    features_ref.at[1 + row, here], out_ref.at[here, row], sems.at[row * PACK_STEPS + step]
+                )
+            )
+            copies[-1].start()
+    for copy in copies:
+        copy.wait()
 
 
 def pack(features):
-    rows = features.shape[1]
+    rows, blocks, channels, tokens = features.shape
+    in_place = pl.BlockSpec(memory_space=pltpu.HBM)
     return pl.pallas_call(
         pack_kernel,
-        out_shape=jax.ShapeDtypeStruct((rows // 4, 8, LANES), bf16),
-        grid=(1,),
-        in_specs=[
-            pl.BlockSpec((1, rows, LANES), lambda i: (1, 0, 0)),
-            pl.BlockSpec((1, rows, LANES), lambda i: (2, 0, 0)),
-        ],
-        out_specs=pl.BlockSpec((rows // 4, 8, LANES), lambda i: (0, 0, 0)),
+        out_shape=jax.ShapeDtypeStruct((blocks, rows - 1, channels, tokens), bf16),
+        in_specs=[in_place],
+        out_specs=in_place,
+        scratch_shapes=[pltpu.SemaphoreType.DMA((2 * PACK_STEPS,))],
         compiler_params=params(16),
         cost_estimate=pl.CostEstimate(flops=1 << 18, bytes_accessed=1 << 19, transcendentals=0),
         name="pack",
-    )(features, features)
+    )(in_hbm(features))
 
 
 def conv_kernel(value_ref, line_ref, tiles_ref, out_ref, pair_ref, sum_ref, table_ref):
@@ -240,23 +245,19 @@
     return (q_ref[...] * mix_ref[...].astype(f32)).astype(bf16)
 
 
+def own_part(member, q_ref, mix_ref, weight_ref):
+    width = mix_ref.shape[0]
+    at = pl.multiple_of(member * width, width)
+    return jnp.dot(weight_ref[pl.ds(at, width), :], gated_of(q_ref, mix_ref), preferred_element_type=f32)
+
+
 def give_kernel(member_ref, q_ref, mix_ref, weight_ref, out_ref):
-    gated = gated_of(q_ref, mix_ref)
-    width = mix_ref.shape[0]
-    for chip in range(2):
-        at = (2 * chip + 1 - member_ref[0] % 2) * width
-        out_ref[chip * width : (chip + 1) * width, :] = jnp.dot(
-            weight_ref[pl.ds(pl.multiple_of(at, width), width), :], gated, preferred_element_type=f32
-        ).astype(bf16)
+    out_ref[...] = own_part(member_ref[0], q_ref, mix_ref, weight_ref).astype(bf16)
 
 
 def keep_kernel(member_ref, q_ref, mix_ref, weight_ref, given_ref, out_ref):
-    gated = gated_of(q_ref, mix_ref)
-    width = mix_ref.shape[0]
-    at = pl.multiple_of(member_ref[0] * width, width)
-    chip = pl.multiple_of(member_ref[0] // 2 * width, width)
-    own = jnp.dot(weight_ref[pl.ds(at, width), :], gated, preferred_element_type=f32)
-    out_ref[...] = (own + given_ref[pl.ds(chip, width), :].astype(f32)).astype(out_ref.dtype)
+    own = own_part(member_ref[0], q_ref, mix_ref, weight_ref)
+    out_ref[...] = (own + given_ref[...].astype(f32)).astype(out_ref.dtype)
 
 
 def project(kernel, member, operands, rows, kind):
@@ -278,8 +279,8 @@
     rank = jnp.full((1,), lax.axis_index("ctx"), jnp.int32)
     member = jnp.full((1,), lax.axis_index("tp"), jnp.int32)
 
-    sent = pack(in_hbm(features))
-    got = lax.all_to_all(sent, "ctx", 0, 0, tiled=True)
+    sent = pack(features.reshape(features.shape[0], ctx_count, chan_dev, tok_local))
+    got = lax.all_to_all(sent, "ctx", 0, 0, tiled=True).reshape(ctx_count, 2 * chan_dev, tok_local)
     line, tiles = prepare(rank, *map(in_hbm, (filters, short_taps, skip_gain)))
     last = edge(in_hbm(features))
     halo = lax.ppermute(last, "ctx", [(i, i + 1) for i in range(ctx_count - 1)])
@@ -287,12 +288,15 @@
     mix = lax.all_to_all(mix, "ctx", 0, 0, tiled=True).reshape(chan_tp, tok_local)
     q = query_conv(features, halo, short_taps)
     weight = turn(in_hbm(out_weight))
-    given = project(give_kernel, member, (q, mix, weight), 2 * chan_tp, bf16)
+    operands = (q, mix, weight)
+    rows = chan_tp
+    given = project(give_kernel, lax.bitwise_xor(member, 3), operands, rows, bf16)
     given = lax.ppermute(given, "tp", CORE_PAIRS)
-    operands = (q, mix, weight, given)
-    away = project(keep_kernel, lax.bitwise_xor(member, 2), operands, chan_tp, bf16)
+    away = project(keep_kernel, lax.bitwise_xor(member, 2), (*operands, given), rows, bf16)
     arrived = lax.ppermute(away, "tp", CHIP_PAIRS)
-    home = project(keep_kernel, member, operands, chan_tp, f32)
+    given_home = project(give_kernel, lax.bitwise_xor(member, 1), operands, rows, bf16)
+    given_home = lax.ppermute(given_home, "tp", CORE_PAIRS)
+    home = project(keep_kernel, member, (*operands, given_home), rows, f32)
     return (home + arrived.astype(f32)).astype(bf16)
 
 

time: 70.8 us -> 79 us (1.12)
  Pallas kernels: 11 us -> 18.5 us
  starting transfers between devices: 38.4 us -> 40.3 us
  waiting for transfers between devices: 20.2 us -> 19 us
    pallas_call x1, Pallas kernels: 1.73 us -> 9.11 us  [pack(): pl.pallas_call(pack_kernel, out_shape=jax.ShapeDtypeStruct((blocks, rows...]
    ppermute x0 -> x1, starting transfers between devices: none -> 1.92 us  [local(): given_home = lax.ppermute(given_home, 'tp', CORE_PAIRS)]
    ppermute x1, waiting for transfers between devices: 1.14 us -> 0.01 us  [local(): given = lax.ppermute(given, 'tp', CORE_PAIRS)]
  transfers between devices with their start and end apart: 5 -> 6, of which waited for: 4 -> 3; matrix products, arithmetic and copies ran while one was open for 0% -> 0% of each run, Pallas kernels for 9% -> 8%
where the time goes in v8:
time: 79 us; the launch traced here: 78.6 us
  starting transfers between devices  40.3 us (51%)
  waiting for transfers between devices  19 us (24%)
  Pallas kernels  18.5 us (23%)
    all_to_all x1, starting transfers between devices, local(): lax.all_to_all(sent, 'ctx', 0, 0, tiled=True)  19.3 us
    all_to_all x1, waiting for transfers between devices, local(): lax.all_to_all(sent, 'ctx', 0, 0, tiled=True)  11.4 us
    pallas_call x1, Pallas kernels, pack(): pl.pallas_call(pack_kernel, out_shape=jax.ShapeDtypeStruct((blocks, rows...  9.11 us
    all_to_all x1, starting transfers between devices, local(): lax.all_to_all(mix, 'ctx', 0, 0, tiled=True).reshape(chan_tp, tok_local)  6.97 us
    ppermute x1, starting transfers between devices, local(): given = lax.ppermute(given, 'tp', CORE_PAIRS)  5.28 us
    ppermute x1, starting transfers between devices, local(): arrived = lax.ppermute(away, 'tp', CHIP_PAIRS)  4.36 us
    all_to_all x1, waiting for transfers between devices, local(): lax.all_to_all(mix, 'ctx', 0, 0, tiled=True).reshape(chan_tp, tok_local)  4.29 us
    ppermute x1, waiting for transfers between devices, local(): arrived = lax.ppermute(away, 'tp', CHIP_PAIRS)  3.27 us
  transfers between devices with their start and end apart: 6, of which 3 were waited for; matrix products, arithmetic and copies ran while one was open for 0% of the time, Pallas kernels for 8%

profile of v8, /device:TPU:1, one launch (start us, length us, event | category | flops | bytes accessed | tf_op | source)
XLA Modules:
  0.0 78.6 jit_solution(1029584328827656290)
XLA Ops:
  0.0 9.1 %pack.1 = bf16[128,2,4,128]{3,2,1,0:T(4,128)(2,1)} custom-call(bf16[3,128,4,128]{3,2,1,0:T(4,128)(2,1)} %bitcast.6), custom_call_target="tpu_custom_call" | custom-call | flops 262144 | bytes 524288 | tf_op jit(solution)/shard_map/pack/pallas_call | solution.py:110
  9.1 19.3 %all-to-all-start = ((bf16[128,2,4,128]{3,2,1,0:T(4,128)(2,1)}), bf16[128,2,4,128]{3,2,1,0:T(4,128)(2,1)S(1)}, u32[]{:S(2)}, u32[]{:S(2)}) async-start(bf16[128,2,4,128]{3,2,1,0:T(4,128)(2,1)} %pack.1), calls=%async_computation | async-start | bytes 524288 | tf_op jit(solution)/shard_map/all_to_all | solution.py:283
  28.4 1.4 %prepare.1 = (bf16[16,16512]{1,0:T(8,128)(2,1)S(1)}, f32[4,8,128]{2,1,0:T(8,128)S(1)}) custom-call(s32[1]{0:T(128)} %bitcast.3.rank_ref, bf16[32,16384]{1,0:T(8,128)(2,1)} %filter_ref.1, f32[3,3,512]{2,1,0:T(4,128)} %taps_ref.3, f32[512]{0:T(512)} %skip_ref.1), custom_call_target="tpu_custom_call" | custom-call | flops 4194304 | bytes 1048576 | tf_op jit(solution)/shard_map/prepare/pallas_call | solution.py:69
  29.8 11.4 %all-to-all-done = bf16[128,2,4,128]{3,2,1,0:T(4,128)(2,1)S(1)} async-done(((bf16[128,2,4,128]{3,2,1,0:T(4,128)(2,1)}), bf16[128,2,4,128]{3,2,1,0:T(4,128)(2,1)S(1)}, u32[]{:S(2)}, u32[]{:S(2)}) %all-to-all-start) | async-done | bytes 262176 | tf_op jit(solution)/shard_map/all_to_all | solution.py:283
  41.2 2.5 %long_conv.1 = bf16[512,128]{1,0:T(8,128)(2,1)} custom-call(bf16[128,8,128]{2,1,0:T(8,128)(2,1)S(1)} %bitcast.11, bf16[16,16512]{1,0:T(8,128)(2,1)S(1)} %get-tuple-element.7.line_ref, f32[4,8,128]{2,1,0:T(8,128)S(1)} %get-tuple-element.8.tiles_ref), custom_call_target="tpu_custom_call" | custom-call | flops 2147483648 | bytes 1048576 | tf_op jit(solution)/shard_map/long_conv/pallas_call | solution.py:163
  43.7 7.0 %all-to-all-start.1 = ((bf16[128,4,128]{2,1,0:T(4,128)(2,1)}), bf16[128,4,128]{2,1,0:T(4,128)(2,1)S(1)}, u32[]{:S(2)}, u32[]{:S(2)}) async-start(bf16[128,4,128]{2,1,0:T(4,128)(2,1)} %bitcast.4), calls=%async_computation.1 | async-start | bytes 262144 | tf_op jit(solution)/shard_map/all_to_all | solution.py:288
  50.7 1.0 %edge.1 = bf16[16,512]{1,0:T(8,128)(2,1)S(1)} custom-call(bf16[3,512,128]{2,1,0:T(8,128)(2,1)} %rows_ref.3), custom_call_target="tpu_custom_call" | custom-call | flops 65536 | bytes 131072 | tf_op jit(solution)/shard_map/edge/pallas_call | solution.py:203
  51.6 2.5 %collective-permute-start = (bf16[16,512]{1,0:T(8,128)(2,1)S(1)}, bf16[16,512]{1,0:T(8,128)(2,1)S(1)}, u32[]{:S(2)}, u32[]{:S(2)}) collective-permute-start(bf16[16,512]{1,0:T(8,128)(2,1)S(1)} %edge.1), channel_id=1, source_target_pairs={{0,4},{4,8},{8,12},{12,16},{16,20},{20,24},{24,28},{28,32},{32,36}... | collective-permute-start | bytes 49160 | tf_op jit(solution)/shard_map/ppermute | solution.py:286
  54.1 0.0 copy-start
  54.1 0.0 copy-start.1
  54.2 2.8 %turn.1.weight_ref = bf16[2048,512]{1,0:T(8,128)(2,1)S(1)} custom-call(bf16[512,2048]{1,0:T(8,128)(2,1)} %weight_ref.1), custom_call_target="tpu_custom_call" | custom-call | flops 1048576 | bytes 4194304 | tf_op jit(solution)/shard_map/turn/pallas_call | solution.py:185
  56.9 0.0 collective-permute-done.halo_ref
  57.0 0.6 query_conv.1.q_ref
  57.6 4.3 %all-to-all-done.1 = bf16[128,4,128]{2,1,0:T(4,128)(2,1)S(1)} async-done(((bf16[128,4,128]{2,1,0:T(4,128)(2,1)}), bf16[128,4,128]{2,1,0:T(4,128)(2,1)S(1)}, u32[]{:S(2)}, u32[]{:S(2)}) %all-to-all-start.1) | async-done | bytes 131104 | tf_op jit(solution)/shard_map/all_to_all | solution.py:288
  61.9 0.3 shard_map.57
  62.2 5.3 %collective-permute-start.2 = (bf16[512,128]{1,0:T(8,128)(2,1)S(1)}, bf16[512,128]{1,0:T(8,128)(2,1)S(1)}, u32[]{:S(2)}, u32[]{:S(2)}) collective-permute-start(bf16[512,128]{1,0:T(8,128)(2,1)S(1)} %shard_map.57), channel_id=1, source_target_pairs={{0,1},{1,0},{2,3},{3,2},{4,5},{5,4},{6,7},{7,6},{8,9},{9,8},{10,11... | collective-permute-start | bytes 393224 | tf_op jit(solution)/shard_map/ppermute | solution.py:294
  67.5 0.3 shard_map.55
  67.8 1.9 %collective-permute-start.1 = (bf16[512,128]{1,0:T(8,128)(2,1)S(1)}, bf16[512,128]{1,0:T(8,128)(2,1)S(1)}, u32[]{:S(2)}, u32[]{:S(2)}) collective-permute-start(bf16[512,128]{1,0:T(8,128)(2,1)S(1)} %shard_map.55), channel_id=1, source_target_pairs={{0,1},{1,0},{2,3},{3,2},{4,5},{5,4},{6,7},{7,6},{8,9},{9,8},{10,11... | collective-permute-start | bytes 393224 | tf_op jit(solution)/shard_map/ppermute | solution.py:298
  69.7 0.0 collective-permute-done.2.given_ref
  69.7 0.3 shard_map.58
  70.0 4.4 %collective-permute-start.3 = (bf16[512,128]{1,0:T(8,128)(2,1)S(1)}, bf16[512,128]{1,0:T(8,128)(2,1)S(1)}, u32[]{:S(2)}, u32[]{:S(2)}) collective-permute-start(bf16[512,128]{1,0:T(8,128)(2,1)S(1)} %shard_map.58), channel_id=1, source_target_pairs={{0,2},{2,0},{1,3},{3,1},{4,6},{6,4},{5,7},{7,5},{8,10},{10,8},{9,1... | collective-permute-start | bytes 393224 | tf_op jit(solution)/shard_map/ppermute | solution.py:296
  74.4 0.3 shard_map.56
  74.7 3.3 %collective-permute-done.3 = bf16[512,128]{1,0:T(8,128)(2,1)S(1)} collective-permute-done((bf16[512,128]{1,0:T(8,128)(2,1)S(1)}, bf16[512,128]{1,0:T(8,128)(2,1)S(1)}, u32[]{:S(2)}, u32[]{:S(2)}) %collective-permute-start.3) | collective-permute-done | bytes 131104 | tf_op jit(solution)/shard_map/ppermute | solution.py:296
  78.0 0.7 add_convert_fusion
  (3 shorter events, 0.0 us)
Async XLA Ops:
  9.1 32.1 %all-to-all-start = ((bf16[128,2,4,128]{3,2,1,0:T(4,128)(2,1)}), bf16[128,2,4,128]{3,2,1,0:T(4,128)(2,1)S(1)}, u32[]{:S(2)}, u32[]{:S(2)}) async-start(bf16[128,2,4,128]{3,2,1,0:T(4,128)(2,1)} %pack.1), calls=%async_computation | async-start | bytes 524288 | tf_op jit(solution)/shard_map/all_to_all | solution.py:283
  43.7 18.2 %all-to-all-start.1 = ((bf16[128,4,128]{2,1,0:T(4,128)(2,1)}), bf16[128,4,128]{2,1,0:T(4,128)(2,1)S(1)}, u32[]{:S(2)}, u32[]{:S(2)}) async-start(bf16[128,4,128]{2,1,0:T(4,128)(2,1)} %bitcast.4), calls=%async_computation.1 | async-start | bytes 262144 | tf_op jit(solution)/shard_map/all_to_all | solution.py:288
  51.6 5.3 %collective-permute-start = (bf16[16,512]{1,0:T(8,128)(2,1)S(1)}, bf16[16,512]{1,0:T(8,128)(2,1)S(1)}, u32[]{:S(2)}, u32[]{:S(2)}) collective-permute-start(bf16[16,512]{1,0:T(8,128)(2,1)S(1)} %edge.1), channel_id=1, source_target_pairs={{0,4},{4,8},{8,12},{12,16},{16,20},{20,24},{24,28},{28,32},{32,36}... | collective-permute-start | bytes 49160 | tf_op jit(solution)/shard_map/ppermute | solution.py:286
  54.1 2.8 %copy-start = (bf16[3,512,128]{2,1,0:T(8,128)(2,1)S(1)}, bf16[3,512,128]{2,1,0:T(8,128)(2,1)}, u32[]{:S(2)}) copy-start(bf16[3,512,128]{2,1,0:T(8,128)(2,1)} %rows_ref.3) | copy-start | bytes 1179652
  54.1 2.8 %copy-start.1 = (f32[3,3,512]{2,1,0:T(4,128)S(1)}, f32[3,3,512]{2,1,0:T(4,128)}, u32[]{:S(2)}) copy-start(f32[3,3,512]{2,1,0:T(4,128)} %taps_ref.3) | copy-start | bytes 55300
  62.2 7.5 %collective-permute-start.2 = (bf16[512,128]{1,0:T(8,128)(2,1)S(1)}, bf16[512,128]{1,0:T(8,128)(2,1)S(1)}, u32[]{:S(2)}, u32[]{:S(2)}) collective-permute-start(bf16[512,128]{1,0:T(8,128)(2,1)S(1)} %shard_map.57), channel_id=1, source_target_pairs={{0,1},{1,0},{2,3},{3,2},{4,5},{5,4},{6,7},{7,6},{8,9},{9,8},{10,11... | collective-permute-start | bytes 393224 | tf_op jit(solution)/shard_map/ppermute | solution.py:294
  67.8 6.6 %collective-permute-start.1 = (bf16[512,128]{1,0:T(8,128)(2,1)S(1)}, bf16[512,128]{1,0:T(8,128)(2,1)S(1)}, u32[]{:S(2)}, u32[]{:S(2)}) collective-permute-start(bf16[512,128]{1,0:T(8,128)(2,1)S(1)} %shard_map.55), channel_id=1, source_target_pairs={{0,1},{1,0},{2,3},{3,2},{4,5},{5,4},{6,7},{7,6},{8,9},{9,8},{10,11... | collective-permute-start | bytes 393224 | tf_op jit(solution)/shard_map/ppermute | solution.py:298
  70.0 8.0 %collective-permute-start.3 = (bf16[512,128]{1,0:T(8,128)(2,1)S(1)}, bf16[512,128]{1,0:T(8,128)(2,1)S(1)}, u32[]{:S(2)}, u32[]{:S(2)}) collective-permute-start(bf16[512,128]{1,0:T(8,128)(2,1)S(1)} %shard_map.58), channel_id=1, source_target_pairs={{0,2},{2,0},{1,3},{3,1},{4,6},{6,4},{5,7},{7,5},{8,10},{10,8},{9,1... | collective-permute-start | bytes 393224 | tf_op jit(solution)/shard_map/ppermute | solution.py:296

commit v9 on v7

--- a/solution.py
+++ b/solution.py
@@ -11,7 +11,6 @@
 CHUNK = 1024
 LEAD = 48
 PACK_STEPS = 4
-OUT_STEPS = 4
 CORE_PAIRS = [(0, 1), (1, 0), (2, 3), (3, 2)]
 CHIP_PAIRS = [(0, 2), (2, 0), (1, 3), (3, 1)]
 
@@ -132,7 +131,7 @@
     )(features)
 
 
-def conv_kernel(value_ref, line_ref, tiles_ref, out_ref, pair_ref, sum_ref, table_ref, mix_ref, sems):
+def conv_kernel(value_ref, line_ref, tiles_ref, out_ref, pair_ref, sum_ref, table_ref):
     blocks = value_ref.shape[0]
     rows = blocks * 4
     value = value_ref[...].astype(f32)
@@ -156,32 +155,17 @@
     direct = tiles_ref[3][None]
     sum_ref[...] = (pair_ref[LEAD:, :LANES].astype(f32).reshape(rows // 8, 8, LANES) * direct).reshape(rows, LANES)
     for index in range(rows // 64):
-        for at in (2 * CHUNK * index, 2 * CHUNK * index + CHUNK):
+        begin, base = 64 * index, CHUNK * index
+        for at in (2 * base, 2 * base + CHUNK):
             fill_table(line_ref, table_ref, at)
-        if index:
-            add_shifted(pair_ref, table_ref, sum_ref, index, 0, rows - 64 * index)
-    stretch = rows // OUT_STEPS
-    leaving = []
-    for begin in range(0, rows, stretch):
-        add_shifted(pair_ref, table_ref, sum_ref, 0, begin, min(stretch, rows - begin))
-        here = slice(begin, begin + stretch)
-        mix_ref[here, :] = sum_ref[here, :].astype(bf16)
-        leaving.append(pltpu.make_async_copy(mix_ref.at[here], out_ref.at[here], sems.at[begin // stretch]))
-        leaving[-1].start()
-    for copy in leaving:
-        copy.wait()
-
-
-def add_shifted(pair_ref, table_ref, sum_ref, index, first, count):
-    base = CHUNK * index
-    left = [pair_ref[LEAD + first - 16 * s : LEAD + first - 16 * s + count, :] for s in range(4)]
-    right = [table_ref[:, base + 256 * s : base + 256 * (s + 1)] for s in range(4)]
-    moved = jnp.dot(jnp.concatenate(left, axis=1), jnp.concatenate(right, axis=0), preferred_element_type=f32)
-    begin = 64 * index + first
-    rows = sum_ref.shape[0]
-    sum_ref[begin : begin + count, :] += moved[:, :LANES]
-    count = min(count, rows - begin - 8)
-    sum_ref[begin + 8 : begin + 8 + count, :] += moved[:count, LANES:]
+        left = [pair_ref[LEAD - 16 * s : LEAD - 16 * s + rows - begin, :] for s in range(4)]
+        right = [table_ref[:, base + 256 * s : base + 256 * (s + 1)] for s in range(4)]
+        moved = jnp.dot(
+            jnp.concatenate(left, axis=1), jnp.concatenate(right, axis=0), preferred_element_type=f32
+        )
+        sum_ref[begin:, :] += moved[:, :LANES]
+        sum_ref[begin + 8 :, :] += moved[: rows - begin - 8, LANES:]
+    out_ref[...] = sum_ref[...].astype(bf16)
 
 
 def long_conv(value, line, tiles):
@@ -192,13 +176,11 @@
         conv_kernel,
         out_shape=jax.ShapeDtypeStruct((rows, LANES), bf16),
         in_specs=[in_vmem] * 3,
-        out_specs=pl.BlockSpec(memory_space=pltpu.HBM),
+        out_specs=in_vmem,
         scratch_shapes=[
             pltpu.VMEM((LEAD + rows, 2 * LANES), bf16),
             pltpu.VMEM((rows, LANES), f32),
             pltpu.VMEM((2 * LANES, seq_len // 2), bf16),
-            pltpu.VMEM((rows, LANES), bf16),
-            pltpu.SemaphoreType.DMA((OUT_STEPS,)),
         ],
         compiler_params=params(16),
         cost_estimate=pl.CostEstimate(flops=1 << 31, bytes_accessed=1 << 20, transcendentals=0),

time: 71.7 us -> 71.7 us (level)
  no operation moved by 1% of the time
where the time goes in v9:
time: 71.7 us; the launch traced here: 71.2 us
  starting transfers between devices  40.3 us (56%)
  waiting for transfers between devices  19 us (26%)
  Pallas kernels  11.1 us (15%)
    all_to_all x1, starting transfers between devices, local(): got = lax.all_to_all(sent, 'ctx', 0, 0, tiled=True)  19.3 us
    all_to_all x1, waiting for transfers between devices, local(): got = lax.all_to_all(sent, 'ctx', 0, 0, tiled=True)  11.4 us
    all_to_all x1, starting transfers between devices, local(): lax.all_to_all(mix, 'ctx', 0, 0, tiled=True).reshape(chan_tp, tok_local)  6.97 us
    ppermute x1, starting transfers between devices, local(): given = lax.ppermute(given, 'tp', CORE_PAIRS)  5.28 us
    ppermute x1, starting transfers between devices, local(): arrived = lax.ppermute(away, 'tp', CHIP_PAIRS)  4.36 us
    all_to_all x1, waiting for transfers between devices, local(): lax.all_to_all(mix, 'ctx', 0, 0, tiled=True).reshape(chan_tp, tok_local)  4.29 us
    ppermute x1, waiting for transfers between devices, local(): arrived = lax.ppermute(away, 'tp', CHIP_PAIRS)  3.28 us
    pallas_call x1, Pallas kernels, turn(): pl.pallas_call(turn_kernel, out_shape=jax.ShapeDtypeStruct((total, width)...  2.77 us
  transfers between devices with their start and end apart: 6, of which 3 were waited for; matrix products, arithmetic and copies ran while one was open for 0% of the time, Pallas kernels for 9%

profile of v9, /device:TPU:1, one launch (start us, length us, event | category | flops | bytes accessed | tf_op | source)
XLA Modules:
  0.0 71.2 jit_solution(6455498125706909885)
XLA Ops:
  0.0 1.7 %pack.1 = bf16[128,8,128]{2,1,0:T(8,128)(2,1)} custom-call(bf16[3,512,128]{2,1,0:T(8,128)(2,1)} %features_ref.1), custom_call_target="tpu_custom_call" | custom-call | flops 262144 | bytes 524288 | tf_op jit(solution)/shard_map/pack/pallas_call | solution.py:117
  1.7 19.3 %all-to-all-start = ((bf16[128,8,128]{2,1,0:T(8,128)(2,1)}), bf16[128,8,128]{2,1,0:T(8,128)(2,1)S(1)}, u32[]{:S(2)}, u32[]{:S(2)}) async-start(bf16[128,8,128]{2,1,0:T(8,128)(2,1)} %pack.1), calls=%async_computation | async-start | bytes 524288 | tf_op jit(solution)/shard_map/all_to_all | solution.py:295
  21.0 1.4 %prepare.1 = (bf16[16,16512]{1,0:T(8,128)(2,1)S(1)}, f32[4,8,128]{2,1,0:T(8,128)S(1)}) custom-call(s32[1]{0:T(128)} %bitcast.1.rank_ref, bf16[32,16384]{1,0:T(8,128)(2,1)} %filter_ref.1, f32[3,3,512]{2,1,0:T(4,128)} %taps_ref.3, f32[512]{0:T(512)} %skip_ref.1), custom_call_target="tpu_custom_call" | custom-call | flops 4194304 | bytes 1048576 | tf_op jit(solution)/shard_map/prepare/pallas_call | solution.py:69
  22.4 11.4 %all-to-all-done.value_ref = bf16[128,8,128]{2,1,0:T(8,128)(2,1)S(1)} async-done(((bf16[128,8,128]{2,1,0:T(8,128)(2,1)}), bf16[128,8,128]{2,1,0:T(8,128)(2,1)S(1)}, u32[]{:S(2)}, u32[]{:S(2)}) %all-to-all-start) | async-done | bytes 262176 | tf_op jit(solution)/shard_map/all_to_all | solution.py:295
  33.7 2.5 %long_conv.1 = bf16[512,128]{1,0:T(8,128)(2,1)} custom-call(bf16[128,8,128]{2,1,0:T(8,128)(2,1)S(1)} %all-to-all-done.value_ref, bf16[16,16512]{1,0:T(8,128)(2,1)S(1)} %get-tuple-element.7.line_ref, f32[4,8,128]{2,1,0:T(8,128)S(1)} %get-tuple-element.8.tiles_ref), custom_call_target="tpu_custom_call" | custom-call | flops 2147483648 | bytes 1048576 | tf_op jit(solution)/shard_map/long_conv/pallas_call | solution.py:175
  36.2 7.0 %all-to-all-start.1 = ((bf16[128,4,128]{2,1,0:T(4,128)(2,1)}), bf16[128,4,128]{2,1,0:T(4,128)(2,1)S(1)}, u32[]{:S(2)}, u32[]{:S(2)}) async-start(bf16[128,4,128]{2,1,0:T(4,128)(2,1)} %bitcast.2), calls=%async_computation.1 | async-start | bytes 262144 | tf_op jit(solution)/shard_map/all_to_all | solution.py:300
  43.2 1.0 %edge.1 = bf16[16,512]{1,0:T(8,128)(2,1)S(1)} custom-call(bf16[3,512,128]{2,1,0:T(8,128)(2,1)} %features_ref.1), custom_call_target="tpu_custom_call" | custom-call | flops 65536 | bytes 131072 | tf_op jit(solution)/shard_map/edge/pallas_call | solution.py:215
  44.2 2.5 %collective-permute-start = (bf16[16,512]{1,0:T(8,128)(2,1)S(1)}, bf16[16,512]{1,0:T(8,128)(2,1)S(1)}, u32[]{:S(2)}, u32[]{:S(2)}) collective-permute-start(bf16[16,512]{1,0:T(8,128)(2,1)S(1)} %edge.1), channel_id=1, source_target_pairs={{0,4},{4,8},{8,12},{12,16},{16,20},{20,24},{24,28},{28,32},{32,36}... | collective-permute-start | bytes 49160 | tf_op jit(solution)/shard_map/ppermute | solution.py:298
  46.7 0.0 copy-start
  46.7 0.0 copy-start.1
  46.7 2.8 %turn.1.weight_ref = bf16[2048,512]{1,0:T(8,128)(2,1)S(1)} custom-call(bf16[512,2048]{1,0:T(8,128)(2,1)} %weight_ref.1), custom_call_target="tpu_custom_call" | custom-call | flops 1048576 | bytes 4194304 | tf_op jit(solution)/shard_map/turn/pallas_call | solution.py:197
  49.5 0.0 collective-permute-done.halo_ref
  49.5 0.6 query_conv.1.q_ref
  50.1 4.3 %all-to-all-done.1 = bf16[128,4,128]{2,1,0:T(4,128)(2,1)S(1)} async-done(((bf16[128,4,128]{2,1,0:T(4,128)(2,1)}), bf16[128,4,128]{2,1,0:T(4,128)(2,1)S(1)}, u32[]{:S(2)}, u32[]{:S(2)}) %all-to-all-start.1) | async-done | bytes 131104 | tf_op jit(solution)/shard_map/all_to_all | solution.py:300
  54.4 0.3 shard_map.57
  54.7 5.3 %collective-permute-start.2 = (bf16[512,128]{1,0:T(8,128)(2,1)S(1)}, bf16[512,128]{1,0:T(8,128)(2,1)S(1)}, u32[]{:S(2)}, u32[]{:S(2)}) collective-permute-start(bf16[512,128]{1,0:T(8,128)(2,1)S(1)} %shard_map.57), channel_id=1, source_target_pairs={{0,1},{1,0},{2,3},{3,2},{4,5},{5,4},{6,7},{7,6},{8,9},{9,8},{10,11... | collective-permute-start | bytes 393224 | tf_op jit(solution)/shard_map/ppermute | solution.py:306
  60.0 0.3 shard_map.55
  60.3 1.9 %collective-permute-start.1 = (bf16[512,128]{1,0:T(8,128)(2,1)S(1)}, bf16[512,128]{1,0:T(8,128)(2,1)S(1)}, u32[]{:S(2)}, u32[]{:S(2)}) collective-permute-start(bf16[512,128]{1,0:T(8,128)(2,1)S(1)} %shard_map.55), channel_id=1, source_target_pairs={{0,1},{1,0},{2,3},{3,2},{4,5},{5,4},{6,7},{7,6},{8,9},{9,8},{10,11... | collective-permute-start | bytes 393224 | tf_op jit(solution)/shard_map/ppermute | solution.py:310
  62.2 0.3 shard_map.58
  62.6 4.4 %collective-permute-start.3 = (bf16[512,128]{1,0:T(8,128)(2,1)S(1)}, bf16[512,128]{1,0:T(8,128)(2,1)S(1)}, u32[]{:S(2)}, u32[]{:S(2)}) collective-permute-start(bf16[512,128]{1,0:T(8,128)(2,1)S(1)} %shard_map.58), channel_id=1, source_target_pairs={{0,2},{2,0},{1,3},{3,1},{4,6},{6,4},{5,7},{7,5},{8,10},{10,8},{9,1... | collective-permute-start | bytes 393224 | tf_op jit(solution)/shard_map/ppermute | solution.py:308
  66.9 0.0 collective-permute-done.1.given_ref
  66.9 0.3 shard_map.56
  67.2 3.3 %collective-permute-done.3 = bf16[512,128]{1,0:T(8,128)(2,1)S(1)} collective-permute-done((bf16[512,128]{1,0:T(8,128)(2,1)S(1)}, bf16[512,128]{1,0:T(8,128)(2,1)S(1)}, u32[]{:S(2)}, u32[]{:S(2)}) %collective-permute-start.3) | collective-permute-done | bytes 131104 | tf_op jit(solution)/shard_map/ppermute | solution.py:308
  70.5 0.7 add_convert_fusion
  (3 shorter events, 0.0 us)
Async XLA Ops:
  1.7 32.1 %all-to-all-start = ((bf16[128,8,128]{2,1,0:T(8,128)(2,1)}), bf16[128,8,128]{2,1,0:T(8,128)(2,1)S(1)}, u32[]{:S(2)}, u32[]{:S(2)}) async-start(bf16[128,8,128]{2,1,0:T(8,128)(2,1)} %pack.1), calls=%async_computation | async-start | bytes 524288 | tf_op jit(solution)/shard_map/all_to_all | solution.py:295
  36.2 18.2 %all-to-all-start.1 = ((bf16[128,4,128]{2,1,0:T(4,128)(2,1)}), bf16[128,4,128]{2,1,0:T(4,128)(2,1)S(1)}, u32[]{:S(2)}, u32[]{:S(2)}) async-start(bf16[128,4,128]{2,1,0:T(4,128)(2,1)} %bitcast.2), calls=%async_computation.1 | async-start | bytes 262144 | tf_op jit(solution)/shard_map/all_to_all | solution.py:300
  44.2 5.3 %collective-permute-start = (bf16[16,512]{1,0:T(8,128)(2,1)S(1)}, bf16[16,512]{1,0:T(8,128)(2,1)S(1)}, u32[]{:S(2)}, u32[]{:S(2)}) collective-permute-start(bf16[16,512]{1,0:T(8,128)(2,1)S(1)} %edge.1), channel_id=1, source_target_pairs={{0,4},{4,8},{8,12},{12,16},{16,20},{20,24},{24,28},{28,32},{32,36}... | collective-permute-start | bytes 49160 | tf_op jit(solution)/shard_map/ppermute | solution.py:298
  46.7 2.8 %copy-start = (bf16[3,512,128]{2,1,0:T(8,128)(2,1)S(1)}, bf16[3,512,128]{2,1,0:T(8,128)(2,1)}, u32[]{:S(2)}) copy-start(bf16[3,512,128]{2,1,0:T(8,128)(2,1)} %features_ref.1) | copy-start | bytes 1179652
  46.7 2.8 %copy-start.1 = (f32[3,3,512]{2,1,0:T(4,128)S(1)}, f32[3,3,512]{2,1,0:T(4,128)}, u32[]{:S(2)}) copy-start(f32[3,3,512]{2,1,0:T(4,128)} %taps_ref.3) | copy-start | bytes 55300
  54.7 7.5 %collective-permute-start.2 = (bf16[512,128]{1,0:T(8,128)(2,1)S(1)}, bf16[512,128]{1,0:T(8,128)(2,1)S(1)}, u32[]{:S(2)}, u32[]{:S(2)}) collective-permute-start(bf16[512,128]{1,0:T(8,128)(2,1)S(1)} %shard_map.57), channel_id=1, source_target_pairs={{0,1},{1,0},{2,3},{3,2},{4,5},{5,4},{6,7},{7,6},{8,9},{9,8},{10,11... | collective-permute-start | bytes 393224 | tf_op jit(solution)/shard_map/ppermute | solution.py:306
  60.3 6.6 %collective-permute-start.1 = (bf16[512,128]{1,0:T(8,128)(2,1)S(1)}, bf16[512,128]{1,0:T(8,128)(2,1)S(1)}, u32[]{:S(2)}, u32[]{:S(2)}) collective-permute-start(bf16[512,128]{1,0:T(8,128)(2,1)S(1)} %shard_map.55), channel_id=1, source_target_pairs={{0,1},{1,0},{2,3},{3,2},{4,5},{5,4},{6,7},{7,6},{8,9},{9,8},{10,11... | collective-permute-start | bytes 393224 | tf_op jit(solution)/shard_map/ppermute | solution.py:310
  62.6 8.0 %collective-permute-start.3 = (bf16[512,128]{1,0:T(8,128)(2,1)S(1)}, bf16[512,128]{1,0:T(8,128)(2,1)S(1)}, u32[]{:S(2)}, u32[]{:S(2)}) collective-permute-start(bf16[512,128]{1,0:T(8,128)(2,1)S(1)} %shard_map.58), channel_id=1, source_target_pairs={{0,2},{2,0},{1,3},{3,1},{4,6},{6,4},{5,7},{7,5},{8,10},{10,8},{9,1... | collective-permute-start | bytes 393224 | tf_op jit(solution)/shard_map/ppermute | solution.py:308

commit v10 on v9

--- a/solution.py
+++ b/solution.py
@@ -103,7 +103,8 @@
         upper = lax.broadcasted_iota(jnp.int32, k.shape, 1) < 4
         even = jnp.where(upper, k, pltpu.roll(v, 4, 1))
         odd = jnp.where(upper, pltpu.roll(k, 4, 1), v)
-        there = slice(step * rows // 4, (step + 1) * rows // 4)
+        after = (step + PACK_STEPS // 2) % PACK_STEPS
+        there = slice(after * rows // 4, (after + 1) * rows // 4)
         packed_ref[there] = jnp.stack([even, odd], axis=1).reshape(rows // 4, 8, LANES).astype(bf16)
         stores.append(pltpu.make_async_copy(packed_ref.at[there], out_ref.at[there], out_sems.at[step]))
         stores[-1].start()
@@ -134,7 +135,7 @@
 def conv_kernel(value_ref, line_ref, tiles_ref, out_ref, pair_ref, sum_ref, table_ref):
     blocks = value_ref.shape[0]
     rows = blocks * 4
-    value = value_ref[...].astype(f32)
+    value = jnp.concatenate([value_ref[blocks // 2 :], value_ref[: blocks // 2]], axis=0).astype(f32)
     lane = lax.broadcasted_iota(jnp.int32, value.shape, 2)
     sub = lax.broadcasted_iota(jnp.int32, (blocks // 2, 8, LANES), 1)
 
@@ -292,7 +293,8 @@
     member = jnp.full((1,), lax.axis_index("tp"), jnp.int32)
 
     sent = pack(in_hbm(features))
-    got = lax.all_to_all(sent, "ctx", 0, 0, tiled=True)
+    order = [(i + ctx_count // 2) % ctx_count for i in range(ctx_count)]
+    got = lax.all_to_all(sent, "ctx", 0, 0, axis_index_groups=[order], tiled=True)
     line, tiles = prepare(rank, *map(in_hbm, (filters, short_taps, skip_gain)))
     last = edge(in_hbm(features))
     halo = lax.ppermute(last, "ctx", [(i, i + 1) for i in range(ctx_count - 1)])

time: 71.7 us -> 71.1 us (level)
  waiting for transfers between devices: 19 us -> 15.8 us
  starting transfers between devices: 40.3 us -> 42.9 us
    all_to_all x1, waiting for transfers between devices: 11.4 us -> 8.22 us  [local(): lax.all_to_all(sent, 'ctx', 0, 0, axis_index_groups=[order], tiled=True)]
    all_to_all x1, starting transfers between devices: 6.97 us -> 9.32 us  [local(): lax.all_to_all(mix, 'ctx', 0, 0, tiled=True).reshape(chan_tp, tok_local)]
where the time goes in v10:
time: 71.1 us; the launch traced here: 70.6 us
  starting transfers between devices  42.9 us (60%)
  waiting for transfers between devices  15.8 us (22%)
  Pallas kernels  11 us (15%)
    all_to_all x1, starting transfers between devices, local(): lax.all_to_all(sent, 'ctx', 0, 0, axis_index_groups=[order], tiled=True)  19.3 us
    all_to_all x1, starting transfers between devices, local(): lax.all_to_all(mix, 'ctx', 0, 0, tiled=True).reshape(chan_tp, tok_local)  9.32 us
    all_to_all x1, waiting for transfers between devices, local(): lax.all_to_all(sent, 'ctx', 0, 0, axis_index_groups=[order], tiled=True)  8.22 us
    ppermute x1, starting transfers between devices, local(): given = lax.ppermute(given, 'tp', CORE_PAIRS)  5.49 us
    ppermute x1, starting transfers between devices, local(): arrived = lax.ppermute(away, 'tp', CHIP_PAIRS)  4.36 us
    all_to_all x1, waiting for transfers between devices, local(): lax.all_to_all(mix, 'ctx', 0, 0, tiled=True).reshape(chan_tp, tok_local)  4.29 us
    ppermute x1, waiting for transfers between devices, local(): arrived = lax.ppermute(away, 'tp', CHIP_PAIRS)  3.27 us
    pallas_call x1, Pallas kernels, turn(): pl.pallas_call(turn_kernel, out_shape=jax.ShapeDtypeStruct((total, width)...  2.77 us
  transfers between devices with their start and end apart: 6, of which 3 were waited for; matrix products, arithmetic and copies ran while one was open for 0% of the time, Pallas kernels for 9%

profile of v10, /device:TPU:1, one launch (start us, length us, event | category | flops | bytes accessed | tf_op | source)
XLA Modules:
  0.0 70.6 jit_solution(8480118054653233488)
XLA Ops:
  0.0 1.6 %pack.1 = bf16[128,8,128]{2,1,0:T(8,128)(2,1)} custom-call(bf16[3,512,128]{2,1,0:T(8,128)(2,1)} %features_ref.1), custom_call_target="tpu_custom_call" | custom-call | flops 262144 | bytes 524288 | tf_op jit(solution)/shard_map/pack/pallas_call | solution.py:118
  1.6 19.3 %all-to-all-start = ((bf16[128,8,128]{2,1,0:T(8,128)(2,1)}), bf16[128,8,128]{2,1,0:T(8,128)(2,1)S(1)}, u32[]{:S(2)}, u32[]{:S(2)}) async-start(bf16[128,8,128]{2,1,0:T(8,128)(2,1)} %pack.1), calls=%async_computation | async-start | bytes 524288 | tf_op jit(solution)/shard_map/all_to_all | solution.py:297
  21.0 1.4 %prepare.1 = (bf16[16,16512]{1,0:T(8,128)(2,1)S(1)}, f32[4,8,128]{2,1,0:T(8,128)S(1)}) custom-call(s32[1]{0:T(128)} %bitcast.1.rank_ref, bf16[32,16384]{1,0:T(8,128)(2,1)} %filter_ref.1, f32[3,3,512]{2,1,0:T(4,128)} %taps_ref.3, f32[512]{0:T(512)} %skip_ref.1), custom_call_target="tpu_custom_call" | custom-call | flops 4194304 | bytes 1048576 | tf_op jit(solution)/shard_map/prepare/pallas_call | solution.py:69
  22.4 8.2 %all-to-all-done.value_ref = bf16[128,8,128]{2,1,0:T(8,128)(2,1)S(1)} async-done(((bf16[128,8,128]{2,1,0:T(8,128)(2,1)}), bf16[128,8,128]{2,1,0:T(8,128)(2,1)S(1)}, u32[]{:S(2)}, u32[]{:S(2)}) %all-to-all-start) | async-done | bytes 262176 | tf_op jit(solution)/shard_map/all_to_all | solution.py:297
  30.6 2.5 %long_conv.1 = bf16[512,128]{1,0:T(8,128)(2,1)} custom-call(bf16[128,8,128]{2,1,0:T(8,128)(2,1)S(1)} %all-to-all-done.value_ref, bf16[16,16512]{1,0:T(8,128)(2,1)S(1)} %get-tuple-element.7.line_ref, f32[4,8,128]{2,1,0:T(8,128)S(1)} %get-tuple-element.8.tiles_ref), custom_call_target="tpu_custom_call" | custom-call | flops 2147483648 | bytes 1048576 | tf_op jit(solution)/shard_map/long_conv/pallas_call | solution.py:176
  33.1 9.3 %all-to-all-start.1 = ((bf16[128,4,128]{2,1,0:T(4,128)(2,1)}), bf16[128,4,128]{2,1,0:T(4,128)(2,1)S(1)}, u32[]{:S(2)}, u32[]{:S(2)}) async-start(bf16[128,4,128]{2,1,0:T(4,128)(2,1)} %bitcast.2), calls=%async_computation.1 | async-start | bytes 262144 | tf_op jit(solution)/shard_map/all_to_all | solution.py:302
  42.4 1.0 %edge.1 = bf16[16,512]{1,0:T(8,128)(2,1)S(1)} custom-call(bf16[3,512,128]{2,1,0:T(8,128)(2,1)} %features_ref.1), custom_call_target="tpu_custom_call" | custom-call | flops 65536 | bytes 131072 | tf_op jit(solution)/shard_map/edge/pallas_call | solution.py:216
  43.4 2.5 %collective-permute-start = (bf16[16,512]{1,0:T(8,128)(2,1)S(1)}, bf16[16,512]{1,0:T(8,128)(2,1)S(1)}, u32[]{:S(2)}, u32[]{:S(2)}) collective-permute-start(bf16[16,512]{1,0:T(8,128)(2,1)S(1)} %edge.1), channel_id=1, source_target_pairs={{0,4},{4,8},{8,12},{12,16},{16,20},{20,24},{24,28},{28,32},{32,36}... | collective-permute-start | bytes 49160 | tf_op jit(solution)/shard_map/ppermute | solution.py:300
  45.9 0.0 copy-start
  45.9 0.0 copy-start.1
  45.9 2.8 %turn.1.weight_ref = bf16[2048,512]{1,0:T(8,128)(2,1)S(1)} custom-call(bf16[512,2048]{1,0:T(8,128)(2,1)} %weight_ref.1), custom_call_target="tpu_custom_call" | custom-call | flops 1048576 | bytes 4194304 | tf_op jit(solution)/shard_map/turn/pallas_call | solution.py:198
  48.7 0.0 collective-permute-done.halo_ref
  48.7 0.6 query_conv.1.q_ref
  49.3 4.3 %all-to-all-done.1 = bf16[128,4,128]{2,1,0:T(4,128)(2,1)S(1)} async-done(((bf16[128,4,128]{2,1,0:T(4,128)(2,1)}), bf16[128,4,128]{2,1,0:T(4,128)(2,1)S(1)}, u32[]{:S(2)}, u32[]{:S(2)}) %all-to-all-start.1) | async-done | bytes 131104 | tf_op jit(solution)/shard_map/all_to_all | solution.py:302
  53.6 0.3 shard_map.57
  53.9 5.5 %collective-permute-start.2 = (bf16[512,128]{1,0:T(8,128)(2,1)S(1)}, bf16[512,128]{1,0:T(8,128)(2,1)S(1)}, u32[]{:S(2)}, u32[]{:S(2)}) collective-permute-start(bf16[512,128]{1,0:T(8,128)(2,1)S(1)} %shard_map.57), channel_id=1, source_target_pairs={{0,1},{1,0},{2,3},{3,2},{4,5},{5,4},{6,7},{7,6},{8,9},{9,8},{10,11... | collective-permute-start | bytes 393224 | tf_op jit(solution)/shard_map/ppermute | solution.py:308
  59.4 0.3 shard_map.55
  59.7 1.9 %collective-permute-start.1 = (bf16[512,128]{1,0:T(8,128)(2,1)S(1)}, bf16[512,128]{1,0:T(8,128)(2,1)S(1)}, u32[]{:S(2)}, u32[]{:S(2)}) collective-permute-start(bf16[512,128]{1,0:T(8,128)(2,1)S(1)} %shard_map.55), channel_id=1, source_target_pairs={{0,1},{1,0},{2,3},{3,2},{4,5},{5,4},{6,7},{7,6},{8,9},{9,8},{10,11... | collective-permute-start | bytes 393224 | tf_op jit(solution)/shard_map/ppermute | solution.py:312
  61.7 0.0 collective-permute-done.2.given_ref
  61.7 0.3 shard_map.58
  62.0 4.4 %collective-permute-start.3 = (bf16[512,128]{1,0:T(8,128)(2,1)S(1)}, bf16[512,128]{1,0:T(8,128)(2,1)S(1)}, u32[]{:S(2)}, u32[]{:S(2)}) collective-permute-start(bf16[512,128]{1,0:T(8,128)(2,1)S(1)} %shard_map.58), channel_id=1, source_target_pairs={{0,2},{2,0},{1,3},{3,1},{4,6},{6,4},{5,7},{7,5},{8,10},{10,8},{9,1... | collective-permute-start | bytes 393224 | tf_op jit(solution)/shard_map/ppermute | solution.py:310
  66.4 0.3 shard_map.56
  66.7 3.3 %collective-permute-done.3 = bf16[512,128]{1,0:T(8,128)(2,1)S(1)} collective-permute-done((bf16[512,128]{1,0:T(8,128)(2,1)S(1)}, bf16[512,128]{1,0:T(8,128)(2,1)S(1)}, u32[]{:S(2)}, u32[]{:S(2)}) %collective-permute-start.3) | collective-permute-done | bytes 131104 | tf_op jit(solution)/shard_map/ppermute | solution.py:310
  69.9 0.7 add_convert_fusion
  (3 shorter events, 0.0 us)
Async XLA Ops:
  1.6 29.0 %all-to-all-start = ((bf16[128,8,128]{2,1,0:T(8,128)(2,1)}), bf16[128,8,128]{2,1,0:T(8,128)(2,1)S(1)}, u32[]{:S(2)}, u32[]{:S(2)}) async-start(bf16[128,8,128]{2,1,0:T(8,128)(2,1)} %pack.1), calls=%async_computation | async-start | bytes 524288 | tf_op jit(solution)/shard_map/all_to_all | solution.py:297
  33.1 20.5 %all-to-all-start.1 = ((bf16[128,4,128]{2,1,0:T(4,128)(2,1)}), bf16[128,4,128]{2,1,0:T(4,128)(2,1)S(1)}, u32[]{:S(2)}, u32[]{:S(2)}) async-start(bf16[128,4,128]{2,1,0:T(4,128)(2,1)} %bitcast.2), calls=%async_computation.1 | async-start | bytes 262144 | tf_op jit(solution)/shard_map/all_to_all | solution.py:302
  43.4 5.3 %collective-permute-start = (bf16[16,512]{1,0:T(8,128)(2,1)S(1)}, bf16[16,512]{1,0:T(8,128)(2,1)S(1)}, u32[]{:S(2)}, u32[]{:S(2)}) collective-permute-start(bf16[16,512]{1,0:T(8,128)(2,1)S(1)} %edge.1), channel_id=1, source_target_pairs={{0,4},{4,8},{8,12},{12,16},{16,20},{20,24},{24,28},{28,32},{32,36}... | collective-permute-start | bytes 49160 | tf_op jit(solution)/shard_map/ppermute | solution.py:300
  45.9 2.8 %copy-start = (bf16[3,512,128]{2,1,0:T(8,128)(2,1)S(1)}, bf16[3,512,128]{2,1,0:T(8,128)(2,1)}, u32[]{:S(2)}) copy-start(bf16[3,512,128]{2,1,0:T(8,128)(2,1)} %features_ref.1) | copy-start | bytes 1179652
  45.9 2.8 %copy-start.1 = (f32[3,3,512]{2,1,0:T(4,128)S(1)}, f32[3,3,512]{2,1,0:T(4,128)}, u32[]{:S(2)}) copy-start(f32[3,3,512]{2,1,0:T(4,128)} %taps_ref.3) | copy-start | bytes 55300
  53.9 7.7 %collective-permute-start.2 = (bf16[512,128]{1,0:T(8,128)(2,1)S(1)}, bf16[512,128]{1,0:T(8,128)(2,1)S(1)}, u32[]{:S(2)}, u32[]{:S(2)}) collective-permute-start(bf16[512,128]{1,0:T(8,128)(2,1)S(1)} %shard_map.57), channel_id=1, source_target_pairs={{0,1},{1,0},{2,3},{3,2},{4,5},{5,4},{6,7},{7,6},{8,9},{9,8},{10,11... | collective-permute-start | bytes 393224 | tf_op jit(solution)/shard_map/ppermute | solution.py:308
  59.7 6.6 %collective-permute-start.1 = (bf16[512,128]{1,0:T(8,128)(2,1)S(1)}, bf16[512,128]{1,0:T(8,128)(2,1)S(1)}, u32[]{:S(2)}, u32[]{:S(2)}) collective-permute-start(bf16[512,128]{1,0:T(8,128)(2,1)S(1)} %shard_map.55), channel_id=1, source_target_pairs={{0,1},{1,0},{2,3},{3,2},{4,5},{5,4},{6,7},{7,6},{8,9},{9,8},{10,11... | collective-permute-start | bytes 393224 | tf_op jit(solution)/shard_map/ppermute | solution.py:312
  62.0 8.0 %collective-permute-start.3 = (bf16[512,128]{1,0:T(8,128)(2,1)S(1)}, bf16[512,128]{1,0:T(8,128)(2,1)S(1)}, u32[]{:S(2)}, u32[]{:S(2)}) collective-permute-start(bf16[512,128]{1,0:T(8,128)(2,1)S(1)} %shard_map.58), channel_id=1, source_target_pairs={{0,2},{2,0},{1,3},{3,1},{4,6},{6,4},{5,7},{7,5},{8,10},{10,8},{9,1... | collective-permute-start | bytes 393224 | tf_op jit(solution)/shard_map/ppermute | solution.py:310

commit v11 on v10

--- a/solution.py
+++ b/solution.py
@@ -166,7 +166,8 @@
         )
         sum_ref[begin:, :] += moved[:, :LANES]
         sum_ref[begin + 8 :, :] += moved[: rows - begin - 8, LANES:]
-    out_ref[...] = sum_ref[...].astype(bf16)
+    out_ref[: rows // 2, :] = sum_ref[rows // 2 :, :].astype(bf16)
+    out_ref[rows // 2 :, :] = sum_ref[: rows // 2, :].astype(bf16)
 
 
 def long_conv(value, line, tiles):
@@ -255,7 +256,9 @@
 
 
 def gated_of(q_ref, mix_ref):
-    return (q_ref[...] * mix_ref[...].astype(f32)).astype(bf16)
+    half = mix_ref.shape[0] // 2
+    mix = jnp.concatenate([mix_ref[half:, :], mix_ref[:half, :]], axis=0)
+    return (q_ref[...] * mix.astype(f32)).astype(bf16)
 
 
 def own_part(member, q_ref, mix_ref, weight_ref):
@@ -299,7 +302,7 @@
     last = edge(in_hbm(features))
     halo = lax.ppermute(last, "ctx", [(i, i + 1) for i in range(ctx_count - 1)])
     mix = long_conv(got, line, tiles).reshape(ctx_count, chan_dev, tok_local)
-    mix = lax.all_to_all(mix, "ctx", 0, 0, tiled=True).reshape(chan_tp, tok_local)
+    mix = lax.all_to_all(mix, "ctx", 0, 0, axis_index_groups=[order], tiled=True).reshape(chan_tp, tok_local)
     q = query_conv(features, halo, short_taps)
     weight = turn(in_hbm(out_weight))
     operands = (q, mix, weight)

time: 71.1 us -> 68.8 us (0.968)
  waiting for transfers between devices: 15.8 us -> 11.8 us
  starting transfers between devices: 42.9 us -> 43.9 us
    all_to_all x1, waiting for transfers between devices: 4.29 us -> 0.34 us  [local(): lax.all_to_all(mix, 'ctx', 0, 0, axis_index_groups=[order], tiled=True)]
    all_to_all x1, starting transfers between devices: 9.32 us -> 10.1 us  [local(): lax.all_to_all(mix, 'ctx', 0, 0, axis_index_groups=[order], tiled=True)]
  transfers between devices with their start and end apart: 6 -> 6, of which waited for: 3 -> 3; matrix products, arithmetic and copies ran while one was open for 0% -> 0% of each run, Pallas kernels for 9% -> 10%
where the time goes in v11:
time: 68.8 us; the launch traced here: 67.6 us
  starting transfers between devices  43.9 us (64%)
  waiting for transfers between devices  11.8 us (17%)
  Pallas kernels  11 us (16%)
    all_to_all x1, starting transfers between devices, local(): lax.all_to_all(sent, 'ctx', 0, 0, axis_index_groups=[order], tiled=True)  19.3 us
    all_to_all x1, starting transfers between devices, local(): lax.all_to_all(mix, 'ctx', 0, 0, axis_index_groups=[order], tiled=True)  10.1 us
    all_to_all x1, waiting for transfers between devices, local(): lax.all_to_all(sent, 'ctx', 0, 0, axis_index_groups=[order], tiled=True)  8.22 us
    ppermute x1, starting transfers between devices, local(): given = lax.ppermute(given, 'tp', CORE_PAIRS)  5.03 us
    ppermute x1, starting transfers between devices, local(): arrived = lax.ppermute(away, 'tp', CHIP_PAIRS)  4.36 us
    ppermute x1, waiting for transfers between devices, local(): arrived = lax.ppermute(away, 'tp', CHIP_PAIRS)  3.27 us
    ppermute x1, starting transfers between devices, local(): halo = lax.ppermute(last, 'ctx', [(i, i + 1) for i in range(ctx_count - 1)])  3.09 us
    pallas_call x1, Pallas kernels, turn(): pl.pallas_call(turn_kernel, out_shape=jax.ShapeDtypeStruct((total, width)...  2.77 us
  transfers between devices with their start and end apart: 6, of which 3 were waited for; matrix products, arithmetic and copies ran while one was open for 0% of the time, Pallas kernels for 10%

profile of v11, /device:TPU:1, one launch (start us, length us, event | category | flops | bytes accessed | tf_op | source)
XLA Modules:
  0.0 67.6 jit_solution(16088581195822247012)
XLA Ops:
  0.0 1.6 %pack.1 = bf16[128,8,128]{2,1,0:T(8,128)(2,1)} custom-call(bf16[3,512,128]{2,1,0:T(8,128)(2,1)} %features_ref.1), custom_call_target="tpu_custom_call" | custom-call | flops 262144 | bytes 524288 | tf_op jit(solution)/shard_map/pack/pallas_call | solution.py:118
  1.6 19.3 %all-to-all-start = ((bf16[128,8,128]{2,1,0:T(8,128)(2,1)}), bf16[128,8,128]{2,1,0:T(8,128)(2,1)S(1)}, u32[]{:S(2)}, u32[]{:S(2)}) async-start(bf16[128,8,128]{2,1,0:T(8,128)(2,1)} %pack.1), calls=%async_computation | async-start | bytes 524288 | tf_op jit(solution)/shard_map/all_to_all | solution.py:300
  21.0 1.4 %prepare.1 = (bf16[16,16512]{1,0:T(8,128)(2,1)S(1)}, f32[4,8,128]{2,1,0:T(8,128)S(1)}) custom-call(s32[1]{0:T(128)} %bitcast.1.rank_ref, bf16[32,16384]{1,0:T(8,128)(2,1)} %filter_ref.1, f32[3,3,512]{2,1,0:T(4,128)} %taps_ref.3, f32[512]{0:T(512)} %skip_ref.1), custom_call_target="tpu_custom_call" | custom-call | flops 4194304 | bytes 1048576 | tf_op jit(solution)/shard_map/prepare/pallas_call | solution.py:69
  22.4 8.2 %all-to-all-done.value_ref = bf16[128,8,128]{2,1,0:T(8,128)(2,1)S(1)} async-done(((bf16[128,8,128]{2,1,0:T(8,128)(2,1)}), bf16[128,8,128]{2,1,0:T(8,128)(2,1)S(1)}, u32[]{:S(2)}, u32[]{:S(2)}) %all-to-all-start) | async-done | bytes 262176 | tf_op jit(solution)/shard_map/all_to_all | solution.py:300
  30.6 2.5 %long_conv.1 = bf16[512,128]{1,0:T(8,128)(2,1)} custom-call(bf16[128,8,128]{2,1,0:T(8,128)(2,1)S(1)} %all-to-all-done.value_ref, bf16[16,16512]{1,0:T(8,128)(2,1)S(1)} %get-tuple-element.7.line_ref, f32[4,8,128]{2,1,0:T(8,128)S(1)} %get-tuple-element.8.tiles_ref), custom_call_target="tpu_custom_call" | custom-call | flops 2147483648 | bytes 1048576 | tf_op jit(solution)/shard_map/long_conv/pallas_call | solution.py:177
  33.1 10.1 %all-to-all-start.1 = ((bf16[128,4,128]{2,1,0:T(4,128)(2,1)}), bf16[128,4,128]{2,1,0:T(4,128)(2,1)S(1)}, u32[]{:S(2)}, u32[]{:S(2)}) async-start(bf16[128,4,128]{2,1,0:T(4,128)(2,1)} %bitcast.2), calls=%async_computation.1 | async-start | bytes 262144 | tf_op jit(solution)/shard_map/all_to_all | solution.py:305
  43.2 1.0 %edge.1 = bf16[16,512]{1,0:T(8,128)(2,1)S(1)} custom-call(bf16[3,512,128]{2,1,0:T(8,128)(2,1)} %features_ref.1), custom_call_target="tpu_custom_call" | custom-call | flops 65536 | bytes 131072 | tf_op jit(solution)/shard_map/edge/pallas_call | solution.py:217
  44.2 3.1 %collective-permute-start = (bf16[16,512]{1,0:T(8,128)(2,1)S(1)}, bf16[16,512]{1,0:T(8,128)(2,1)S(1)}, u32[]{:S(2)}, u32[]{:S(2)}) collective-permute-start(bf16[16,512]{1,0:T(8,128)(2,1)S(1)} %edge.1), channel_id=1, source_target_pairs={{0,4},{4,8},{8,12},{12,16},{16,20},{20,24},{24,28},{28,32},{32,36}... | collective-permute-start | bytes 49160 | tf_op jit(solution)/shard_map/ppermute | solution.py:303
  47.3 0.0 copy-start
  47.3 0.0 copy-start.1
  47.4 2.8 %turn.1.weight_ref = bf16[2048,512]{1,0:T(8,128)(2,1)S(1)} custom-call(bf16[512,2048]{1,0:T(8,128)(2,1)} %weight_ref.1), custom_call_target="tpu_custom_call" | custom-call | flops 1048576 | bytes 4194304 | tf_op jit(solution)/shard_map/turn/pallas_call | solution.py:199
  50.2 0.6 query_conv.1.q_ref
  50.8 0.3 all-to-all-done.1
  51.1 0.3 shard_map.57
  51.4 5.0 %collective-permute-start.2 = (bf16[512,128]{1,0:T(8,128)(2,1)S(1)}, bf16[512,128]{1,0:T(8,128)(2,1)S(1)}, u32[]{:S(2)}, u32[]{:S(2)}) collective-permute-start(bf16[512,128]{1,0:T(8,128)(2,1)S(1)} %shard_map.57), channel_id=1, source_target_pairs={{0,1},{1,0},{2,3},{3,2},{4,5},{5,4},{6,7},{7,6},{8,9},{9,8},{10,11... | collective-permute-start | bytes 393224 | tf_op jit(solution)/shard_map/ppermute | solution.py:311
  56.4 0.3 shard_map.55
  56.8 1.9 %collective-permute-start.1 = (bf16[512,128]{1,0:T(8,128)(2,1)S(1)}, bf16[512,128]{1,0:T(8,128)(2,1)S(1)}, u32[]{:S(2)}, u32[]{:S(2)}) collective-permute-start(bf16[512,128]{1,0:T(8,128)(2,1)S(1)} %shard_map.55), channel_id=1, source_target_pairs={{0,1},{1,0},{2,3},{3,2},{4,5},{5,4},{6,7},{7,6},{8,9},{9,8},{10,11... | collective-permute-start | bytes 393224 | tf_op jit(solution)/shard_map/ppermute | solution.py:315
  58.7 0.0 collective-permute-done.2.given_ref
  58.7 0.3 shard_map.58
  59.0 4.4 %collective-permute-start.3 = (bf16[512,128]{1,0:T(8,128)(2,1)S(1)}, bf16[512,128]{1,0:T(8,128)(2,1)S(1)}, u32[]{:S(2)}, u32[]{:S(2)}) collective-permute-start(bf16[512,128]{1,0:T(8,128)(2,1)S(1)} %shard_map.58), channel_id=1, source_target_pairs={{0,2},{2,0},{1,3},{3,1},{4,6},{6,4},{5,7},{7,5},{8,10},{10,8},{9,1... | collective-permute-start | bytes 393224 | tf_op jit(solution)/shard_map/ppermute | solution.py:313
  63.4 0.0 collective-permute-done.1.given_ref
  63.4 0.3 shard_map.56
  63.7 3.3 %collective-permute-done.3 = bf16[512,128]{1,0:T(8,128)(2,1)S(1)} collective-permute-done((bf16[512,128]{1,0:T(8,128)(2,1)S(1)}, bf16[512,128]{1,0:T(8,128)(2,1)S(1)}, u32[]{:S(2)}, u32[]{:S(2)}) %collective-permute-start.3) | collective-permute-done | bytes 131104 | tf_op jit(solution)/shard_map/ppermute | solution.py:313
  67.0 0.7 %add_convert_fusion = bf16[512,128]{1,0:T(8,128)(2,1)} fusion(f32[512,128]{1,0:T(8,128)S(1)} %shard_map.56, bf16[512,128]{1,0:T(8,128)(2,1)S(1)} %collective-permute-done.3), kind=kLoop, calls=%fused_computation | loop fusion | flops 196608 | bytes 524288 | tf_op jit(solution)/shard_map/convert_element_type | solution.py:317
  (3 shorter events, 0.0 us)
Async XLA Ops:
  1.6 29.0 %all-to-all-start = ((bf16[128,8,128]{2,1,0:T(8,128)(2,1)}), bf16[128,8,128]{2,1,0:T(8,128)(2,1)S(1)}, u32[]{:S(2)}, u32[]{:S(2)}) async-start(bf16[128,8,128]{2,1,0:T(8,128)(2,1)} %pack.1), calls=%async_computation | async-start | bytes 524288 | tf_op jit(solution)/shard_map/all_to_all | solution.py:300
  33.1 18.0 %all-to-all-start.1 = ((bf16[128,4,128]{2,1,0:T(4,128)(2,1)}), bf16[128,4,128]{2,1,0:T(4,128)(2,1)S(1)}, u32[]{:S(2)}, u32[]{:S(2)}) async-start(bf16[128,4,128]{2,1,0:T(4,128)(2,1)} %bitcast.2), calls=%async_computation.1 | async-start | bytes 262144 | tf_op jit(solution)/shard_map/all_to_all | solution.py:305
  44.2 5.9 %collective-permute-start = (bf16[16,512]{1,0:T(8,128)(2,1)S(1)}, bf16[16,512]{1,0:T(8,128)(2,1)S(1)}, u32[]{:S(2)}, u32[]{:S(2)}) collective-permute-start(bf16[16,512]{1,0:T(8,128)(2,1)S(1)} %edge.1), channel_id=1, source_target_pairs={{0,4},{4,8},{8,12},{12,16},{16,20},{20,24},{24,28},{28,32},{32,36}... | collective-permute-start | bytes 49160 | tf_op jit(solution)/shard_map/ppermute | solution.py:303
  47.3 2.8 %copy-start = (bf16[3,512,128]{2,1,0:T(8,128)(2,1)S(1)}, bf16[3,512,128]{2,1,0:T(8,128)(2,1)}, u32[]{:S(2)}) copy-start(bf16[3,512,128]{2,1,0:T(8,128)(2,1)} %features_ref.1) | copy-start | bytes 1179652
  47.3 2.8 %copy-start.1 = (f32[3,3,512]{2,1,0:T(4,128)S(1)}, f32[3,3,512]{2,1,0:T(4,128)}, u32[]{:S(2)}) copy-start(f32[3,3,512]{2,1,0:T(4,128)} %taps_ref.3) | copy-start | bytes 55300
  51.4 7.3 %collective-permute-start.2 = (bf16[512,128]{1,0:T(8,128)(2,1)S(1)}, bf16[512,128]{1,0:T(8,128)(2,1)S(1)}, u32[]{:S(2)}, u32[]{:S(2)}) collective-permute-start(bf16[512,128]{1,0:T(8,128)(2,1)S(1)} %shard_map.57), channel_id=1, source_target_pairs={{0,1},{1,0},{2,3},{3,2},{4,5},{5,4},{6,7},{7,6},{8,9},{9,8},{10,11... | collective-permute-start | bytes 393224 | tf_op jit(solution)/shard_map/ppermute | solution.py:311
  56.8 6.6 %collective-permute-start.1 = (bf16[512,128]{1,0:T(8,128)(2,1)S(1)}, bf16[512,128]{1,0:T(8,128)(2,1)S(1)}, u32[]{:S(2)}, u32[]{:S(2)}) collective-permute-start(bf16[512,128]{1,0:T(8,128)(2,1)S(1)} %shard_map.55), channel_id=1, source_target_pairs={{0,1},{1,0},{2,3},{3,2},{4,5},{5,4},{6,7},{7,6},{8,9},{9,8},{10,11... | collective-permute-start | bytes 393224 | tf_op jit(solution)/shard_map/ppermute | solution.py:315
  59.0 8.0 %collective-permute-start.3 = (bf16[512,128]{1,0:T(8,128)(2,1)S(1)}, bf16[512,128]{1,0:T(8,128)(2,1)S(1)}, u32[]{:S(2)}, u32[]{:S(2)}) collective-permute-start(bf16[512,128]{1,0:T(8,128)(2,1)S(1)} %shard_map.58), channel_id=1, source_target_pairs={{0,2},{2,0},{1,3},{3,1},{4,6},{6,4},{5,7},{7,5},{8,10},{10,8},{9,1... | collective-permute-start | bytes 393224 | tf_op jit(solution)/shard_map/ppermute | solution.py:313

commit v12 on v10

--- a/solution.py
+++ b/solution.py
@@ -20,6 +20,11 @@
 
 def params(mib):
     return pltpu.CompilerParams(vmem_limit_bytes=mib << 20)
+
+
+def swapped(array, pieces=32, flip=19):
+    size = array.shape[0] // pieces
+    return jnp.concatenate([array[(i ^ flip) * size : ((i ^ flip) + 1) * size] for i in range(pieces)], axis=0)
 
 
 def in_hbm(array):
@@ -105,7 +110,7 @@
         odd = jnp.where(upper, pltpu.roll(k, 4, 1), v)
         after = (step + PACK_STEPS // 2) % PACK_STEPS
         there = slice(after * rows // 4, (after + 1) * rows // 4)
-        packed_ref[there] = jnp.stack([even, odd], axis=1).reshape(rows // 4, 8, LANES).astype(bf16)
+        packed_ref[there] = swapped(jnp.stack([even, odd], axis=1).reshape(rows // 4, 8, LANES), 8, 3).astype(bf16)
         stores.append(pltpu.make_async_copy(packed_ref.at[there], out_ref.at[there], out_sems.at[step]))
         stores[-1].start()
     for store in stores:
@@ -135,7 +140,7 @@
 def conv_kernel(value_ref, line_ref, tiles_ref, out_ref, pair_ref, sum_ref, table_ref):
     blocks = value_ref.shape[0]
     rows = blocks * 4
-    value = jnp.concatenate([value_ref[blocks // 2 :], value_ref[: blocks // 2]], axis=0).astype(f32)
+    value = swapped(value_ref[...].astype(f32))
     lane = lax.broadcasted_iota(jnp.int32, value.shape, 2)
     sub = lax.broadcasted_iota(jnp.int32, (blocks // 2, 8, LANES), 1)
 
@@ -166,7 +171,7 @@
         )
         sum_ref[begin:, :] += moved[:, :LANES]
         sum_ref[begin + 8 :, :] += moved[: rows - begin - 8, LANES:]
-    out_ref[...] = sum_ref[...].astype(bf16)
+    out_ref[...] = swapped(sum_ref[...]).astype(bf16)
 
 
 def long_conv(value, line, tiles):
@@ -255,7 +260,7 @@
 
 
 def gated_of(q_ref, mix_ref):
-    return (q_ref[...] * mix_ref[...].astype(f32)).astype(bf16)
+    return (q_ref[...] * swapped(mix_ref[...].astype(f32))).astype(bf16)
 
 
 def own_part(member, q_ref, mix_ref, weight_ref):
@@ -293,13 +298,13 @@
     member = jnp.full((1,), lax.axis_index("tp"), jnp.int32)
 
     sent = pack(in_hbm(features))
-    order = [(i + ctx_count // 2) % ctx_count for i in range(ctx_count)]
+    order = [i ^ 76 for i in range(ctx_count)]
     got = lax.all_to_all(sent, "ctx", 0, 0, axis_index_groups=[order], tiled=True)
     line, tiles = prepare(rank, *map(in_hbm, (filters, short_taps, skip_gain)))
     last = edge(in_hbm(features))
     halo = lax.ppermute(last, "ctx", [(i, i + 1) for i in range(ctx_count - 1)])
     mix = long_conv(got, line, tiles).reshape(ctx_count, chan_dev, tok_local)
-    mix = lax.all_to_all(mix, "ctx", 0, 0, tiled=True).reshape(chan_tp, tok_local)
+    mix = lax.all_to_all(mix, "ctx", 0, 0, axis_index_groups=[order], tiled=True).reshape(chan_tp, tok_local)
     q = query_conv(features, halo, short_taps)
     weight = turn(in_hbm(out_weight))
     operands = (q, mix, weight)

time: 71.1 us -> 70 us (0.985)
  the two profiles are of different devices: /device:TPU:1 before, /device:TPU:12 now
where the time goes in v12:
time: 70 us; the launch traced here: 69.5 us
  starting transfers between devices  41.5 us (59%)
  waiting for transfers between devices  16.1 us (23%)
  Pallas kernels  11 us (16%)
    all_to_all x1, starting transfers between devices, local(): lax.all_to_all(sent, 'ctx', 0, 0, axis_index_groups=[order], tiled=True)  19.1 us
    all_to_all x1, starting transfers between devices, local(): lax.all_to_all(mix, 'ctx', 0, 0, axis_index_groups=[order], tiled=True)  12.3 us
    all_to_all x1, waiting for transfers between devices, local(): lax.all_to_all(sent, 'ctx', 0, 0, axis_index_groups=[order], tiled=True)  7.6 us
    ppermute x1, waiting for transfers between devices, local(): arrived = lax.ppermute(away, 'tp', CHIP_PAIRS)  6.08 us
    ppermute x1, starting transfers between devices, local(): halo = lax.ppermute(last, 'ctx', [(i, i + 1) for i in range(ctx_count - 1)])  3.38 us
    pallas_call x1, Pallas kernels, turn(): pl.pallas_call(turn_kernel, out_shape=jax.ShapeDtypeStruct((total, width)...  2.77 us
    pallas_call x1, Pallas kernels, long_conv(): pl.pallas_call(conv_kernel, out_shape=jax.ShapeDtypeStruct((rows, LANES),...  2.47 us
    ppermute x1, waiting for transfers between devices, local(): halo = lax.ppermute(last, 'ctx', [(i, i + 1) for i in range(ctx_count - 1)])  2.45 us
  transfers between devices with their start and end apart: 6, of which 3 were waited for; matrix products, arithmetic and copies ran while one was open for 0% of the time, Pallas kernels for 10%

profile of v12, /device:TPU:12, one launch (start us, length us, event | category | flops | bytes accessed | tf_op | source)
XLA Modules:
  0.0 69.5 jit_solution(5098182370726555084)
XLA Ops:
  0.0 1.6 %pack.1 = bf16[128,8,128]{2,1,0:T(8,128)(2,1)} custom-call(bf16[3,512,128]{2,1,0:T(8,128)(2,1)} %features_ref.1), custom_call_target="tpu_custom_call" | custom-call | flops 262144 | bytes 524288 | tf_op jit(solution)/shard_map/pack/pallas_call | solution.py:123
  1.6 19.1 %all-to-all-start = ((bf16[128,8,128]{2,1,0:T(8,128)(2,1)}), bf16[128,8,128]{2,1,0:T(8,128)(2,1)S(1)}, u32[]{:S(2)}, u32[]{:S(2)}) async-start(bf16[128,8,128]{2,1,0:T(8,128)(2,1)} %pack.1), calls=%async_computation | async-start | bytes 524288 | tf_op jit(solution)/shard_map/all_to_all | solution.py:302
  20.7 1.4 %prepare.1 = (bf16[16,16512]{1,0:T(8,128)(2,1)S(1)}, f32[4,8,128]{2,1,0:T(8,128)S(1)}) custom-call(s32[1]{0:T(128)} %bitcast.1.rank_ref, bf16[32,16384]{1,0:T(8,128)(2,1)} %filter_ref.1, f32[3,3,512]{2,1,0:T(4,128)} %taps_ref.3, f32[512]{0:T(512)} %skip_ref.1), custom_call_target="tpu_custom_call" | custom-call | flops 4194304 | bytes 1048576 | tf_op jit(solution)/shard_map/prepare/pallas_call | solution.py:74
  22.1 7.6 %all-to-all-done.value_ref = bf16[128,8,128]{2,1,0:T(8,128)(2,1)S(1)} async-done(((bf16[128,8,128]{2,1,0:T(8,128)(2,1)}), bf16[128,8,128]{2,1,0:T(8,128)(2,1)S(1)}, u32[]{:S(2)}, u32[]{:S(2)}) %all-to-all-start) | async-done | bytes 262176 | tf_op jit(solution)/shard_map/all_to_all | solution.py:302
  29.7 2.5 %long_conv.1 = bf16[512,128]{1,0:T(8,128)(2,1)} custom-call(bf16[128,8,128]{2,1,0:T(8,128)(2,1)S(1)} %all-to-all-done.value_ref, bf16[16,16512]{1,0:T(8,128)(2,1)S(1)} %get-tuple-element.7.line_ref, f32[4,8,128]{2,1,0:T(8,128)S(1)} %get-tuple-element.8.tiles_ref), custom_call_target="tpu_custom_call" | custom-call | flops 2147483648 | bytes 1048576 | tf_op jit(solution)/shard_map/long_conv/pallas_call | solution.py:181
  32.2 12.3 %all-to-all-start.1 = ((bf16[128,4,128]{2,1,0:T(4,128)(2,1)}), bf16[128,4,128]{2,1,0:T(4,128)(2,1)S(1)}, u32[]{:S(2)}, u32[]{:S(2)}) async-start(bf16[128,4,128]{2,1,0:T(4,128)(2,1)} %bitcast.2), calls=%async_computation.1 | async-start | bytes 262144 | tf_op jit(solution)/shard_map/all_to_all | solution.py:307
  44.5 1.0 %edge.1 = bf16[16,512]{1,0:T(8,128)(2,1)S(1)} custom-call(bf16[3,512,128]{2,1,0:T(8,128)(2,1)} %features_ref.1), custom_call_target="tpu_custom_call" | custom-call | flops 65536 | bytes 131072 | tf_op jit(solution)/shard_map/edge/pallas_call | solution.py:221
  45.5 3.4 %collective-permute-start = (bf16[16,512]{1,0:T(8,128)(2,1)S(1)}, bf16[16,512]{1,0:T(8,128)(2,1)S(1)}, u32[]{:S(2)}, u32[]{:S(2)}) collective-permute-start(bf16[16,512]{1,0:T(8,128)(2,1)S(1)} %edge.1), channel_id=1, source_target_pairs={{0,4},{4,8},{8,12},{12,16},{16,20},{20,24},{24,28},{28,32},{32,36}... | collective-permute-start | bytes 49160 | tf_op jit(solution)/shard_map/ppermute | solution.py:305
  48.9 0.0 copy-start
  48.9 0.0 copy-start.1
  48.9 2.8 %turn.1.weight_ref = bf16[2048,512]{1,0:T(8,128)(2,1)S(1)} custom-call(bf16[512,2048]{1,0:T(8,128)(2,1)} %weight_ref.1), custom_call_target="tpu_custom_call" | custom-call | flops 1048576 | bytes 4194304 | tf_op jit(solution)/shard_map/turn/pallas_call | solution.py:203
  51.7 2.4 %collective-permute-done.halo_ref = bf16[16,512]{1,0:T(8,128)(2,1)S(1)} collective-permute-done((bf16[16,512]{1,0:T(8,128)(2,1)S(1)}, bf16[16,512]{1,0:T(8,128)(2,1)S(1)}, u32[]{:S(2)}, u32[]{:S(2)}) %collective-permute-start) | collective-permute-done | bytes 16416 | tf_op jit(solution)/shard_map/ppermute | solution.py:305
  54.1 0.6 query_conv.1.q_ref
  54.7 0.0 all-to-all-done.1
  54.7 0.3 shard_map.57
  55.1 1.9 %collective-permute-start.2 = (bf16[512,128]{1,0:T(8,128)(2,1)S(1)}, bf16[512,128]{1,0:T(8,128)(2,1)S(1)}, u32[]{:S(2)}, u32[]{:S(2)}) collective-permute-start(bf16[512,128]{1,0:T(8,128)(2,1)S(1)} %shard_map.57), channel_id=1, source_target_pairs={{0,1},{1,0},{2,3},{3,2},{4,5},{5,4},{6,7},{7,6},{8,9},{9,8},{10,11... | collective-permute-start | bytes 393224 | tf_op jit(solution)/shard_map/ppermute | solution.py:313
  57.0 0.3 shard_map.55
  57.3 2.4 %collective-permute-start.1 = (bf16[512,128]{1,0:T(8,128)(2,1)S(1)}, bf16[512,128]{1,0:T(8,128)(2,1)S(1)}, u32[]{:S(2)}, u32[]{:S(2)}) collective-permute-start(bf16[512,128]{1,0:T(8,128)(2,1)S(1)} %shard_map.55), channel_id=1, source_target_pairs={{0,1},{1,0},{2,3},{3,2},{4,5},{5,4},{6,7},{7,6},{8,9},{9,8},{10,11... | collective-permute-start | bytes 393224 | tf_op jit(solution)/shard_map/ppermute | solution.py:317
  59.7 0.0 collective-permute-done.2.given_ref
  59.7 0.3 shard_map.58
  60.0 2.4 %collective-permute-start.3 = (bf16[512,128]{1,0:T(8,128)(2,1)S(1)}, bf16[512,128]{1,0:T(8,128)(2,1)S(1)}, u32[]{:S(2)}, u32[]{:S(2)}) collective-permute-start(bf16[512,128]{1,0:T(8,128)(2,1)S(1)} %shard_map.58), channel_id=1, source_target_pairs={{0,2},{2,0},{1,3},{3,1},{4,6},{6,4},{5,7},{7,5},{8,10},{10,8},{9,1... | collective-permute-start | bytes 393224 | tf_op jit(solution)/shard_map/ppermute | solution.py:315
  62.5 0.3 shard_map.56
  62.8 6.1 %collective-permute-done.3 = bf16[512,128]{1,0:T(8,128)(2,1)S(1)} collective-permute-done((bf16[512,128]{1,0:T(8,128)(2,1)S(1)}, bf16[512,128]{1,0:T(8,128)(2,1)S(1)}, u32[]{:S(2)}, u32[]{:S(2)}) %collective-permute-start.3) | collective-permute-done | bytes 131104 | tf_op jit(solution)/shard_map/ppermute | solution.py:315
  68.8 0.7 add_convert_fusion
  (3 shorter events, 0.0 us)
Async XLA Ops:
  1.6 28.1 %all-to-all-start = ((bf16[128,8,128]{2,1,0:T(8,128)(2,1)}), bf16[128,8,128]{2,1,0:T(8,128)(2,1)S(1)}, u32[]{:S(2)}, u32[]{:S(2)}) async-start(bf16[128,8,128]{2,1,0:T(8,128)(2,1)} %pack.1), calls=%async_computation | async-start | bytes 524288 | tf_op jit(solution)/shard_map/all_to_all | solution.py:302
  32.2 22.6 %all-to-all-start.1 = ((bf16[128,4,128]{2,1,0:T(4,128)(2,1)}), bf16[128,4,128]{2,1,0:T(4,128)(2,1)S(1)}, u32[]{:S(2)}, u32[]{:S(2)}) async-start(bf16[128,4,128]{2,1,0:T(4,128)(2,1)} %bitcast.2), calls=%async_computation.1 | async-start | bytes 262144 | tf_op jit(solution)/shard_map/all_to_all | solution.py:307
  45.5 8.6 %collective-permute-start = (bf16[16,512]{1,0:T(8,128)(2,1)S(1)}, bf16[16,512]{1,0:T(8,128)(2,1)S(1)}, u32[]{:S(2)}, u32[]{:S(2)}) collective-permute-start(bf16[16,512]{1,0:T(8,128)(2,1)S(1)} %edge.1), channel_id=1, source_target_pairs={{0,4},{4,8},{8,12},{12,16},{16,20},{20,24},{24,28},{28,32},{32,36}... | collective-permute-start | bytes 49160 | tf_op jit(solution)/shard_map/ppermute | solution.py:305
  48.9 5.3 %copy-start = (bf16[3,512,128]{2,1,0:T(8,128)(2,1)S(1)}, bf16[3,512,128]{2,1,0:T(8,128)(2,1)}, u32[]{:S(2)}) copy-start(bf16[3,512,128]{2,1,0:T(8,128)(2,1)} %features_ref.1) | copy-start | bytes 1179652
  48.9 5.2 %copy-start.1 = (f32[3,3,512]{2,1,0:T(4,128)S(1)}, f32[3,3,512]{2,1,0:T(4,128)}, u32[]{:S(2)}) copy-start(f32[3,3,512]{2,1,0:T(4,128)} %taps_ref.3) | copy-start | bytes 55300
  55.1 4.7 %collective-permute-start.2 = (bf16[512,128]{1,0:T(8,128)(2,1)S(1)}, bf16[512,128]{1,0:T(8,128)(2,1)S(1)}, u32[]{:S(2)}, u32[]{:S(2)}) collective-permute-start(bf16[512,128]{1,0:T(8,128)(2,1)S(1)} %shard_map.57), channel_id=1, source_target_pairs={{0,1},{1,0},{2,3},{3,2},{4,5},{5,4},{6,7},{7,6},{8,9},{9,8},{10,11... | collective-permute-start | bytes 393224 | tf_op jit(solution)/shard_map/ppermute | solution.py:313
  57.3 5.2 %collective-permute-start.1 = (bf16[512,128]{1,0:T(8,128)(2,1)S(1)}, bf16[512,128]{1,0:T(8,128)(2,1)S(1)}, u32[]{:S(2)}, u32[]{:S(2)}) collective-permute-start(bf16[512,128]{1,0:T(8,128)(2,1)S(1)} %shard_map.55), channel_id=1, source_target_pairs={{0,1},{1,0},{2,3},{3,2},{4,5},{5,4},{6,7},{7,6},{8,9},{9,8},{10,11... | collective-permute-start | bytes 393224 | tf_op jit(solution)/shard_map/ppermute | solution.py:317
  60.0 8.8 %collective-permute-start.3 = (bf16[512,128]{1,0:T(8,128)(2,1)S(1)}, bf16[512,128]{1,0:T(8,128)(2,1)S(1)}, u32[]{:S(2)}, u32[]{:S(2)}) collective-permute-start(bf16[512,128]{1,0:T(8,128)(2,1)S(1)} %shard_map.58), channel_id=1, source_target_pairs={{0,2},{2,0},{1,3},{3,1},{4,6},{6,4},{5,7},{7,5},{8,10},{10,8},{9,1... | collective-permute-start | bytes 393224 | tf_op jit(solution)/shard_map/ppermute | solution.py:315
